TPU v7x, 256 devices: a whole 4x4x8 slice. The times are simulated.
256 devices in a mesh: seq: 16 (over z_hi, x, core), chan: 16 (over y, z_lo).
Axes of the slice: x: 4, y: 4, z: 8 (z_hi: 2, z_lo: 4; z = z_hi * 4 + z_lo), core: 2. Of those that a mesh axis runs over, the one named last changes fastest.
Arguments:
- inputs: bfloat16 [768, 262144], P('chan', 'seq'), may hold values from -6 to 6
- kernel: bfloat16 [768, 512, 512], P('chan', 'seq'), may hold values from -6 to 6
- forward_one: bfloat16 [512, 512], replicated, may hold values from -0.25 to 0.25
- forward_two: bfloat16 [512, 512], replicated, may hold values from -0.25 to 0.25
- inverse_one: bfloat16 [512, 512], replicated, may hold values from -0.25 to 0.25
- inverse_two: bfloat16 [512, 512], replicated, may hold values from -0.25 to 0.25
- norm_gain: float32 [768], replicated, may hold values from 0.1 to 1.9
- w_gate: bfloat16 [1536, 768], P('chan'), may hold values from -0.21875 to 0.21875
- w_up: bfloat16 [1536, 768], P('chan'), may hold values from -0.21875 to 0.21875
- w_down: bfloat16 [1536, 768], P('chan'), may hold values from -0.15625 to 0.15625
Outputs:
- output: bfloat16 [768, 262144], P('chan', 'seq')
All inputs are finite; a program needn't handle non-finite values.
Results may differ from a plain program's by a relative error of at most 0.0075.
Values may be sent and summed in bfloat16 or wider, within the bound.
No kernel may reach another device: no remote copies, remote signals or barrier semaphores. Data moves between devices by JAX's collectives and lax.ppermute only.
A program may use at most 128 MiB of HBM per device.

v0:
```python
import jax
import jax.numpy as jnp
from jax import lax
from jax.sharding import PartitionSpec as P


def shards(
    inputs,
    kernel,
    forward_one,
    forward_two,
    inverse_one,
    inverse_two,
    norm_gain,
    w_gate,
    w_up,
    w_down,
):
    channels_here = inputs.shape[0]
    block_width = forward_one.shape[0]
    block_rows = inputs.shape[1] // block_width
    cube = inputs.reshape(channels_here, block_rows, block_width)
    first_section = jnp.einsum(
        "cab,bk->cak", cube, forward_one, preferred_element_type=jnp.float32
    ).astype(jnp.bfloat16)
    spectrum = jnp.einsum(
        "cak,aj->ckj",
        lax.all_to_all(first_section, "seq", split_axis=2, concat_axis=1, tiled=True),
        forward_two,
        preferred_element_type=jnp.float32,
    )
    scaled = (spectrum * kernel.astype(jnp.float32)).astype(jnp.bfloat16)
    partial_inv = jnp.einsum(
        "ckj,ji->cki", scaled, inverse_two, preferred_element_type=jnp.float32
    ).astype(jnp.bfloat16)
    mixed_out = jnp.einsum(
        "cki,km->cim",
        lax.all_to_all(partial_inv, "seq", split_axis=2, concat_axis=1, tiled=True),
        inverse_one,
        preferred_element_type=jnp.float32,
    )
    resid = (cube.astype(jnp.float32) + mixed_out).astype(jnp.bfloat16)
    resid = resid.reshape(channels_here, block_rows * block_width)
    tokens = lax.all_to_all(resid, "chan", split_axis=1, concat_axis=0, tiled=True)
    stream = tokens.astype(jnp.float32)
    mean_square = jnp.mean(stream * stream, axis=0, keepdims=True)
    normed = (stream * lax.rsqrt(mean_square + 1e-05) * norm_gain[:, None]).astype(jnp.bfloat16)
    gate_rows = lax.all_gather(w_gate, "chan", axis=0, tiled=True)
    up_rows = lax.all_gather(w_up, "chan", axis=0, tiled=True)
    down_rows = lax.all_gather(w_down, "chan", axis=0, tiled=True)
    gate_part = jnp.dot(gate_rows, normed, preferred_element_type=jnp.float32)
    up_part = jnp.dot(up_rows, normed, preferred_element_type=jnp.float32)
    hidden = (jax.nn.gelu(gate_part, approximate=True) * up_part).astype(jnp.bfloat16)
    summed = lax.dot_general(
        down_rows, hidden, (((0,), (0,)), ((), ())), preferred_element_type=jnp.float32
    )
    result = (stream + summed).astype(jnp.bfloat16)
    return lax.all_to_all(result, "chan", split_axis=0, concat_axis=1, tiled=True)


def solution(mesh):
    return jax.shard_map(
        shards,
        mesh=mesh,
        in_specs=(
            P("chan", "seq"),
            P("chan", "seq", None),
            P(),
            P(),
            P(),
            P(),
            P(),
            P("chan", None),
            P("chan", None),
            P("chan", None),
        ),
        out_specs=P("chan", "seq"),
        check_vma=False,
    )
```

profile of v0, /device:TPU:6, one launch (start us, length us, event | category | flops | bytes accessed | tf_op | source)
XLA Modules:
  0.0 398.5 jit_solution(8053570124747493535)
XLA Ops:
  6.5 0.0 copy-start
  6.5 0.0 all-gather.4.cloned.1.call-start
  6.5 0.7 all-gather.4.cloned.1.call-update
  7.3 2.0 copy.39
  9.2 0.0 copy-start.2
  9.2 1.1 copy-done.2
  10.4 0.0 copy-done
  10.4 1.0 convolution_convert_fusion.1
  11.4 7.5 %copy.26 = bf16[48,32,512]{0,1,2:T(8,128)(2,1)} copy(bf16[48,32,512]{2,1,0:T(8,128)(2,1)S(1)} %convolution_convert_fusion.1) | data formatting | bytes 3145728 | tf_op jit(solution)/shard_map/convert_element_type | solution.py:25
  18.8 10.1 %reshape.28 = bf16[16,2,24576]{2,1,0:T(2,128)(2,1)} reshape(bf16[512,32,48]{2,1,0:T(8,128)(2,1)} %bitcast.68) | data formatting | bytes 3145728
  28.9 11.4 %all-to-all-start = ((bf16[16,2,24576]{2,1,0:T(2,128)(2,1)}), bf16[16,2,24576]{2,1,0:T(2,128)(2,1)S(1)}, u32[]{:S(2)}, u32[]{:S(2)}) async-start(bf16[16,2,24576]{2,1,0:T(2,128)(2,1)} %reshape.28), calls=%async_computation | async-start | bytes 3145728 | tf_op jit(solution)/shard_map/all_to_all | solution.py:28
  40.4 0.2 all-gather.6.cloned.1.call-start
  40.6 0.5 all-gather.6.cloned.1.call-update
  41.1 47.8 %all-to-all-done = bf16[16,2,24576]{2,1,0:T(2,128)(2,1)S(1)} async-done(((bf16[16,2,24576]{2,1,0:T(2,128)(2,1)}), bf16[16,2,24576]{2,1,0:T(2,128)(2,1)S(1)}, u32[]{:S(2)}, u32[]{:S(2)}) %all-to-all-start) | async-done | bytes 1572896 | tf_op jit(solution)/shard_map/all_to_all | solution.py:28
  88.9 5.2 %reshape.29 = bf16[512,32,48]{2,1,0:T(8,128)(2,1)} reshape(bf16[16,2,24576]{2,1,0:T(2,128)(2,1)S(1)} %all-to-all-done) | data formatting | bytes 3145728
  94.1 11.6 %copy.28 = bf16[48,16,32,32]{2,1,3,0:T(8,128)(2,1)} copy(bf16[48,16,32,32]{0,2,3,1:T(8,128)(2,1)} %bitcast.69) | data formatting | bytes 3145728 | tf_op jit(solution)/shard_map/all_to_all | solution.py:28
  105.7 0.0 copy-start.5
  105.7 0.0 copy-start.6
  105.7 9.4 %all_to_all.53 = bf16[48,512,32]{1,2,0:T(8,128)(2,1)} reshape(bf16[48,16,32,32]{2,1,3,0:T(8,128)(2,1)} %copy.28) | data formatting | bytes 3145728 | tf_op jit(solution)/shard_map/all_to_all | solution.py:28
  115.1 0.0 copy-done.5
  115.1 0.0 copy-done.6
  115.1 3.7 convolution_convert_fusion
  118.7 7.5 %copy.29 = bf16[48,32,512]{0,1,2:T(8,128)(2,1)} copy(bf16[48,32,512]{2,1,0:T(8,128)(2,1)S(1)} %convolution_convert_fusion) | data formatting | bytes 3145728 | tf_op jit(solution)/shard_map/convert_element_type | solution.py:35
  126.2 10.1 %reshape.30 = bf16[16,2,24576]{2,1,0:T(2,128)(2,1)} reshape(bf16[512,32,48]{2,1,0:T(8,128)(2,1)} %bitcast.70) | data formatting | bytes 3145728
  136.3 6.2 %all-to-all-start.1 = ((bf16[16,2,24576]{2,1,0:T(2,128)(2,1)}), bf16[16,2,24576]{2,1,0:T(2,128)(2,1)S(1)}, u32[]{:S(2)}, u32[]{:S(2)}) async-start(bf16[16,2,24576]{2,1,0:T(2,128)(2,1)} %reshape.30), calls=%async_computation.1 | async-start | bytes 3145728 | tf_op jit(solution)/shard_map/all_to_all | solution.py:38
  142.6 0.3 all-gather.8.cloned.1.call-start
  142.8 0.5 all-gather.8.cloned.1.call-update
  143.3 42.3 %all-to-all-done.1 = bf16[16,2,24576]{2,1,0:T(2,128)(2,1)S(1)} async-done(((bf16[16,2,24576]{2,1,0:T(2,128)(2,1)}), bf16[16,2,24576]{2,1,0:T(2,128)(2,1)S(1)}, u32[]{:S(2)}, u32[]{:S(2)}) %all-to-all-start.1) | async-done | bytes 1572896 | tf_op jit(solution)/shard_map/all_to_all | solution.py:38
  185.6 5.2 %reshape.31 = bf16[512,32,48]{2,1,0:T(8,128)(2,1)} reshape(bf16[16,2,24576]{2,1,0:T(2,128)(2,1)S(1)} %all-to-all-done.1) | data formatting | bytes 3145728
  190.8 11.6 %copy.31 = bf16[48,16,32,32]{2,1,3,0:T(8,128)(2,1)} copy(bf16[48,16,32,32]{0,2,3,1:T(8,128)(2,1)} %bitcast.71) | data formatting | bytes 3145728 | tf_op jit(solution)/shard_map/all_to_all | solution.py:38
  202.3 0.0 copy-start.3
  202.3 0.0 copy-start.7
  202.3 9.5 %all_to_all.57 = bf16[48,512,32]{1,2,0:T(8,128)(2,1)} reshape(bf16[48,16,32,32]{2,1,3,0:T(8,128)(2,1)} %copy.31) | data formatting | bytes 3145728 | tf_op jit(solution)/shard_map/all_to_all | solution.py:38
  211.8 0.0 copy-done.3
  211.8 0.0 copy-done.7
  211.8 3.5 add_convert_fusion
  215.4 2.4 all_to_all.58
  217.8 0.9 copy.32
  218.7 0.0 copy-start.4
  218.7 108.2 %all_to_all.68 = bf16[48,16,1024]{2,0,1:T(8,128)(2,1)S(1)} all-to-all(bf16[48,16,1024]{2,0,1:T(8,128)(2,1)S(1)} %copy.32), channel_id=1, replica_groups=mesh['seq'=16,'chan'=16] {'chan'}, dimensions={1} | all-to-all | bytes 3145728 | tf_op jit(solution)/shard_map/all_to_all | solution.py:44
  326.9 0.4 fusion.10
  327.2 0.0 copy-done.4
  327.2 1.5 fusion.12
  328.8 0.0 all-gather.4.cloned.1.call-done
  328.8 7.5 %fusion.22 = f32[1024,1536]{1,0:T(8,128)} fusion(bf16[768,1024]{1,0:T(8,128)(2,1)} %fusion.12, bf16[1536,768]{1,0:T(8,128)(2,1)} %all-gather.4.cloned.1.call-done), kind=kOutput, calls=%fused_computation.30 | convolution fusion | flops 2415919104 | bytes 10223616 | tf_op jit(solution)/shard_map/dot_general | solution.py:51
  336.2 0.0 all-gather.6.cloned.1.call-done
  336.2 0.0 all-gather.8.cloned.1.call-done
  336.2 11.3 %fusion.9 = bf16[768,1024]{1,0:T(8,128)(2,1)} fusion(bf16[48,16,1024]{2,0,1:T(8,128)(2,1)S(1)} %all_to_all.68, bf16[1536,768]{1,0:T(8,128)(2,1)} %all-gather.8.cloned.1.call-done, f32[1024,1536]{1,0:T(8,128)} %fusion.22, bf16[768,1024]{1,0:T(8,128)(2,1)} %fusion.12, bf16[1536,768]{1,0:T(8,128)(2,1)} %all-gather.6.cloned.1.call-done), kind=kOutput, calls=%fused_computation.11 | convolution fusion | flops 4849926144 | bytes 15728640 | tf_op jit(solution)/shard_map/dot_general | solution.py:54
  347.6 0.0 copy-start.1
  347.6 43.2 %all_to_all.69 = bf16[16,48,1024]{2,1,0:T(8,128)(2,1)S(1)} all-to-all(bf16[16,48,1024]{2,1,0:T(8,128)(2,1)} %bitcast.76), channel_id=1, replica_groups=mesh['seq'=16,'chan'=16] {'chan'}, dimensions={0} | all-to-all | bytes 3145728 | tf_op jit(solution)/shard_map/all_to_all | solution.py:58
  390.7 1.3 copy.38
  392.0 0.0 copy-done.1
  (1 shorter events, 0.0 us)
Async XLA Ops:
  6.5 3.8 copy-start
  6.5 322.2 %all-gather.4.cloned.1.call-start = ((), (), s32[]{:S(2)}) async-start(), calls=%async_computation.4 | async-start | bytes 2506752 | tf_op jit(solution)/shard_map/all_gather | solution.py:48
  9.2 1.1 copy-start.2
  28.9 60.0 %all-to-all-start = ((bf16[16,2,24576]{2,1,0:T(2,128)(2,1)}), bf16[16,2,24576]{2,1,0:T(2,128)(2,1)S(1)}, u32[]{:S(2)}, u32[]{:S(2)}) async-start(bf16[16,2,24576]{2,1,0:T(2,128)(2,1)} %reshape.28), calls=%async_computation | async-start | bytes 3145728 | tf_op jit(solution)/shard_map/all_to_all | solution.py:28
  40.4 295.9 %all-gather.6.cloned.1.call-start = ((), (), s32[]{:S(2)}) async-start(), calls=%async_computation.5 | async-start | bytes 2506752 | tf_op jit(solution)/shard_map/all_gather | solution.py:49
  105.7 9.4 %copy-start.5 = (bf16[512,512]{1,0:T(8,128)(2,1)S(1)}, bf16[512,512]{1,0:T(8,128)(2,1)}, u32[]{:S(2)}) copy-start(bf16[512,512]{1,0:T(8,128)(2,1)} %param.15) | copy-start | bytes 1572868
  105.7 9.4 %copy-start.6 = (bf16[512,512]{1,0:T(8,128)(2,1)S(1)}, bf16[512,512]{1,0:T(8,128)(2,1)}, u32[]{:S(2)}) copy-start(bf16[512,512]{1,0:T(8,128)(2,1)} %param.13) | copy-start | bytes 1572868
  136.3 49.3 %all-to-all-start.1 = ((bf16[16,2,24576]{2,1,0:T(2,128)(2,1)}), bf16[16,2,24576]{2,1,0:T(2,128)(2,1)S(1)}, u32[]{:S(2)}, u32[]{:S(2)}) async-start(bf16[16,2,24576]{2,1,0:T(2,128)(2,1)} %reshape.30), calls=%async_computation.1 | async-start | bytes 3145728 | tf_op jit(solution)/shard_map/all_to_all | solution.py:38
  142.6 193.7 %all-gather.8.cloned.1.call-start = ((), (), s32[]{:S(2)}) async-start(), calls=%async_computation.6 | async-start | bytes 2506752 | tf_op jit(solution)/shard_map/all_gather | solution.py:50
  202.3 9.5 %copy-start.3 = (bf16[6,8,32,512]{3,2,1,0:T(8,128)(2,1)S(1)}, bf16[6,8,32,512]{3,2,1,0:T(8,128)(2,1)}, u32[]{:S(2)}) copy-start(bf16[6,8,32,512]{3,2,1,0:T(8,128)(2,1)} %copy-done.2) | copy-start | bytes 4718596
  202.3 9.5 %copy-start.7 = (bf16[512,512]{1,0:T(8,128)(2,1)S(1)}, bf16[512,512]{1,0:T(8,128)(2,1)}, u32[]{:S(2)}) copy-start(bf16[512,512]{1,0:T(8,128)(2,1)} %param.14) | copy-start | bytes 1572868
  218.7 108.5 %copy-start.4 = (f32[768]{0:T(1024)S(1)}, f32[768]{0:T(1024)}, u32[]{:S(2)}) copy-start(f32[768]{0:T(1024)} %param.16) | copy-start | bytes 9220
  347.6 44.4 %copy-start.1 = (bf16[512,512]{1,0:T(8,128)(2,1)S(1)}, bf16[512,512]{1,0:T(8,128)(2,1)}, u32[]{:S(2)}) copy-start(bf16[512,512]{1,0:T(8,128)(2,1)} %param.12) | copy-start | bytes 1572868
Sparse Core Ops, SparseCore 0:
  9.1 109.6 all-gather.3
  120.7 101.9 all-gather.5
  224.5 98.9 all-gather.7
where the time goes:
time: 400 us; the launch traced here: 399 us
  blocking collectives  151 us (38%)
  local copies, waits for them, and re-layouts  95.2 us (24%)
  waiting for transfers between devices  91.8 us (23%)
  matrix products  27 us (7%)
  starting transfers between devices  18.1 us (5%)
  between operations  13.2 us (3%)
    all_to_all x1, blocking collectives, shards(): lax.all_to_all(resid, 'chan', split_axis=1, concat_axis=0, tiled=True)  108 us
    all_to_all x1, waiting for transfers between devices, shards(): lax.all_to_all(first_section, 'seq', split_axis=2, concat_axis=1, tiled=T...  47.8 us
    all_to_all x1, blocking collectives, shards(): lax.all_to_all(result, 'chan', split_axis=0, concat_axis=1, tiled=True)  43.2 us
    all_to_all x1, waiting for transfers between devices, shards(): lax.all_to_all(partial_inv, 'seq', split_axis=2, concat_axis=1, tiled=True)  42.3 us
    unnamed x21, local copies, waits for them, and re-layouts  33.6 us
    all_to_all x2, local copies, waits for them, and re-layouts, shards(): lax.all_to_all(partial_inv, 'seq', split_axis=2, concat_axis=1, tiled=True)  21 us
    all_to_all x2, local copies, waits for them, and re-layouts, shards(): lax.all_to_all(first_section, 'seq', split_axis=2, concat_axis=1, tiled=T...  21 us
    all_to_all x1, starting transfers between devices, shards(): lax.all_to_all(first_section, 'seq', split_axis=2, concat_axis=1, tiled=T...  11.4 us
  transfers between devices with their start and end apart: 5, of which 2 were waited for; matrix products, arithmetic and copies ran while one was open for 22% of the time, Pallas kernels for 0%

commit v1 on v0

v1 whole, which is shorter than its diff:
```python
import functools

import jax
import jax.numpy as jnp
from jax import lax
from jax.experimental import pallas as pl
from jax.experimental.pallas import tpu as pltpu
from jax.sharding import Mesh
from jax.sharding import PartitionSpec as P

SEQ_AXES = ("zh", "x", "core")
CHAN_AXES = ("y", "zl")
F32 = jnp.float32
BF16 = jnp.bfloat16
NT = (((1,), (1,)), ((), ()))
NN = (((1,), (0,)), ((), ()))


def params(mib):
    return pltpu.CompilerParams(vmem_limit_bytes=mib << 20)


def whole(shape):
    return pl.BlockSpec(shape, lambda *_: (0,) * len(shape), pipeline_mode=pl.Buffered(1))


def swap_matrix(n):
    r = lax.broadcasted_iota(jnp.int32, (n * n, n * n), 0)
    c = lax.broadcasted_iota(jnp.int32, (n * n, n * n), 1)
    return ((r // n == c % n) & (r % n == c // n)).astype(F32).astype(BF16)


def chunk_matrix(n, width):
    size = n * n * width
    r = lax.broadcasted_iota(jnp.int32, (size, size), 0)
    c = lax.broadcasted_iota(jnp.int32, (size, size), 1)
    ri, rj, rl = r // (n * width), (r // width) % n, r % width
    ci, cj, cl = c // (n * width), (c // width) % n, c % width
    return ((ri == cj) & (rj == ci) & (rl == cl)).astype(F32).astype(BF16)


def dot(a, b, dims=NN):
    return lax.dot_general(a, b, dims, preferred_element_type=F32)


def section_kernel(x_ref, factor_ref, out_ref, swap, turned, rows):
    @pl.when(pl.program_id(0) == 0)
    def _():
        swap[...] = swap_matrix(16)
        turned[...] = factor_ref[...].astype(F32).T.astype(BF16)

    for half in range(2):
        stack = jnp.concatenate(
            [x_ref[:, (half * 16 + a) * 512 : (half * 16 + a + 1) * 512] for a in range(16)], axis=0
        )
        moved = dot(swap[...], stack).astype(BF16)
        for c in range(16):
            rows[c * 32 + half * 16 : c * 32 + half * 16 + 16, :] = moved[c * 16 : c * 16 + 16]
    out_ref[...] = dot(turned[...], rows[...], NT).astype(BF16)


def first_sections(inputs, forward_one):
    channels, positions = inputs.shape
    return pl.pallas_call(
        section_kernel,
        grid=(channels // 16,),
        in_specs=[pl.BlockSpec((16, positions), lambda g: (g, 0)), whole((512, 512))],
        out_specs=pl.BlockSpec((512, 512), lambda g: (0, g)),
        out_shape=jax.ShapeDtypeStruct((512, channels * 32), BF16),
        scratch_shapes=[
            pltpu.VMEM((256, 256), BF16),
            pltpu.VMEM((512, 512), BF16),
            pltpu.VMEM((512, 512), BF16),
        ],
        compiler_params=params(32),
        name="first_sections",
    )(inputs, forward_one)


def gather_rows(in_ref, chunks, rows):
    for tile in range(2):
        lanes = slice(tile * 128, tile * 128 + 128)
        stack = jnp.concatenate(
            [
                jnp.concatenate([in_ref[4 * g + i, :, lanes] for i in range(4)], axis=1)
                for g in range(4)
            ],
            axis=0,
        )
        moved = dot(stack, chunks[...]).astype(BF16)
        for j in range(4):
            for g in range(4):
                rows[(tile * 4 + j) * 32 : (tile * 4 + j) * 32 + 32, g * 128 : g * 128 + 128] = moved[
                    g * 32 : g * 32 + 32, j * 128 : j * 128 + 128
                ]


def spectrum_kernel(in_ref, kernel_ref, forward_ref, inverse_ref, out_ref, chunks, turned, rows):
    @pl.when(pl.program_id(0) == 0)
    def _():
        chunks[...] = chunk_matrix(4, 32)
        turned[...] = inverse_ref[...].astype(F32).T.astype(BF16)

    gather_rows(in_ref, chunks, rows)
    spectrum = dot(rows[...], forward_ref[...])
    scaled = (spectrum * kernel_ref[...].reshape(256, 512).astype(F32)).astype(BF16)
    out_ref[...] = dot(turned[...], scaled, NT).astype(BF16)


def partial_inverses(sections, kernel, forward_two, inverse_two):
    channels = kernel.shape[0]
    return pl.pallas_call(
        spectrum_kernel,
        grid=(channels // 8,),
        in_specs=[
            pl.BlockSpec((16, 32, 256), lambda g: (0, 0, g)),
            pl.BlockSpec((8, 32, 512), lambda g: (g, 0, 0)),
            whole((512, 512)),
            whole((512, 512)),
        ],
        out_specs=pl.BlockSpec((512, 256), lambda g: (0, g)),
        out_shape=jax.ShapeDtypeStruct((512, channels * 32), BF16),
        scratch_shapes=[
            pltpu.VMEM((512, 512), BF16),
            pltpu.VMEM((512, 512), BF16),
            pltpu.VMEM((256, 512), BF16),
        ],
        compiler_params=params(32),
        name="partial_inverses",
    )(sections, kernel, forward_two, inverse_two)


def resid_kernel(in_ref, x_ref, inverse_ref, out_ref, chunks, swap, rows, mixed):
    @pl.when(pl.program_id(0) == 0)
    def _():
        chunks[...] = chunk_matrix(4, 32)
        swap[...] = swap_matrix(16)

    for part in range(2):
        gather_rows(in_ref.at[:, :, part * 256 : part * 256 + 256], chunks, rows)
        mixed[part * 256 : part * 256 + 256, :] = dot(rows[...], inverse_ref[...])
    for half in range(2):
        stack = jnp.concatenate(
            [mixed[c * 32 + half * 16 : c * 32 + half * 16 + 16, :] for c in range(16)], axis=0
        )
        high = stack.astype(BF16)
        rest = stack - high.astype(F32)
        mid = rest.astype(BF16)
        low = (rest - mid.astype(F32)).astype(BF16)
        moved = dot(swap[...], high) + dot(swap[...], mid) + dot(swap[...], low)
        for a in range(16):
            i = half * 16 + a
            value = x_ref[:, i * 512 : i * 512 + 512].astype(F32) + moved[a * 16 : a * 16 + 16]
            out_ref[i // 2, :, (i % 2) * 512 : (i % 2) * 512 + 512] = value.astype(BF16)


def residuals(parts, inputs, inverse_one):
    channels, positions = inputs.shape
    return pl.pallas_call(
        resid_kernel,
        grid=(channels // 16,),
        in_specs=[
            pl.BlockSpec((16, 32, 512), lambda g: (0, 0, g)),
            pl.BlockSpec((16, positions), lambda g: (g, 0)),
            whole((512, 512)),
        ],
        out_specs=pl.BlockSpec((16, 16, 1024), lambda g: (0, g, 0)),
        out_shape=jax.ShapeDtypeStruct((16, channels, positions // 16), BF16),
        scratch_shapes=[
            pltpu.VMEM((512, 512), BF16),
            pltpu.VMEM((256, 256), BF16),
            pltpu.VMEM((256, 512), BF16),
            pltpu.VMEM((512, 512), F32),
        ],
        compiler_params=params(32),
        name="residuals",
    )(parts, inputs, inverse_one)


def mlp_kernel(x_ref, gain_ref, gate_ref, up_ref, down_ref, out_ref, turned):
    hidden_units, channels = gate_ref.shape
    width = x_ref.shape[2]

    @pl.when(pl.program_id(0) == 0)
    def _():
        for h in range(0, hidden_units, 256):
            turned[:, h : h + 256] = down_ref[h : h + 256, :].astype(F32).T.astype(BF16)

    stream = x_ref[...].reshape(channels, width).astype(F32)
    mean_square = jnp.mean(stream * stream, axis=0, keepdims=True)
    normed = (stream * lax.rsqrt(mean_square + 1e-05) * gain_ref[...]).astype(BF16)
    total = stream
    step = 512
    for h in range(0, hidden_units, step):
        gate_part = dot(gate_ref[h : h + step, :], normed)
        up_part = dot(up_ref[h : h + step, :], normed)
        curve = 0.7978845608 * (gate_part + 0.044715 * gate_part * gate_part * gate_part)
        hidden = (0.5 * gate_part * (1.0 + jnp.tanh(curve)) * up_part).astype(BF16)
        total = total + dot(turned[:, h : h + step], hidden)
    out_ref[...] = total.astype(BF16).reshape(out_ref.shape)


def mlp(tokens, norm_gain, weights):
    sources, channels_each, count = tokens.shape
    hidden_units = weights.shape[0]
    channels = sources * channels_each
    tile = 256
    weight = lambda w: pl.BlockSpec((hidden_units, channels), lambda t: (0, w), pipeline_mode=pl.Buffered(1))
    block = pl.BlockSpec((sources, channels_each, tile), lambda t: (0, 0, t))
    return pl.pallas_call(
        mlp_kernel,
        grid=(count // tile,),
        in_specs=[block, whole((channels, 1)), weight(0), weight(1), weight(2)],
        out_specs=block,
        out_shape=jax.ShapeDtypeStruct(tokens.shape, BF16),
        scratch_shapes=[pltpu.VMEM((channels, hidden_units), BF16)],
        compiler_params=params(48),
        name="mlp",
    )(tokens, norm_gain.reshape(channels, 1), weights, weights, weights)


def gather_weights(w_gate, w_up, w_down, lines):
    half = w_gate.shape[0] // 2
    start = lax.axis_index("core") * half
    mine = jnp.concatenate(
        [lax.dynamic_slice_in_dim(w, start, half, 0) for w in (w_gate, w_up, w_down)], axis=1
    )
    pieces = [mine] + [
        lax.ppermute(mine, "zl", [(i, i ^ d) for i in range(lines)]) for d in range(1, lines)
    ]
    return lax.all_gather(jnp.concatenate(pieces, axis=0), ("y", "core"), axis=0, tiled=True)


def exchange(value, axes):
    return lax.all_to_all(value, axes, split_axis=0, concat_axis=0, tiled=True)


def shards(
    inputs,
    kernel,
    forward_one,
    forward_two,
    inverse_one,
    inverse_two,
    norm_gain,
    w_gate,
    w_up,
    w_down,
    lines,
):
    channels = inputs.shape[0]
    weights = gather_weights(w_gate, w_up, w_down, lines)
    sections = first_sections(inputs, forward_one).reshape(16, 32, channels * 32)
    parts = partial_inverses(exchange(sections, SEQ_AXES), kernel, forward_two, inverse_two)
    parts = exchange(parts.reshape(16, 32, channels * 32), SEQ_AXES)
    tokens = exchange(residuals(parts, inputs, inverse_one), CHAN_AXES)
    result = exchange(mlp(tokens, norm_gain, weights), CHAN_AXES)
    return result.transpose(1, 0, 2).reshape(inputs.shape)


def solution(mesh):
    fine = Mesh(mesh.devices.reshape(2, 4, 2, 4, 4), ("zh", "x", "core", "y", "zl"))
    return jax.shard_map(
        functools.partial(shards, lines=4),
        mesh=fine,
        in_specs=(
            P(CHAN_AXES, SEQ_AXES),
            P(CHAN_AXES, SEQ_AXES, None),
            P(),
            P(),
            P(),
            P(),
            P(),
            P(CHAN_AXES, None),
            P(CHAN_AXES, None),
            P(CHAN_AXES, None),
        ),
        out_specs=P(CHAN_AXES, SEQ_AXES),
        check_vma=False,
    )
```

time: 400 us -> 252 us (0.63)
  local copies, waits for them, and re-layouts: 95.2 us -> 3.49 us
  waiting for transfers between devices: 91.8 us -> 54.9 us
  blocking collectives: 151 us -> 121 us
  Pallas kernels: 0 us -> 28 us
  matrix products: 27 us -> 0 us
  starting transfers between devices: 18.1 us -> 28.9 us
    all_to_all x2 -> x1, waiting for transfers between devices: 90.1 us -> 39.1 us  [exchange(): return lax.all_to_all(value, axes, split_axis=0, concat_axis=0, tiled=True)]
    all_to_all x7 -> x0, local copies, waits for them, and re-layouts: 46.6 us -> none  [the longest x2 21 us: shards(): lax.all_to_all(partial_inv, 'seq', split_axis=2, concat_axis=1, tiled=True)]
    unnamed x21 -> x16, local copies, waits for them, and re-layouts: 33.6 us -> 0.94 us
    all_to_all x2 -> x3, blocking collectives: 151 us -> 121 us  [exchange(): return lax.all_to_all(value, axes, split_axis=0, concat_axis=0, tiled=True)]
    pallas_call x0 -> x4, Pallas kernels: none -> 28 us  [the longest x1 14.6 us: mlp(): pl.pallas_call(mlp_kernel, grid=(count // tile,), in_specs=[block, whole(...]
    dot_general x5 -> x0, matrix products: 27 us -> none  [the longest x1 11.3 us: shards(): lax.dot_general(down_rows, hidden, (((0,), (0,)), ((), ())), preferred_el...]
    ppermute x0 -> x3, waiting for transfers between devices: none -> 15.8 us  [gather_weights(): lax.ppermute(mine, 'zl', [(i, i ^ d) for i in range(lines)])]
    convert_element_type x2 -> x0, local copies, waits for them, and re-layouts: 15 us -> none  [the longest x1 7.49 us: shards(): first_section = jnp.einsum('cab,bk->cak', cube, forward_one, preferred_el...]
  transfers between devices with their start and end apart: 5 -> 5, of which waited for: 2 -> 3; matrix products, arithmetic and copies ran while one was open for 22% -> 0% of each run, Pallas kernels for 0% -> 5%
where the time goes in v1:
time: 252 us; the launch traced here: 251 us
  blocking collectives  121 us (48%)
  waiting for transfers between devices  54.9 us (22%)
  starting transfers between devices  28.9 us (11%)
  Pallas kernels  28 us (11%)
  between operations  13.5 us (5%)
  local copies, waits for them, and re-layouts  3.49 us (1%)
    all_to_all x3, blocking collectives, exchange(): return lax.all_to_all(value, axes, split_axis=0, concat_axis=0, tiled=True)  121 us
    all_to_all x1, waiting for transfers between devices, exchange(): return lax.all_to_all(value, axes, split_axis=0, concat_axis=0, tiled=True)  39.1 us
    all_to_all x1, starting transfers between devices, exchange(): return lax.all_to_all(value, axes, split_axis=0, concat_axis=0, tiled=True)  23.6 us
    ppermute x3, waiting for transfers between devices, gather_weights(): lax.ppermute(mine, 'zl', [(i, i ^ d) for i in range(lines)])  15.8 us
    pallas_call x1, Pallas kernels, mlp(): pl.pallas_call(mlp_kernel, grid=(count // tile,), in_specs=[block, whole(...  14.6 us
    pallas_call x1, Pallas kernels, residuals(): pl.pallas_call(resid_kernel, grid=(channels // 16,), in_specs=[pl.BlockSp...  5.49 us
    pallas_call x1, Pallas kernels, partial_inverses(): pl.pallas_call(spectrum_kernel, grid=(channels // 8,), in_specs=[pl.Block...  5.41 us
    ppermute x3, starting transfers between devices, gather_weights(): lax.ppermute(mine, 'zl', [(i, i ^ d) for i in range(lines)])  5.28 us
  transfers between devices with their start and end apart: 5, of which 3 were waited for; matrix products, arithmetic and copies ran while one was open for 0% of the time, Pallas kernels for 5%

profile of v1, /device:TPU:6, one launch (start us, length us, event | category | flops | bytes accessed | tf_op | source)
XLA Modules:
  0.0 250.8 jit_solution(14781110444105044051)
XLA Ops:
  6.5 0.0 copy-start
  6.5 0.0 all-gather.2.cloned.1.call-start
  6.5 0.9 copy-done
  7.4 0.0 copy-start.1
  7.4 0.0 copy-start.3
  7.5 1.1 constant_dynamic-slice_fusion
  8.6 2.0 collective-permute-start
  10.6 3.3 %collective-permute-start.1 = (bf16[48,2304]{1,0:T(8,128)(2,1)S(1)}, bf16[48,2304]{1,0:T(8,128)(2,1)S(1)}, u32[]{:S(2)}, u32[]{:S(2)}) collective-permute-start(bf16[48,2304]{1,0:T(8,128)(2,1)S(1)} %pad_maximum_fusion.1), channel_id=1, source_target_pairs={{0,2},{1,3},{2,0},{3,1},{4,6},{5,7},{6,4},{7,5},{8,10},{9,11},{10,... | collective-permute-start | bytes 663560 | tf_op jit(solution)/shard_map/ppermute | solution.py:229
  13.8 0.0 collective-permute-start.2
  13.8 6.2 %collective-permute-done = bf16[48,2304]{1,0:T(8,128)(2,1)S(1)} collective-permute-done((bf16[48,2304]{1,0:T(8,128)(2,1)S(1)}, bf16[48,2304]{1,0:T(8,128)(2,1)S(1)}, u32[]{:S(2)}, u32[]{:S(2)}) %collective-permute-start) | collective-permute-done | bytes 221216 | tf_op jit(solution)/shard_map/ppermute | solution.py:229
  20.1 9.5 %collective-permute-done.1 = bf16[48,2304]{1,0:T(8,128)(2,1)S(1)} collective-permute-done((bf16[48,2304]{1,0:T(8,128)(2,1)S(1)}, bf16[48,2304]{1,0:T(8,128)(2,1)S(1)}, u32[]{:S(2)}, u32[]{:S(2)}) %collective-permute-start.1) | collective-permute-done | bytes 221216 | tf_op jit(solution)/shard_map/ppermute | solution.py:229
  29.6 0.0 collective-permute-done.2
  29.6 1.0 pad_maximum_fusion
  30.6 0.0 all-gather.2.cloned.1.call-update
  30.6 0.0 copy-done.1
  30.6 0.0 copy-done.3
  30.6 2.5 first_sections.1
  33.1 0.0 copy-start.2
  33.2 0.0 copy-start.5
  33.2 0.0 copy-start.6
  33.2 34.2 %all_to_all.20.in_ref = bf16[16,32,1536]{2,1,0:T(8,128)(2,1)S(1)} all-to-all(bf16[16,32,1536]{2,1,0:T(8,128)(2,1)S(1)} %bitcast.5), channel_id=1, replica_groups=mesh['zh'=2,'x'=4,'core'=2,'y'=4,'zl'=4] {'zh','x','core'}, dimensions={0} | all-to-all | bytes 3145728 | tf_op jit(solution)/shard_map/all_to_all | solution.py:235
  67.3 0.0 copy-done.2
  67.3 0.0 copy-done.5
  67.4 0.0 copy-done.6
  67.4 5.4 %partial_inverses.1 = bf16[512,1536]{1,0:T(8,128)(2,1)S(1)} custom-call(bf16[16,32,1536]{2,1,0:T(8,128)(2,1)S(1)} %all_to_all.20.in_ref, bf16[48,32,512]{2,1,0:T(8,128)(2,1)S(1)} %copy-done.2, bf16[512,512]{1,0:T(8,128)(2,1)S(1)} %copy-done.5, bf16[512,512]{1,0:T(8,128)(2,1)S(1)} %copy-done.6), custom_call_target="tpu_custom_call" | custom-call | tf_op jit(solution)/shard_map/partial_inverses/pallas_call | solution.py:112
  72.8 0.0 copy-start.4
  72.8 44.2 %all_to_all.21.in_ref = bf16[16,32,1536]{2,1,0:T(8,128)(2,1)S(1)} all-to-all(bf16[16,32,1536]{2,1,0:T(8,128)(2,1)S(1)} %bitcast.6), channel_id=1, replica_groups=mesh['zh'=2,'x'=4,'core'=2,'y'=4,'zl'=4] {'zh','x','core'}, dimensions={0} | all-to-all | bytes 3145728 | tf_op jit(solution)/shard_map/all_to_all | solution.py:235
  117.0 0.0 copy-done.4
  117.0 5.5 %residuals.1 = bf16[16,48,1024]{2,1,0:T(8,128)(2,1)} custom-call(bf16[16,32,1536]{2,1,0:T(8,128)(2,1)S(1)} %all_to_all.21.in_ref, bf16[48,16384]{1,0:T(8,128)(2,1)S(1)} %copy-done.1, bf16[512,512]{1,0:T(8,128)(2,1)S(1)} %copy-done.4), custom_call_target="tpu_custom_call" | custom-call | tf_op jit(solution)/shard_map/residuals/pallas_call | solution.py:159
  122.5 0.0 copy-start.7
  122.5 23.6 %all-to-all-start.2 = ((bf16[16,48,1024]{2,1,0:T(8,128)(2,1)}), bf16[16,48,1024]{2,1,0:T(8,128)(2,1)S(1)}, u32[]{:S(2)}, u32[]{:S(2)}) async-start(bf16[16,48,1024]{2,1,0:T(8,128)(2,1)} %residuals.1), calls=%async_computation.2 | async-start | bytes 3145728 | tf_op jit(solution)/shard_map/all_to_all | solution.py:235
  146.1 0.0 copy-done.7
  146.1 0.2 reshape.16.gain_ref
  146.2 39.1 %all-to-all-done.2.x_ref = bf16[16,48,1024]{2,1,0:T(8,128)(2,1)S(1)} async-done(((bf16[16,48,1024]{2,1,0:T(8,128)(2,1)}), bf16[16,48,1024]{2,1,0:T(8,128)(2,1)S(1)}, u32[]{:S(2)}, u32[]{:S(2)}) %all-to-all-start.2) | async-done | bytes 1572896 | tf_op jit(solution)/shard_map/all_to_all | solution.py:235
  185.3 0.0 all-gather.2.cloned.1.call-done.gate_ref.up_ref.down_ref
  185.4 14.6 %mlp.1 = bf16[16,48,1024]{2,1,0:T(8,128)(2,1)S(1)} custom-call(bf16[16,48,1024]{2,1,0:T(8,128)(2,1)S(1)} %all-to-all-done.2.x_ref, f32[768,1]{1,0:T(8,128)S(1)} %reshape.16.gain_ref, bf16[1536,2304]{1,0:T(8,128)(2,1)} %all-gather.2.cloned.1.call-done.gate_ref.up_ref.down_ref, bf16[1536,2304]{1,0:T(8,128)(2,1)} %all-gather.2.cloned.1.call-done.gate_ref.up_ref.down_ref, ...), custom_call_target="tpu_custom_call" | custom-call | tf_op jit(solution)/shard_map/mlp/pallas_call | solution.py:210
  200.0 42.6 %all_to_all.22 = bf16[16,48,1024]{2,1,0:T(8,128)(2,1)S(1)} all-to-all(bf16[16,48,1024]{2,1,0:T(8,128)(2,1)S(1)} %mlp.1), channel_id=1, replica_groups=mesh['zh'=2,'x'=4,'core'=2,'y'=4,'zl'=4] {'y','zl'}, dimensions={0} | all-to-all | bytes 3145728 | tf_op jit(solution)/shard_map/all_to_all | solution.py:235
  242.6 1.3 copy.13
  (2 shorter events, 0.0 us)
Async XLA Ops:
  6.5 0.9 copy-start
  6.5 178.8 %all-gather.2.cloned.1.call-start = ((), (), s32[]{:S(2)}) async-start(), calls=%async_computation.4 | async-start | bytes 7962624 | tf_op jit(solution)/shard_map/all_gather | solution.py:231
  7.4 23.2 %copy-start.1 = (bf16[48,16384]{1,0:T(8,128)(2,1)S(1)}, bf16[48,16384]{1,0:T(8,128)(2,1)}, u32[]{:S(2)}) copy-start(bf16[48,16384]{1,0:T(8,128)(2,1)} %x_ref.3) | copy-start | bytes 4718596
  7.4 23.2 %copy-start.3 = (bf16[512,512]{1,0:T(8,128)(2,1)S(1)}, bf16[512,512]{1,0:T(8,128)(2,1)}, u32[]{:S(2)}) copy-start(bf16[512,512]{1,0:T(8,128)(2,1)} %factor_ref.1) | copy-start | bytes 1572868
  8.6 11.5 %collective-permute-start = (bf16[48,2304]{1,0:T(8,128)(2,1)S(1)}, bf16[48,2304]{1,0:T(8,128)(2,1)S(1)}, u32[]{:S(2)}, u32[]{:S(2)}) collective-permute-start(bf16[48,2304]{1,0:T(8,128)(2,1)S(1)} %pad_maximum_fusion.1), channel_id=1, source_target_pairs={{0,1},{1,0},{2,3},{3,2},{4,5},{5,4},{6,7},{7,6},{8,9},{9,8},{10,11... | collective-permute-start | bytes 663560 | tf_op jit(solution)/shard_map/ppermute | solution.py:229
  10.6 19.0 %collective-permute-start.1 = (bf16[48,2304]{1,0:T(8,128)(2,1)S(1)}, bf16[48,2304]{1,0:T(8,128)(2,1)S(1)}, u32[]{:S(2)}, u32[]{:S(2)}) collective-permute-start(bf16[48,2304]{1,0:T(8,128)(2,1)S(1)} %pad_maximum_fusion.1), channel_id=1, source_target_pairs={{0,2},{1,3},{2,0},{3,1},{4,6},{5,7},{6,4},{7,5},{8,10},{9,11},{10,... | collective-permute-start | bytes 663560 | tf_op jit(solution)/shard_map/ppermute | solution.py:229
  13.8 15.8 %collective-permute-start.2 = (bf16[48,2304]{1,0:T(8,128)(2,1)S(1)}, bf16[48,2304]{1,0:T(8,128)(2,1)S(1)}, u32[]{:S(2)}, u32[]{:S(2)}) collective-permute-start(bf16[48,2304]{1,0:T(8,128)(2,1)S(1)} %pad_maximum_fusion.1), channel_id=1, source_target_pairs={{0,3},{1,2},{2,1},{3,0},{4,7},{5,6},{6,5},{7,4},{8,11},{9,10},{10,... | collective-permute-start | bytes 663560 | tf_op jit(solution)/shard_map/ppermute | solution.py:229
  33.1 34.2 %copy-start.2 = (bf16[48,32,512]{2,1,0:T(8,128)(2,1)S(1)}, bf16[48,32,512]{2,1,0:T(8,128)(2,1)}, u32[]{:S(2)}) copy-start(bf16[48,32,512]{2,1,0:T(8,128)(2,1)} %kernel_ref.1) | copy-start | bytes 4718596
  33.2 34.2 %copy-start.5 = (bf16[512,512]{1,0:T(8,128)(2,1)S(1)}, bf16[512,512]{1,0:T(8,128)(2,1)}, u32[]{:S(2)}) copy-start(bf16[512,512]{1,0:T(8,128)(2,1)} %forward_ref.1) | copy-start | bytes 1572868
  33.2 34.2 %copy-start.6 = (bf16[512,512]{1,0:T(8,128)(2,1)S(1)}, bf16[512,512]{1,0:T(8,128)(2,1)}, u32[]{:S(2)}) copy-start(bf16[512,512]{1,0:T(8,128)(2,1)} %inverse_ref.2) | copy-start | bytes 1572868
  72.8 44.2 %copy-start.4 = (bf16[512,512]{1,0:T(8,128)(2,1)S(1)}, bf16[512,512]{1,0:T(8,128)(2,1)}, u32[]{:S(2)}) copy-start(bf16[512,512]{1,0:T(8,128)(2,1)} %inverse_ref.3) | copy-start | bytes 1572868
  122.5 23.6 %copy-start.7 = (f32[768]{0:T(1024)S(1)}, f32[768]{0:T(1024)}, u32[]{:S(2)}) copy-start(f32[768]{0:T(1024)} %param.16) | copy-start | bytes 9220
  122.5 62.9 %all-to-all-start.2 = ((bf16[16,48,1024]{2,1,0:T(8,128)(2,1)}), bf16[16,48,1024]{2,1,0:T(8,128)(2,1)S(1)}, u32[]{:S(2)}, u32[]{:S(2)}) async-start(bf16[16,48,1024]{2,1,0:T(8,128)(2,1)} %residuals.1), calls=%async_computation.2 | async-start | bytes 3145728 | tf_op jit(solution)/shard_map/all_to_all | solution.py:235
Sparse Core Ops, SparseCore 0:
  30.7 50.8 all-gather.1

commit v2 on v1

--- a/solution.py
+++ b/solution.py
@@ -18,6 +18,10 @@
 
 def params(mib):
     return pltpu.CompilerParams(vmem_limit_bytes=mib << 20)
+
+
+def in_hbm(*values):
+    return [pltpu.with_memory_space_constraint(value, pltpu.HBM) for value in values]
 
 
 def whole(shape):
@@ -74,7 +78,7 @@
         ],
         compiler_params=params(32),
         name="first_sections",
-    )(inputs, forward_one)
+    )(*in_hbm(inputs, forward_one))
 
 
 def gather_rows(in_ref, chunks, rows):
@@ -127,31 +131,34 @@
         ],
         compiler_params=params(32),
         name="partial_inverses",
-    )(sections, kernel, forward_two, inverse_two)
-
-
-def resid_kernel(in_ref, x_ref, inverse_ref, out_ref, chunks, swap, rows, mixed):
+    )(sections, *in_hbm(kernel, forward_two, inverse_two))
+
+
+def resid_kernel(in_ref, x_ref, inverse_ref, out_ref, chunks, swap, rows, total):
     @pl.when(pl.program_id(0) == 0)
     def _():
         chunks[...] = chunk_matrix(4, 32)
         swap[...] = swap_matrix(16)
 
+    for half in range(2):
+        stack = jnp.concatenate(
+            [x_ref[:, (half * 16 + i) * 512 : (half * 16 + i + 1) * 512] for i in range(16)], axis=0
+        )
+        moved = dot(swap[...], stack)
+        for c in range(16):
+            total[c * 32 + half * 16 : c * 32 + half * 16 + 16, :] = moved[c * 16 : c * 16 + 16]
     for part in range(2):
         gather_rows(in_ref.at[:, :, part * 256 : part * 256 + 256], chunks, rows)
-        mixed[part * 256 : part * 256 + 256, :] = dot(rows[...], inverse_ref[...])
+        here = slice(part * 256, part * 256 + 256)
+        total[here, :] = total[here, :] + dot(rows[...], inverse_ref[...])
     for half in range(2):
         stack = jnp.concatenate(
-            [mixed[c * 32 + half * 16 : c * 32 + half * 16 + 16, :] for c in range(16)], axis=0
+            [total[c * 32 + half * 16 : c * 32 + half * 16 + 16, :] for c in range(16)], axis=0
         )
-        high = stack.astype(BF16)
-        rest = stack - high.astype(F32)
-        mid = rest.astype(BF16)
-        low = (rest - mid.astype(F32)).astype(BF16)
-        moved = dot(swap[...], high) + dot(swap[...], mid) + dot(swap[...], low)
+        moved = dot(swap[...], stack.astype(BF16)).astype(BF16)
         for a in range(16):
             i = half * 16 + a
-            value = x_ref[:, i * 512 : i * 512 + 512].astype(F32) + moved[a * 16 : a * 16 + 16]
-            out_ref[i // 2, :, (i % 2) * 512 : (i % 2) * 512 + 512] = value.astype(BF16)
+            out_ref[i // 2, :, (i % 2) * 512 : (i % 2) * 512 + 512] = moved[a * 16 : a * 16 + 16]
 
 
 def residuals(parts, inputs, inverse_one):
@@ -174,61 +181,116 @@
         ],
         compiler_params=params(32),
         name="residuals",
-    )(parts, inputs, inverse_one)
-
-
-def mlp_kernel(x_ref, gain_ref, gate_ref, up_ref, down_ref, out_ref, turned):
-    hidden_units, channels = gate_ref.shape
-    width = x_ref.shape[2]
-
-    @pl.when(pl.program_id(0) == 0)
-    def _():
-        for h in range(0, hidden_units, 256):
-            turned[:, h : h + 256] = down_ref[h : h + 256, :].astype(F32).T.astype(BF16)
-
-    stream = x_ref[...].reshape(channels, width).astype(F32)
-    mean_square = jnp.mean(stream * stream, axis=0, keepdims=True)
-    normed = (stream * lax.rsqrt(mean_square + 1e-05) * gain_ref[...]).astype(BF16)
-    total = stream
-    step = 512
-    for h in range(0, hidden_units, step):
-        gate_part = dot(gate_ref[h : h + step, :], normed)
-        up_part = dot(up_ref[h : h + step, :], normed)
+    )(parts, *in_hbm(inputs, inverse_one))
+
+
+def layout_kernel(core_ref, *refs):
+    pieces, (gate_ref, up_ref, down_ref) = refs[:-3], refs[-3:]
+    count = len(pieces) // 2
+    rows, columns = pieces[0].shape
+    channels, odd = 2 * columns // 3, columns // 3
+
+    def emit(lefts, rights):
+        for n, (left, right) in enumerate(zip(lefts, rights)):
+            here = slice(n * rows, n * rows + rows)
+            gate_ref[here, :] = left[:, :channels]
+            up_ref[here, :odd] = left[:, channels:]
+            up_ref[here, odd:] = right[:, :odd]
+            down_ref[:, here] = right[:, odd:].astype(F32).T.astype(BF16)
+
+    @pl.when(core_ref[0] == 0)
+    def _():
+        emit(pieces[:count], pieces[count:])
+
+    @pl.when(core_ref[0] == 1)
+    def _():
+        emit(pieces[count:], pieces[:count])
+
+
+def lay_out(core, mine, others):
+    rows, columns = mine[0].shape
+    channels, hidden_units = 2 * columns // 3, rows * len(mine)
+    pieces = [*mine, *others]
+    return pl.pallas_call(
+        layout_kernel,
+        in_specs=[pl.BlockSpec(memory_space=pltpu.SMEM)] + [whole((rows, columns))] * len(pieces),
+        grid=(1,),
+        out_specs=[
+            whole((hidden_units, channels)),
+            whole((hidden_units, channels)),
+            whole((channels, hidden_units)),
+        ],
+        out_shape=[
+            jax.ShapeDtypeStruct((hidden_units, channels), BF16),
+            jax.ShapeDtypeStruct((hidden_units, channels), BF16),
+            jax.ShapeDtypeStruct((channels, hidden_units), BF16),
+        ],
+        compiler_params=params(40),
+        cost_estimate=pl.CostEstimate(flops=0, bytes_accessed=12 * rows * columns * len(pieces), transcendentals=0),
+        name="lay_out_weights",
+    )(core.reshape(1), *pieces)
+
+
+def mlp_kernel(x_ref, gain_ref, gate_ref, up_ref, down_ref, out_ref, normed, total):
+    channels, width = normed.shape
+    part = pl.program_id(0)
+
+    @pl.when(part == 0)
+    def _():
+        stream = x_ref[...].reshape(channels, width).astype(F32)
+        mean_square = jnp.mean(stream * stream, axis=0, keepdims=True)
+        normed[...] = (stream * lax.rsqrt(mean_square + 1e-05) * gain_ref[...]).astype(BF16)
+        total[...] = stream
+
+    for t in range(0, width, 512):
+        here = slice(t, t + 512)
+        gate_part = dot(gate_ref[...], normed[:, here])
+        up_part = dot(up_ref[...], normed[:, here])
         curve = 0.7978845608 * (gate_part + 0.044715 * gate_part * gate_part * gate_part)
         hidden = (0.5 * gate_part * (1.0 + jnp.tanh(curve)) * up_part).astype(BF16)
-        total = total + dot(turned[:, h : h + step], hidden)
-    out_ref[...] = total.astype(BF16).reshape(out_ref.shape)
+        total[:, here] = total[:, here] + dot(down_ref[...], hidden)
+
+    @pl.when(part == pl.num_programs(0) - 1)
+    def _():
+        out_ref[...] = total[...].astype(BF16).reshape(out_ref.shape)
 
 
 def mlp(tokens, norm_gain, weights):
     sources, channels_each, count = tokens.shape
-    hidden_units = weights.shape[0]
     channels = sources * channels_each
-    tile = 256
-    weight = lambda w: pl.BlockSpec((hidden_units, channels), lambda t: (0, w), pipeline_mode=pl.Buffered(1))
-    block = pl.BlockSpec((sources, channels_each, tile), lambda t: (0, 0, t))
+    hidden_units = weights[0].shape[0]
+    step = 512
     return pl.pallas_call(
         mlp_kernel,
-        grid=(count // tile,),
-        in_specs=[block, whole((channels, 1)), weight(0), weight(1), weight(2)],
-        out_specs=block,
+        grid=(hidden_units // step,),
+        in_specs=[
+            whole(tokens.shape),
+            whole((channels, 1)),
+            pl.BlockSpec((step, channels), lambda h: (h, 0)),
+            pl.BlockSpec((step, channels), lambda h: (h, 0)),
+            pl.BlockSpec((channels, step), lambda h: (0, h)),
+        ],
+        out_specs=whole(tokens.shape),
         out_shape=jax.ShapeDtypeStruct(tokens.shape, BF16),
-        scratch_shapes=[pltpu.VMEM((channels, hidden_units), BF16)],
-        compiler_params=params(48),
+        scratch_shapes=[pltpu.VMEM((channels, count), BF16), pltpu.VMEM((channels, count), F32)],
+        compiler_params=params(40),
         name="mlp",
-    )(tokens, norm_gain.reshape(channels, 1), weights, weights, weights)
-
-
-def gather_weights(w_gate, w_up, w_down, lines):
-    half = w_gate.shape[0] // 2
-    start = lax.axis_index("core") * half
-    mine = jnp.concatenate(
-        [lax.dynamic_slice_in_dim(w, start, half, 0) for w in (w_gate, w_up, w_down)], axis=1
-    )
-    pieces = [mine] + [
-        lax.ppermute(mine, "zl", [(i, i ^ d) for i in range(lines)]) for d in range(1, lines)
+    )(tokens, norm_gain.reshape(channels, 1), *in_hbm(*weights))
+
+
+def pack(w_gate, w_up, w_down, core):
+    rows, odd = w_gate.shape[0] // 4, w_up.shape[1] // 2
+    start = lax.axis_index("x") * rows
+    gate, up, down = (lax.dynamic_slice_in_dim(w, start, rows, 0) for w in (w_gate, w_up, w_down))
+    left = jnp.concatenate([gate, up[:, :odd]], axis=1)
+    right = jnp.concatenate([up[:, odd:], down], axis=1)
+    return jnp.where(core == 0, left, right)
+
+
+def with_partners(value, axis, size):
+    return [value] + [
+        lax.ppermute(value, axis, [(i, i ^ d) for i in range(size)]) for d in range(1, size)
     ]
-    return lax.all_gather(jnp.concatenate(pieces, axis=0), ("y", "core"), axis=0, tiled=True)
 
 
 def exchange(value, axes):
@@ -249,11 +311,22 @@
     lines,
 ):
     channels = inputs.shape[0]
-    weights = gather_weights(w_gate, w_up, w_down, lines)
+    core = lax.axis_index("core")
+    lined = with_partners(pack(w_gate, w_up, w_down, core), "zl", lines)
     sections = first_sections(inputs, forward_one).reshape(16, 32, channels * 32)
-    parts = partial_inverses(exchange(sections, SEQ_AXES), kernel, forward_two, inverse_two)
+    sections, lined = lax.optimization_barrier((sections, lined))
+    line = jnp.concatenate(lined, axis=0)
+    half = line.shape[0] // 2
+    first = [with_partners(line[:half], "x", lines), with_partners(line[half:], "y", lines)]
+    sections, first = lax.optimization_barrier((exchange(sections, SEQ_AXES), first))
+    pieces = with_partners(jnp.concatenate(first[0], axis=0), "y", lines)
+    pieces += with_partners(jnp.concatenate(first[1], axis=0), "x", lines)
+    parts = partial_inverses(sections, kernel, forward_two, inverse_two)
     parts = exchange(parts.reshape(16, 32, channels * 32), SEQ_AXES)
+    parts, pieces = lax.optimization_barrier((parts, pieces))
+    others = [lax.ppermute(piece, "core", [(0, 1), (1, 0)]) for piece in pieces]
     tokens = exchange(residuals(parts, inputs, inverse_one), CHAN_AXES)
+    weights = lay_out(core, pieces, others)
     result = exchange(mlp(tokens, norm_gain, weights), CHAN_AXES)
     return result.transpose(1, 0, 2).reshape(inputs.shape)
 

time: 252 us -> 227 us (0.901)
  blocking collectives: 121 us -> 42.6 us
  waiting for transfers between devices: 54.9 us -> 84.3 us
  starting transfers between devices: 28.9 us -> 56.6 us
  between operations: 13.5 us -> 0.2 us
  local copies, waits for them, and re-layouts: 3.49 us -> 10.3 us
  Pallas kernels: 28 us -> 32.3 us
    all_to_all x3 -> x1, blocking collectives: 121 us -> 42.6 us  [exchange(): return lax.all_to_all(value, axes, split_axis=0, concat_axis=0, tiled=True)]
    ppermute x3 -> x23, waiting for transfers between devices: 15.8 us -> 43.3 us  [the longest x15 38.9 us: with_partners(): lax.ppermute(value, axis, [(i, i ^ d) for i in range(size)])]
    ppermute x3 -> x23, starting transfers between devices: 5.28 us -> 27.6 us  [the longest x15 25.7 us: with_partners(): lax.ppermute(value, axis, [(i, i ^ d) for i in range(size)])]
    unnamed x16 -> x36, local copies, waits for them, and re-layouts: 0.94 us -> 7.25 us
    all_to_all x1 -> x3, starting transfers between devices: 23.6 us -> 29.1 us  [exchange(): return lax.all_to_all(value, axes, split_axis=0, concat_axis=0, tiled=True)]
    all_to_all x1 -> x3, waiting for transfers between devices: 39.1 us -> 41 us  [exchange(): return lax.all_to_all(value, axes, split_axis=0, concat_axis=0, tiled=True)]
    pallas_call x1 -> x2, Pallas kernels: 14.6 us -> 13.4 us  [the longest x1 10.6 us: mlp(): pl.pallas_call(mlp_kernel, grid=(hidden_units // step,), in_specs=[whole(...]
  transfers between devices with their start and end apart: 5 -> 26, of which waited for: 3 -> 16; matrix products, arithmetic and copies ran while one was open for 0% -> 0% of each run, Pallas kernels for 5% -> 3%
where the time goes in v2:
time: 227 us; the launch traced here: 226 us
  waiting for transfers between devices  84.3 us (37%)
  starting transfers between devices  56.6 us (25%)
  blocking collectives  42.6 us (19%)
  Pallas kernels  32.3 us (14%)
  local copies, waits for them, and re-layouts  10.3 us (5%)
    all_to_all x1, blocking collectives, exchange(): return lax.all_to_all(value, axes, split_axis=0, concat_axis=0, tiled=True)  42.6 us
    all_to_all x3, waiting for transfers between devices, exchange(): return lax.all_to_all(value, axes, split_axis=0, concat_axis=0, tiled=True)  41 us
    ppermute x15, waiting for transfers between devices, with_partners(): lax.ppermute(value, axis, [(i, i ^ d) for i in range(size)])  38.9 us
    all_to_all x3, starting transfers between devices, exchange(): return lax.all_to_all(value, axes, split_axis=0, concat_axis=0, tiled=True)  29.1 us
    ppermute x15, starting transfers between devices, with_partners(): lax.ppermute(value, axis, [(i, i ^ d) for i in range(size)])  25.7 us
    pallas_call x1, Pallas kernels, mlp(): pl.pallas_call(mlp_kernel, grid=(hidden_units // step,), in_specs=[whole(...  10.6 us
    pallas_call x1, Pallas kernels, partial_inverses(): pl.pallas_call(spectrum_kernel, grid=(channels // 8,), in_specs=[pl.Block...  7.78 us
    unnamed x36, local copies, waits for them, and re-layouts  7.25 us
  transfers between devices with their start and end apart: 26, of which 16 were waited for; matrix products, arithmetic and copies ran while one was open for 0% of the time, Pallas kernels for 3%

profile of v2, /device:TPU:6, one launch (start us, length us, event | category | flops | bytes accessed | tf_op | source)
XLA Modules:
  0.0 226.4 jit_solution(12700988727475901991)
XLA Ops:
  0.0 0.8 constant_dynamic-slice_fusion.1
  0.8 0.7 fusion
  1.6 2.0 collective-permute-start
  3.6 3.3 %collective-permute-start.1 = (bf16[24,1152]{1,0:T(8,128)(2,1)S(1)}, bf16[24,1152]{1,0:T(8,128)(2,1)S(1)}, u32[]{:S(2)}, u32[]{:S(2)}) collective-permute-start(bf16[24,1152]{1,0:T(8,128)(2,1)S(1)} %maximum_select_fusion), channel_id=1, source_target_pairs={{0,2},{1,3},{2,0},{3,1},{4,6},{5,7},{6,4},{7,5},{8,10},{9,11},{10,... | collective-permute-start | bytes 165896 | tf_op jit(solution)/shard_map/ppermute | solution.py:292
  6.8 0.0 collective-permute-start.2
  6.8 4.9 %first_sections.1 = bf16[512,1536]{1,0:T(8,128)(2,1)} custom-call(bf16[48,16384]{1,0:T(8,128)(2,1)} %x_ref.3, bf16[512,512]{1,0:T(8,128)(2,1)} %factor_ref.1), custom_call_target="tpu_custom_call" | custom-call | tf_op jit(solution)/shard_map/first_sections/pallas_call | solution.py:68
  11.8 0.0 collective-permute-done
  11.8 0.0 collective-permute-done.1
  11.8 1.0 collective-permute-done.2
  12.8 9.6 %all-to-all-start = ((bf16[16,32,1536]{2,1,0:T(8,128)(2,1)}), bf16[16,32,1536]{2,1,0:T(8,128)(2,1)S(1)}, u32[]{:S(2)}, u32[]{:S(2)}) async-start(bf16[16,32,1536]{2,1,0:T(8,128)(2,1)} %bitcast), calls=%async_computation | async-start | bytes 3145728 | tf_op jit(solution)/shard_map/all_to_all | solution.py:297
  22.4 1.7 collective-permute-start.6
  24.1 2.9 %collective-permute-start.7 = (bf16[48,1152]{1,0:T(8,128)(2,1)S(1)}, bf16[48,1152]{1,0:T(8,128)(2,1)S(1)}, u32[]{:S(2)}, u32[]{:S(2)}) collective-permute-start(bf16[48,1152]{1,0:T(8,128)(2,1)S(1)} %constant_dynamic-update-slice_fusion.2), channel_id=1, source_target_pairs={{0,8},{4,12},{8,0},{12,4},{1,9},{5,13},{9,1},{13,5},{2,10},{6,14},... | collective-permute-start | bytes 331784 | tf_op jit(solution)/shard_map/ppermute | solution.py:292
  27.0 0.2 collective-permute-start.8
  27.2 0.9 collective-permute-start.3
  28.2 0.7 collective-permute-start.4
  28.9 3.1 %collective-permute-start.5 = (bf16[48,1152]{1,0:T(8,128)(2,1)S(1)}, bf16[48,1152]{1,0:T(8,128)(2,1)S(1)}, u32[]{:S(2)}, u32[]{:S(2)}) collective-permute-start(bf16[48,1152]{1,0:T(8,128)(2,1)S(1)} %constant_dynamic-update-slice_fusion), channel_id=1, source_target_pairs={{0,96},{32,64},{64,32},{96,0},{1,97},{33,65},{65,33},{97,1},{2,98}... | collective-permute-start | bytes 331784 | tf_op jit(solution)/shard_map/ppermute | solution.py:292
  32.0 0.5 collective-permute-done.7
  32.6 2.0 collective-permute-done.8
  34.6 4.1 %collective-permute-done.3 = bf16[48,1152]{1,0:T(8,128)(2,1)S(1)} collective-permute-done((bf16[48,1152]{1,0:T(8,128)(2,1)S(1)}, bf16[48,1152]{1,0:T(8,128)(2,1)S(1)}, u32[]{:S(2)}, u32[]{:S(2)}) %collective-permute-start.3) | collective-permute-done | bytes 110624 | tf_op jit(solution)/shard_map/ppermute | solution.py:292
  38.7 2.7 %collective-permute-done.4 = bf16[48,1152]{1,0:T(8,128)(2,1)S(1)} collective-permute-done((bf16[48,1152]{1,0:T(8,128)(2,1)S(1)}, bf16[48,1152]{1,0:T(8,128)(2,1)S(1)}, u32[]{:S(2)}, u32[]{:S(2)}) %collective-permute-start.4) | collective-permute-done | bytes 110624 | tf_op jit(solution)/shard_map/ppermute | solution.py:292
  41.5 17.2 %all-to-all-done.in_ref = bf16[16,32,1536]{2,1,0:T(8,128)(2,1)S(1)} async-done(((bf16[16,32,1536]{2,1,0:T(8,128)(2,1)}), bf16[16,32,1536]{2,1,0:T(8,128)(2,1)S(1)}, u32[]{:S(2)}, u32[]{:S(2)}) %all-to-all-start) | async-done | bytes 1572896 | tf_op jit(solution)/shard_map/all_to_all | solution.py:297
  58.6 7.8 %partial_inverses.1 = bf16[512,1536]{1,0:T(8,128)(2,1)} custom-call(bf16[16,32,1536]{2,1,0:T(8,128)(2,1)S(1)} %all-to-all-done.in_ref, bf16[48,32,512]{2,1,0:T(8,128)(2,1)} %kernel_ref.1, bf16[512,512]{1,0:T(8,128)(2,1)} %forward_ref.1, bf16[512,512]{1,0:T(8,128)(2,1)} %inverse_ref.2), custom_call_target="tpu_custom_call" | custom-call | tf_op jit(solution)/shard_map/partial_inverses/pallas_call | solution.py:116
  66.4 7.0 %all-to-all-start.1 = ((bf16[16,32,1536]{2,1,0:T(8,128)(2,1)}), bf16[16,32,1536]{2,1,0:T(8,128)(2,1)S(1)}, u32[]{:S(2)}, u32[]{:S(2)}) async-start(bf16[16,32,1536]{2,1,0:T(8,128)(2,1)} %bitcast.1), calls=%async_computation.1 | async-start | bytes 3145728 | tf_op jit(solution)/shard_map/all_to_all | solution.py:297
  73.5 0.9 collective-permute-start.12
  74.4 0.7 collective-permute-start.13
  75.2 3.1 %collective-permute-start.14 = (bf16[192,1152]{1,0:T(8,128)(2,1)S(1)}, bf16[192,1152]{1,0:T(8,128)(2,1)}, u32[]{:S(2)}, u32[]{:S(2)}) collective-permute-start(bf16[192,1152]{1,0:T(8,128)(2,1)S(1)} %constant_dynamic-update-slice_fusion.8.refs_4_), channel_id=1, source_target_pairs={{0,96},{32,64},{64,32},{96,0},{1,97},{33,65},{65,33},{97,1},{2,98}... | collective-permute-start | bytes 1327112 | tf_op jit(solution)/shard_map/ppermute | solution.py:292
  78.4 3.4 %collective-permute-start.10 = (bf16[192,1152]{1,0:T(8,128)(2,1)S(1)}, bf16[192,1152]{1,0:T(8,128)(2,1)S(1)}, u32[]{:S(2)}, u32[]{:S(2)}) collective-permute-start(bf16[192,1152]{1,0:T(8,128)(2,1)S(1)} %constant_dynamic-update-slice_fusion.4.refs_0_), channel_id=1, source_target_pairs={{0,8},{4,12},{8,0},{12,4},{1,9},{5,13},{9,1},{13,5},{2,10},{6,14},... | collective-permute-start | bytes 1327112 | tf_op jit(solution)/shard_map/ppermute | solution.py:292
  81.7 1.1 collective-permute-start.11
  82.8 19.6 %collective-permute-done.12.refs_5_ = bf16[192,1152]{1,0:T(8,128)(2,1)S(1)} collective-permute-done((bf16[192,1152]{1,0:T(8,128)(2,1)S(1)}, bf16[192,1152]{1,0:T(8,128)(2,1)S(1)}, u32[]{:S(2)}, u32[]{:S(2)}) %collective-permute-start.12) | collective-permute-done | bytes 442400 | tf_op jit(solution)/shard_map/ppermute | solution.py:292
  102.3 1.7 collective-permute-start.9
  104.0 8.1 %collective-permute-done.13.refs_6_ = bf16[192,1152]{1,0:T(8,128)(2,1)} collective-permute-done((bf16[192,1152]{1,0:T(8,128)(2,1)S(1)}, bf16[192,1152]{1,0:T(8,128)(2,1)}, u32[]{:S(2)}, u32[]{:S(2)}) %collective-permute-start.13) | collective-permute-done | bytes 442400 | tf_op jit(solution)/shard_map/ppermute | solution.py:292
  112.1 0.0 collective-permute-done.14.refs_7_
  112.1 0.0 collective-permute-done.10.refs_2_
  112.1 0.0 collective-permute-done.11.refs_3_
  112.1 0.8 copy-done.5
  112.9 0.8 collective-permute-done.9.refs_1_
  113.7 6.2 %residuals.1 = bf16[16,48,1024]{2,1,0:T(8,128)(2,1)} custom-call(bf16[16,32,1536]{2,1,0:T(8,128)(2,1)S(1)} %all-to-all-done.1.in_ref, bf16[48,16384]{1,0:T(8,128)(2,1)} %x_ref.3, bf16[512,512]{1,0:T(8,128)(2,1)} %inverse_ref.3), custom_call_target="tpu_custom_call" | custom-call | tf_op jit(solution)/shard_map/residuals/pallas_call | solution.py:166
  119.9 12.5 %all-to-all-start.2 = ((bf16[16,48,1024]{2,1,0:T(8,128)(2,1)}), bf16[16,48,1024]{2,1,0:T(8,128)(2,1)S(1)}, u32[]{:S(2)}, u32[]{:S(2)}) async-start(bf16[16,48,1024]{2,1,0:T(8,128)(2,1)} %residuals.1), calls=%async_computation.2 | async-start | bytes 3145728 | tf_op jit(solution)/shard_map/all_to_all | solution.py:297
  132.4 0.1 collective-permute-start.15
  132.5 0.5 collective-permute-start.16
  133.0 0.1 collective-permute-start.17
  133.1 0.4 collective-permute-start.18
  133.5 0.1 collective-permute-start.19
  133.6 0.7 collective-permute-done.15.refs_8_
  134.2 0.1 collective-permute-start.20
  134.4 1.3 collective-permute-done.16.refs_9_
  135.7 0.1 collective-permute-start.21
  135.9 0.0 collective-permute-done.17.refs_10_
  135.9 0.4 collective-permute-start.22
  136.2 0.2 reshape.20.gain_ref
  136.4 0.6 collective-permute-done.18.refs_11_
  137.0 0.4 collective-permute-done.20.refs_13_
  137.4 0.8 collective-permute-done.21.refs_14_
  138.3 0.6 collective-permute-done.22.refs_15_
  138.9 1.0 copy-done.4
  139.9 1.0 copy-done.6
  140.9 2.9 %lay_out_weights.1 = (bf16[1536,768]{1,0:T(8,128)(2,1)S(1)}, bf16[1536,768]{1,0:T(8,128)(2,1)S(1)}, bf16[768,1536]{1,0:T(8,128)(2,1)S(1)}) custom-call(s32[1]{0:T(128)} %bitcast.2.core_ref, bf16[192,1152]{1,0:T(8,128)(2,1)S(1)} %constant_dynamic-update-slice_fusion.4.refs_0_, bf16[192,1152]{1,0:T(8,128)(2,1)} %collective-permute-done.9.refs_1_, ...), custom_call_target="tpu_custom_call" | custom-call | bytes 42467328 | tf_op jit(solution)/shard_map/lay_out_weights/pallas_call | solution.py:214
  143.8 1.4 copy-done
  145.2 1.4 copy-done.1
  146.7 1.4 copy-done.2
  148.1 23.8 %all-to-all-done.2.x_ref = bf16[16,48,1024]{2,1,0:T(8,128)(2,1)S(1)} async-done(((bf16[16,48,1024]{2,1,0:T(8,128)(2,1)}), bf16[16,48,1024]{2,1,0:T(8,128)(2,1)S(1)}, u32[]{:S(2)}, u32[]{:S(2)}) %all-to-all-start.2) | async-done | bytes 1572896 | tf_op jit(solution)/shard_map/all_to_all | solution.py:297
  171.9 10.6 %mlp.1 = bf16[16,48,1024]{2,1,0:T(8,128)(2,1)S(1)} custom-call(bf16[16,48,1024]{2,1,0:T(8,128)(2,1)S(1)} %all-to-all-done.2.x_ref, f32[768,1]{1,0:T(8,128)S(1)} %reshape.20.gain_ref, bf16[1536,768]{1,0:T(8,128)(2,1)} %copy-done, bf16[1536,768]{1,0:T(8,128)(2,1)} %copy-done.1, bf16[768,1536]{1,0:T(8,128)(2,1)} %copy-done.2), custom_call_target="tpu_custom_call" | custom-call | tf_op jit(solution)/shard_map/mlp/pallas_call | solution.py:263
  182.5 42.6 %all_to_all.20 = bf16[16,48,1024]{2,1,0:T(8,128)(2,1)S(1)} all-to-all(bf16[16,48,1024]{2,1,0:T(8,128)(2,1)S(1)} %mlp.1), channel_id=1, replica_groups=mesh['zh'=2,'x'=4,'core'=2,'y'=4,'zl'=4] {'y','zl'}, dimensions={0} | all-to-all | bytes 3145728 | tf_op jit(solution)/shard_map/all_to_all | solution.py:297
  225.1 1.3 copy.13
  (39 shorter events, 0.2 us)
Async XLA Ops:
  1.6 10.2 %collective-permute-start = (bf16[24,1152]{1,0:T(8,128)(2,1)S(1)}, bf16[24,1152]{1,0:T(8,128)(2,1)S(1)}, u32[]{:S(2)}, u32[]{:S(2)}) collective-permute-start(bf16[24,1152]{1,0:T(8,128)(2,1)S(1)} %maximum_select_fusion), channel_id=1, source_target_pairs={{0,1},{1,0},{2,3},{3,2},{4,5},{5,4},{6,7},{7,6},{8,9},{9,8},{10,11... | collective-permute-start | bytes 165896 | tf_op jit(solution)/shard_map/ppermute | solution.py:292
  3.6 8.2 %collective-permute-start.1 = (bf16[24,1152]{1,0:T(8,128)(2,1)S(1)}, bf16[24,1152]{1,0:T(8,128)(2,1)S(1)}, u32[]{:S(2)}, u32[]{:S(2)}) collective-permute-start(bf16[24,1152]{1,0:T(8,128)(2,1)S(1)} %maximum_select_fusion), channel_id=1, source_target_pairs={{0,2},{1,3},{2,0},{3,1},{4,6},{5,7},{6,4},{7,5},{8,10},{9,11},{10,... | collective-permute-start | bytes 165896 | tf_op jit(solution)/shard_map/ppermute | solution.py:292
  6.8 6.0 %collective-permute-start.2 = (bf16[24,1152]{1,0:T(8,128)(2,1)S(1)}, bf16[24,1152]{1,0:T(8,128)(2,1)S(1)}, u32[]{:S(2)}, u32[]{:S(2)}) collective-permute-start(bf16[24,1152]{1,0:T(8,128)(2,1)S(1)} %maximum_select_fusion), channel_id=1, source_target_pairs={{0,3},{1,2},{2,1},{3,0},{4,7},{5,6},{6,5},{7,4},{8,11},{9,10},{10,... | collective-permute-start | bytes 165896 | tf_op jit(solution)/shard_map/ppermute | solution.py:292
  12.8 45.8 %all-to-all-start = ((bf16[16,32,1536]{2,1,0:T(8,128)(2,1)}), bf16[16,32,1536]{2,1,0:T(8,128)(2,1)S(1)}, u32[]{:S(2)}, u32[]{:S(2)}) async-start(bf16[16,32,1536]{2,1,0:T(8,128)(2,1)} %bitcast), calls=%async_computation | async-start | bytes 3145728 | tf_op jit(solution)/shard_map/all_to_all | solution.py:297
  22.4 6.5 %collective-permute-start.6 = (bf16[48,1152]{1,0:T(8,128)(2,1)S(1)}, bf16[48,1152]{1,0:T(8,128)(2,1)S(1)}, u32[]{:S(2)}, u32[]{:S(2)}) collective-permute-start(bf16[48,1152]{1,0:T(8,128)(2,1)S(1)} %constant_dynamic-update-slice_fusion.2), channel_id=1, source_target_pairs={{0,4},{4,0},{8,12},{12,8},{1,5},{5,1},{9,13},{13,9},{2,6},{6,2},{1... | collective-permute-start | bytes 331784 | tf_op jit(solution)/shard_map/ppermute | solution.py:292
  24.1 8.5 %collective-permute-start.7 = (bf16[48,1152]{1,0:T(8,128)(2,1)S(1)}, bf16[48,1152]{1,0:T(8,128)(2,1)S(1)}, u32[]{:S(2)}, u32[]{:S(2)}) collective-permute-start(bf16[48,1152]{1,0:T(8,128)(2,1)S(1)} %constant_dynamic-update-slice_fusion.2), channel_id=1, source_target_pairs={{0,8},{4,12},{8,0},{12,4},{1,9},{5,13},{9,1},{13,5},{2,10},{6,14},... | collective-permute-start | bytes 331784 | tf_op jit(solution)/shard_map/ppermute | solution.py:292
  27.0 7.6 %collective-permute-start.8 = (bf16[48,1152]{1,0:T(8,128)(2,1)S(1)}, bf16[48,1152]{1,0:T(8,128)(2,1)S(1)}, u32[]{:S(2)}, u32[]{:S(2)}) collective-permute-start(bf16[48,1152]{1,0:T(8,128)(2,1)S(1)} %constant_dynamic-update-slice_fusion.2), channel_id=1, source_target_pairs={{0,12},{4,8},{8,4},{12,0},{1,13},{5,9},{9,5},{13,1},{2,14},{6,10},... | collective-permute-start | bytes 331784 | tf_op jit(solution)/shard_map/ppermute | solution.py:292
  27.2 11.5 %collective-permute-start.3 = (bf16[48,1152]{1,0:T(8,128)(2,1)S(1)}, bf16[48,1152]{1,0:T(8,128)(2,1)S(1)}, u32[]{:S(2)}, u32[]{:S(2)}) collective-permute-start(bf16[48,1152]{1,0:T(8,128)(2,1)S(1)} %constant_dynamic-update-slice_fusion), channel_id=1, source_target_pairs={{0,32},{32,0},{64,96},{96,64},{1,33},{33,1},{65,97},{97,65},{2,34}... | collective-permute-start | bytes 331784 | tf_op jit(solution)/shard_map/ppermute | solution.py:292
  28.2 13.3 %collective-permute-start.4 = (bf16[48,1152]{1,0:T(8,128)(2,1)S(1)}, bf16[48,1152]{1,0:T(8,128)(2,1)S(1)}, u32[]{:S(2)}, u32[]{:S(2)}) collective-permute-start(bf16[48,1152]{1,0:T(8,128)(2,1)S(1)} %constant_dynamic-update-slice_fusion), channel_id=1, source_target_pairs={{0,64},{32,96},{64,0},{96,32},{1,65},{33,97},{65,1},{97,33},{2,66}... | collective-permute-start | bytes 331784 | tf_op jit(solution)/shard_map/ppermute | solution.py:292
  28.9 37.5 %copy-start.7 = (bf16[48,1152]{1,0:T(8,128)(2,1)}, bf16[48,1152]{1,0:T(8,128)(2,1)S(1)}, u32[]{:S(2)}) copy-start(bf16[48,1152]{1,0:T(8,128)(2,1)S(1)} %collective-permute-done.6) | copy-start | bytes 331780
  28.9 12.6 %collective-permute-start.5 = (bf16[48,1152]{1,0:T(8,128)(2,1)S(1)}, bf16[48,1152]{1,0:T(8,128)(2,1)S(1)}, u32[]{:S(2)}, u32[]{:S(2)}) collective-permute-start(bf16[48,1152]{1,0:T(8,128)(2,1)S(1)} %constant_dynamic-update-slice_fusion), channel_id=1, source_target_pairs={{0,96},{32,64},{64,32},{96,0},{1,97},{33,65},{65,33},{97,1},{2,98}... | collective-permute-start | bytes 331784 | tf_op jit(solution)/shard_map/ppermute | solution.py:292
  32.6 33.8 %copy-start.9 = (bf16[48,1152]{1,0:T(8,128)(2,1)}, bf16[48,1152]{1,0:T(8,128)(2,1)S(1)}, u32[]{:S(2)}) copy-start(bf16[48,1152]{1,0:T(8,128)(2,1)S(1)} %collective-permute-done.7) | copy-start | bytes 331780
  34.6 31.8 %copy-start.11 = (bf16[48,1152]{1,0:T(8,128)(2,1)}, bf16[48,1152]{1,0:T(8,128)(2,1)S(1)}, u32[]{:S(2)}) copy-start(bf16[48,1152]{1,0:T(8,128)(2,1)S(1)} %collective-permute-done.8) | copy-start | bytes 331780
  66.4 7.0 %copy-start.8 = (bf16[48,1152]{1,0:T(8,128)(2,1)S(1)}, bf16[48,1152]{1,0:T(8,128)(2,1)}, u32[]{:S(2)}) copy-start(bf16[48,1152]{1,0:T(8,128)(2,1)} %copy-done.7) | copy-start | bytes 331780
  66.4 7.0 %copy-start.10 = (bf16[48,1152]{1,0:T(8,128)(2,1)S(1)}, bf16[48,1152]{1,0:T(8,128)(2,1)}, u32[]{:S(2)}) copy-start(bf16[48,1152]{1,0:T(8,128)(2,1)} %copy-done.9) | copy-start | bytes 331780
  66.4 7.1 %copy-start.12 = (bf16[48,1152]{1,0:T(8,128)(2,1)S(1)}, bf16[48,1152]{1,0:T(8,128)(2,1)}, u32[]{:S(2)}) copy-start(bf16[48,1152]{1,0:T(8,128)(2,1)} %copy-done.11) | copy-start | bytes 331780
  66.4 47.3 %all-to-all-start.1 = ((bf16[16,32,1536]{2,1,0:T(8,128)(2,1)}), bf16[16,32,1536]{2,1,0:T(8,128)(2,1)S(1)}, u32[]{:S(2)}, u32[]{:S(2)}) async-start(bf16[16,32,1536]{2,1,0:T(8,128)(2,1)} %bitcast.1), calls=%async_computation.1 | async-start | bytes 3145728 | tf_op jit(solution)/shard_map/all_to_all | solution.py:297
  73.5 28.8 %collective-permute-start.12 = (bf16[192,1152]{1,0:T(8,128)(2,1)S(1)}, bf16[192,1152]{1,0:T(8,128)(2,1)S(1)}, u32[]{:S(2)}, u32[]{:S(2)}) collective-permute-start(bf16[192,1152]{1,0:T(8,128)(2,1)S(1)} %constant_dynamic-update-slice_fusion.8.refs_4_), channel_id=1, source_target_pairs={{0,32},{32,0},{64,96},{96,64},{1,33},{33,1},{65,97},{97,65},{2,34}... | collective-permute-start | bytes 1327112 | tf_op jit(solution)/shard_map/ppermute | solution.py:292
  74.4 37.7 %collective-permute-start.13 = (bf16[192,1152]{1,0:T(8,128)(2,1)S(1)}, bf16[192,1152]{1,0:T(8,128)(2,1)}, u32[]{:S(2)}, u32[]{:S(2)}) collective-permute-start(bf16[192,1152]{1,0:T(8,128)(2,1)S(1)} %constant_dynamic-update-slice_fusion.8.refs_4_), channel_id=1, source_target_pairs={{0,64},{32,96},{64,0},{96,32},{1,65},{33,97},{65,1},{97,33},{2,66}... | collective-permute-start | bytes 1327112 | tf_op jit(solution)/shard_map/ppermute | solution.py:292
  75.2 37.0 %collective-permute-start.14 = (bf16[192,1152]{1,0:T(8,128)(2,1)S(1)}, bf16[192,1152]{1,0:T(8,128)(2,1)}, u32[]{:S(2)}, u32[]{:S(2)}) collective-permute-start(bf16[192,1152]{1,0:T(8,128)(2,1)S(1)} %constant_dynamic-update-slice_fusion.8.refs_4_), channel_id=1, source_target_pairs={{0,96},{32,64},{64,32},{96,0},{1,97},{33,65},{65,33},{97,1},{2,98}... | collective-permute-start | bytes 1327112 | tf_op jit(solution)/shard_map/ppermute | solution.py:292
  78.4 33.7 %collective-permute-start.10 = (bf16[192,1152]{1,0:T(8,128)(2,1)S(1)}, bf16[192,1152]{1,0:T(8,128)(2,1)S(1)}, u32[]{:S(2)}, u32[]{:S(2)}) collective-permute-start(bf16[192,1152]{1,0:T(8,128)(2,1)S(1)} %constant_dynamic-update-slice_fusion.4.refs_0_), channel_id=1, source_target_pairs={{0,8},{4,12},{8,0},{12,4},{1,9},{5,13},{9,1},{13,5},{2,10},{6,14},... | collective-permute-start | bytes 1327112 | tf_op jit(solution)/shard_map/ppermute | solution.py:292
  81.7 30.4 %collective-permute-start.11 = (bf16[192,1152]{1,0:T(8,128)(2,1)S(1)}, bf16[192,1152]{1,0:T(8,128)(2,1)S(1)}, u32[]{:S(2)}, u32[]{:S(2)}) collective-permute-start(bf16[192,1152]{1,0:T(8,128)(2,1)S(1)} %constant_dynamic-update-slice_fusion.4.refs_0_), channel_id=1, source_target_pairs={{0,12},{4,8},{8,4},{12,0},{1,13},{5,9},{9,5},{13,1},{2,14},{6,10},... | collective-permute-start | bytes 1327112 | tf_op jit(solution)/shard_map/ppermute | solution.py:292
  102.3 11.3 %collective-permute-start.9 = (bf16[192,1152]{1,0:T(8,128)(2,1)S(1)}, bf16[192,1152]{1,0:T(8,128)(2,1)}, u32[]{:S(2)}, u32[]{:S(2)}) collective-permute-start(bf16[192,1152]{1,0:T(8,128)(2,1)S(1)} %constant_dynamic-update-slice_fusion.4.refs_0_), channel_id=1, source_target_pairs={{0,4},{4,0},{8,12},{12,8},{1,5},{5,1},{9,13},{13,9},{2,6},{6,2},{1... | collective-permute-start | bytes 1327112 | tf_op jit(solution)/shard_map/ppermute | solution.py:292
  112.1 20.9 %copy-start.3 = (bf16[192,1152]{1,0:T(8,128)(2,1)}, bf16[192,1152]{1,0:T(8,128)(2,1)S(1)}, u32[]{:S(2)}) copy-start(bf16[192,1152]{1,0:T(8,128)(2,1)S(1)} %collective-permute-done.10.refs_2_) | copy-start | bytes 1327108
  112.1 0.8 copy-start.5
  119.9 16.4 %copy-start.13 = (f32[768]{0:T(1024)S(1)}, f32[768]{0:T(1024)}, u32[]{:S(2)}) copy-start(f32[768]{0:T(1024)} %param.16) | copy-start | bytes 9220
  119.9 52.0 %all-to-all-start.2 = ((bf16[16,48,1024]{2,1,0:T(8,128)(2,1)}), bf16[16,48,1024]{2,1,0:T(8,128)(2,1)S(1)}, u32[]{:S(2)}, u32[]{:S(2)}) async-start(bf16[16,48,1024]{2,1,0:T(8,128)(2,1)} %residuals.1), calls=%async_computation.2 | async-start | bytes 3145728 | tf_op jit(solution)/shard_map/all_to_all | solution.py:297
  132.4 1.9 collective-permute-start.15
  132.5 3.2 %collective-permute-start.16 = (bf16[192,1152]{1,0:T(8,128)(2,1)}, bf16[192,1152]{1,0:T(8,128)(2,1)S(1)}, u32[]{:S(2)}, u32[]{:S(2)}) collective-permute-start(bf16[192,1152]{1,0:T(8,128)(2,1)} %collective-permute-done.9.refs_1_), channel_id=1, source_target_pairs={{0,16},{16,0},{1,17},{17,1},{2,18},{18,2},{3,19},{19,3},{4,20},{20... | collective-permute-start | bytes 1327112 | tf_op jit(solution)/shard_map/ppermute | solution.py:327
  133.0 2.9 %collective-permute-start.17 = (bf16[192,1152]{1,0:T(8,128)(2,1)S(1)}, bf16[192,1152]{1,0:T(8,128)(2,1)S(1)}, u32[]{:S(2)}, u32[]{:S(2)}) collective-permute-start(bf16[192,1152]{1,0:T(8,128)(2,1)S(1)} %collective-permute-done.10.refs_2_), channel_id=1, source_target_pairs={{0,16},{16,0},{1,17},{17,1},{2,18},{18,2},{3,19},{19,3},{4,20},{20... | collective-permute-start | bytes 1327112 | tf_op jit(solution)/shard_map/ppermute | solution.py:327
  133.1 3.9 %collective-permute-start.18 = (bf16[192,1152]{1,0:T(8,128)(2,1)}, bf16[192,1152]{1,0:T(8,128)(2,1)S(1)}, u32[]{:S(2)}, u32[]{:S(2)}) collective-permute-start(bf16[192,1152]{1,0:T(8,128)(2,1)} %copy-done.5), channel_id=1, source_target_pairs={{0,16},{16,0},{1,17},{17,1},{2,18},{18,2},{3,19},{19,3},{4,20},{20... | collective-permute-start | bytes 1327112 | tf_op jit(solution)/shard_map/ppermute | solution.py:327
  133.5 3.5 %collective-permute-start.19 = (bf16[192,1152]{1,0:T(8,128)(2,1)S(1)}, bf16[192,1152]{1,0:T(8,128)(2,1)S(1)}, u32[]{:S(2)}, u32[]{:S(2)}) collective-permute-start(bf16[192,1152]{1,0:T(8,128)(2,1)S(1)} %constant_dynamic-update-slice_fusion.8.refs_4_), channel_id=1, source_target_pairs={{0,16},{16,0},{1,17},{17,1},{2,18},{18,2},{3,19},{19,3},{4,20},{20... | collective-permute-start | bytes 1327112 | tf_op jit(solution)/shard_map/ppermute | solution.py:327
  134.2 3.2 %collective-permute-start.20 = (bf16[192,1152]{1,0:T(8,128)(2,1)S(1)}, bf16[192,1152]{1,0:T(8,128)(2,1)S(1)}, u32[]{:S(2)}, u32[]{:S(2)}) collective-permute-start(bf16[192,1152]{1,0:T(8,128)(2,1)S(1)} %collective-permute-done.12.refs_5_), channel_id=1, source_target_pairs={{0,16},{16,0},{1,17},{17,1},{2,18},{18,2},{3,19},{19,3},{4,20},{20... | collective-permute-start | bytes 1327112 | tf_op jit(solution)/shard_map/ppermute | solution.py:327
  135.7 2.5 %collective-permute-start.21 = (bf16[192,1152]{1,0:T(8,128)(2,1)}, bf16[192,1152]{1,0:T(8,128)(2,1)S(1)}, u32[]{:S(2)}, u32[]{:S(2)}) collective-permute-start(bf16[192,1152]{1,0:T(8,128)(2,1)} %collective-permute-done.13.refs_6_), channel_id=1, source_target_pairs={{0,16},{16,0},{1,17},{17,1},{2,18},{18,2},{3,19},{19,3},{4,20},{20... | collective-permute-start | bytes 1327112 | tf_op jit(solution)/shard_map/ppermute | solution.py:327
  135.9 3.0 %collective-permute-start.22 = (bf16[192,1152]{1,0:T(8,128)(2,1)}, bf16[192,1152]{1,0:T(8,128)(2,1)S(1)}, u32[]{:S(2)}, u32[]{:S(2)}) collective-permute-start(bf16[192,1152]{1,0:T(8,128)(2,1)} %collective-permute-done.14.refs_7_), channel_id=1, source_target_pairs={{0,16},{16,0},{1,17},{17,1},{2,18},{18,2},{3,19},{19,3},{4,20},{20... | collective-permute-start | bytes 1327112 | tf_op jit(solution)/shard_map/ppermute | solution.py:327
  138.9 1.0 copy-start.4
  139.9 1.0 copy-start.6
  143.8 1.4 copy-start
  145.2 1.4 copy-start.1
  146.7 1.4 copy-start.2

commit v3 on v2

v3 whole, which is shorter than its diff:
```python
import functools

import jax
import jax.numpy as jnp
import numpy as np
from jax import lax
from jax.experimental import pallas as pl
from jax.experimental.pallas import tpu as pltpu
from jax.sharding import Mesh
from jax.sharding import PartitionSpec as P

SEQ_AXES = ("zh", "x", "core")
CHAN_AXES = ("y", "zl")
F32 = jnp.float32
BF16 = jnp.bfloat16
NT = (((1,), (1,)), ((), ()))
NN = (((1,), (0,)), ((), ()))


def params(mib):
    return pltpu.CompilerParams(vmem_limit_bytes=mib << 20)


def in_hbm(*values):
    return [pltpu.with_memory_space_constraint(value, pltpu.HBM) for value in values]


def whole(shape):
    return pl.BlockSpec(shape, lambda *_: (0,) * len(shape), pipeline_mode=pl.Buffered(1))


def swap_matrix(n):
    r = np.arange(n * n)
    return jnp.asarray(np.eye(n * n)[(r % n) * n + r // n], BF16)


def dot(a, b, dims=NN):
    return lax.dot_general(a, b, dims, preferred_element_type=F32)


def swapped(blocks, swap_ref):
    moved = dot(swap_ref[...], jnp.concatenate(blocks, axis=0)).astype(BF16)
    return [moved[n * 16 : n * 16 + 16] for n in range(16)]


def section_kernel(x_ref, factor_ref, swap_ref, out_ref, turned):
    @pl.when(pl.program_id(0) == 0)
    def _():
        turned[...] = factor_ref[...].astype(F32).T.astype(BF16)

    for n in range(0, x_ref.shape[0], 16):
        halves = [
            swapped([x_ref[n : n + 16, a * 512 : a * 512 + 512] for a in range(h, h + 16)], swap_ref)
            for h in (0, 16)
        ]
        rows = jnp.concatenate([half[c] for c in range(16) for half in halves], axis=0)
        out_ref[:, n * 32 : n * 32 + 512] = dot(turned[...], rows, NT).astype(BF16)


def first_sections(inputs, forward_one):
    channels, positions = inputs.shape
    return pl.pallas_call(
        section_kernel,
        grid=(channels // 48,),
        in_specs=[
            pl.BlockSpec((48, positions), lambda g: (g, 0)),
            whole((512, 512)),
            whole((256, 256)),
        ],
        out_specs=pl.BlockSpec((512, 48 * 32), lambda g: (0, g)),
        out_shape=jax.ShapeDtypeStruct((512, channels * 32), BF16),
        scratch_shapes=[pltpu.VMEM((512, 512), BF16)],
        compiler_params=params(32),
        name="first_sections",
    )(*in_hbm(inputs, forward_one, swap_matrix(16)))


def gathered(in_ref, tiles):
    chunk = lax.broadcasted_iota(jnp.int32, (128, 128), 1) // 32
    masks = [chunk == i for i in range(4)]
    rows = []
    for t in tiles:
        parts = [
            jnp.concatenate(
                [in_ref[4 * g + i, :, t * 128 : t * 128 + 128] for g in range(4)], axis=0
            )
            for i in range(4)
        ]
        for j in range(4):
            out = parts[j]
            for i in range(4):
                if i != j:
                    out = jnp.where(masks[i], pltpu.roll(parts[i], (i - j) % 4 * 32, axis=1), out)
            rows.append(jnp.concatenate([out[g * 32 : g * 32 + 32] for g in range(4)], axis=1))
    return jnp.concatenate(rows, axis=0)


def spectrum_kernel(in_ref, kernel_ref, forward_ref, turned_ref, out_ref):
    channels = kernel_ref.shape[0]
    for c in range(0, channels, 8):
        rows = gathered(in_ref, (c // 4, c // 4 + 1))
        spectrum = dot(rows, forward_ref[...])
        scaled = (spectrum * kernel_ref[c : c + 8].reshape(256, 512).astype(F32)).astype(BF16)
        out_ref[:, c * 32 : c * 32 + 256] = dot(turned_ref[...], scaled, NT).astype(BF16)


def partial_inverses(sections, kernel, forward_two, turned_two):
    channels, step = kernel.shape[0], 48
    return pl.pallas_call(
        spectrum_kernel,
        grid=(channels // step,),
        in_specs=[
            pl.BlockSpec((16, 32, step * 32), lambda g: (0, 0, g)),
            pl.BlockSpec((step, 32, 512), lambda g: (g, 0, 0)),
            whole((512, 512)),
            whole((512, 512)),
        ],
        out_specs=pl.BlockSpec((512, step * 32), lambda g: (0, g)),
        out_shape=jax.ShapeDtypeStruct((512, channels * 32), BF16),
        compiler_params=params(32),
        name="partial_inverses",
    )(sections, *in_hbm(kernel, forward_two, turned_two))


def resid_kernel(in_ref, x_ref, inverse_ref, swap_ref, out_ref):
    for first in range(0, x_ref.shape[0], 16):
        here = slice(first, first + 16)
        halves = [
            swapped([x_ref[here, i * 512 : i * 512 + 512] for i in range(h, h + 16)], swap_ref)
            for h in (0, 16)
        ]
        resid = []
        for c in range(0, 16, 8):
            tile = (first + c) // 4
            mixed = dot(gathered(in_ref, (tile, tile + 1)), inverse_ref[...])
            x = jnp.concatenate([half[n] for n in range(c, c + 8) for half in halves], axis=0)
            resid.append((x.astype(F32) + mixed).astype(BF16))
        for h in range(2):
            blocks = [
                resid[c // 8][(c % 8) * 32 + h * 16 : (c % 8) * 32 + h * 16 + 16] for c in range(16)
            ]
            for n, block in enumerate(swapped(blocks, swap_ref)):
                i = h * 16 + n
                out_ref[i // 2, here, (i % 2) * 512 : (i % 2) * 512 + 512] = block


def residuals(parts, inputs, inverse_one):
    channels, positions = inputs.shape
    return pl.pallas_call(
        resid_kernel,
        grid=(channels // 48,),
        in_specs=[
            pl.BlockSpec((16, 32, 48 * 32), lambda g: (0, 0, g)),
            pl.BlockSpec((48, positions), lambda g: (g, 0)),
            whole((512, 512)),
            whole((256, 256)),
        ],
        out_specs=pl.BlockSpec((16, 48, 1024), lambda g: (0, g, 0)),
        out_shape=jax.ShapeDtypeStruct((16, channels, positions // 16), BF16),
        compiler_params=params(32),
        name="residuals",
    )(parts, *in_hbm(inputs, inverse_one, swap_matrix(16)))


def layout_kernel(core_ref, *refs):
    pieces, (gate_ref, up_ref, down_ref) = refs[:-3], refs[-3:]
    count = len(pieces) // 2
    rows, columns = pieces[0].shape
    channels, odd = 2 * columns // 3, columns // 3

    def emit(lefts, rights):
        for n, (left, right) in enumerate(zip(lefts, rights)):
            here = slice(n * rows, n * rows + rows)
            gate_ref[here, :] = left[:, :channels]
            up_ref[here, :odd] = left[:, channels:]
            up_ref[here, odd:] = right[:, :odd]
            down_ref[:, here] = right[:, odd:].astype(F32).T.astype(BF16)

    @pl.when(core_ref[0] == 0)
    def _():
        emit(pieces[:count], pieces[count:])

    @pl.when(core_ref[0] == 1)
    def _():
        emit(pieces[count:], pieces[:count])


def lay_out(core, mine, others):
    rows, columns = mine[0].shape
    channels, hidden_units = 2 * columns // 3, rows * len(mine)
    pieces = [*mine, *others]
    return pl.pallas_call(
        layout_kernel,
        in_specs=[pl.BlockSpec(memory_space=pltpu.SMEM)] + [whole((rows, columns))] * len(pieces),
        grid=(1,),
        out_specs=[
            whole((hidden_units, channels)),
            whole((hidden_units, channels)),
            whole((channels, hidden_units)),
        ],
        out_shape=[
            jax.ShapeDtypeStruct((hidden_units, channels), BF16),
            jax.ShapeDtypeStruct((hidden_units, channels), BF16),
            jax.ShapeDtypeStruct((channels, hidden_units), BF16),
        ],
        compiler_params=params(40),
        cost_estimate=pl.CostEstimate(flops=0, bytes_accessed=12 * rows * columns * len(pieces), transcendentals=0),
        name="lay_out_weights",
    )(core.reshape(1), *pieces)


def mlp_kernel(x_ref, gain_ref, gate_hbm, up_hbm, down_hbm, out_ref, gate, up, down, sems, normed):
    hidden_units, channels = gate.shape
    width = normed.shape[1]
    step = hidden_units // 3
    copies = []
    for n in range(3):
        here = pl.ds(n * step, step)
        copies.append(
            [
                pltpu.make_async_copy(gate_hbm.at[here, :], gate.at[here, :], sems.at[n, 0]),
                pltpu.make_async_copy(up_hbm.at[here, :], up.at[here, :], sems.at[n, 1]),
                pltpu.make_async_copy(down_hbm.at[:, here], down.at[:, here], sems.at[n, 2]),
            ]
        )
    for group in copies:
        for copy in group:
            copy.start()
    for t in range(0, width, 1024):
        tokens = slice(t, t + 1024)
        stream = x_ref[:, :, tokens].reshape(channels, 1024).astype(F32)
        mean_square = jnp.mean(stream * stream, axis=0, keepdims=True)
        normed[:, tokens] = (stream * lax.rsqrt(mean_square + 1e-05) * gain_ref[...]).astype(BF16)
    for t in range(0, width, 1024):
        tokens = slice(t, t + 1024)
        total = x_ref[:, :, tokens].reshape(channels, 1024).astype(F32)
        for n in range(3):
            if t == 0:
                for copy in copies[n]:
                    copy.wait()
            here = slice(n * step, n * step + step)
            gate_part = dot(gate[here, :], normed[:, tokens])
            up_part = dot(up[here, :], normed[:, tokens])
            curve = gate_part * (0.7978845608 + (0.7978845608 * 0.044715) * (gate_part * gate_part))
            half = 0.5 * gate_part
            hidden = ((half + half * jnp.tanh(curve)) * up_part).astype(BF16)
            total = total + dot(down[:, here], hidden)
        out_ref[:, :, tokens] = total.astype(BF16).reshape(out_ref.shape[0], out_ref.shape[1], 1024)


def mlp(tokens, norm_gain, weights):
    sources, channels_each, count = tokens.shape
    channels = sources * channels_each
    hidden_units = weights[0].shape[0]
    anywhere = pl.BlockSpec(memory_space=pl.ANY)
    return pl.pallas_call(
        mlp_kernel,
        in_specs=[
            pl.BlockSpec(memory_space=pltpu.VMEM),
            pl.BlockSpec(memory_space=pltpu.VMEM),
            anywhere,
            anywhere,
            anywhere,
        ],
        out_specs=pl.BlockSpec(memory_space=pltpu.VMEM),
        out_shape=jax.ShapeDtypeStruct(tokens.shape, BF16),
        scratch_shapes=[
            pltpu.VMEM((hidden_units, channels), BF16),
            pltpu.VMEM((hidden_units, channels), BF16),
            pltpu.VMEM((channels, hidden_units), BF16),
            pltpu.SemaphoreType.DMA((3, 3)),
            pltpu.VMEM((channels, count), BF16),
        ],
        compiler_params=params(40),
        name="mlp",
    )(tokens, norm_gain.reshape(channels, 1), *in_hbm(*weights))


def pack(w_gate, w_up, w_down, core):
    rows, odd = w_gate.shape[0] // 4, w_up.shape[1] // 2
    start = lax.axis_index("x") * rows
    gate, up, down = (lax.dynamic_slice_in_dim(w, start, rows, 0) for w in (w_gate, w_up, w_down))
    left = jnp.concatenate([gate, up[:, :odd]], axis=1)
    right = jnp.concatenate([up[:, odd:], down], axis=1)
    return jnp.where(core == 0, left, right)


def with_partners(value, axis, size):
    return [value] + [
        lax.ppermute(value, axis, [(i, i ^ d) for i in range(size)]) for d in range(1, size)
    ]


def exchange(value, axes):
    return lax.all_to_all(value, axes, split_axis=0, concat_axis=0, tiled=True)


def shards(
    inputs,
    kernel,
    forward_one,
    forward_two,
    inverse_one,
    inverse_two,
    norm_gain,
    w_gate,
    w_up,
    w_down,
    lines,
):
    channels = inputs.shape[0]
    core = lax.axis_index("core")
    lined = with_partners(pack(w_gate, w_up, w_down, core), "zl", lines)
    sections = first_sections(inputs, forward_one).reshape(16, 32, channels * 32)
    sections, lined = lax.optimization_barrier((sections, lined))
    line = jnp.concatenate(lined, axis=0)
    half = line.shape[0] // 2
    first = [with_partners(line[:half], "x", lines), with_partners(line[half:], "y", lines)]
    sections, first = lax.optimization_barrier((exchange(sections, SEQ_AXES), first))
    pieces = with_partners(jnp.concatenate(first[0], axis=0), "y", lines)
    pieces += with_partners(jnp.concatenate(first[1], axis=0), "x", lines)
    parts = partial_inverses(sections, kernel, forward_two, inverse_two.T)
    parts = exchange(parts.reshape(16, 32, channels * 32), SEQ_AXES)
    parts, pieces = lax.optimization_barrier((parts, pieces))
    others = [lax.ppermute(piece, "core", [(0, 1), (1, 0)]) for piece in pieces]
    tokens = exchange(residuals(parts, inputs, inverse_one), CHAN_AXES)
    weights = lay_out(core, pieces, others)
    result = exchange(mlp(tokens, norm_gain, weights), CHAN_AXES)
    return result.transpose(1, 0, 2).reshape(inputs.shape)


def solution(mesh):
    fine = Mesh(mesh.devices.reshape(2, 4, 2, 4, 4), ("zh", "x", "core", "y", "zl"))
    return jax.shard_map(
        functools.partial(shards, lines=4),
        mesh=fine,
        in_specs=(
            P(CHAN_AXES, SEQ_AXES),
            P(CHAN_AXES, SEQ_AXES, None),
            P(),
            P(),
            P(),
            P(),
            P(),
            P(CHAN_AXES, None),
            P(CHAN_AXES, None),
            P(CHAN_AXES, None),
        ),
        out_specs=P(CHAN_AXES, SEQ_AXES),
        check_vma=False,
    )
```

time: 227 us -> 223 us (0.982)
  starting transfers between devices: 56.6 us -> 62 us
  waiting for transfers between devices: 84.3 us -> 79 us
  Pallas kernels: 32.3 us -> 27.5 us
    all_to_all x3, waiting for transfers between devices: 41 us -> 32.2 us  [exchange(): return lax.all_to_all(value, axes, split_axis=0, concat_axis=0, tiled=True)]
    all_to_all x3, starting transfers between devices: 29.1 us -> 34.6 us  [exchange(): return lax.all_to_all(value, axes, split_axis=0, concat_axis=0, tiled=True)]
    pallas_call x4, Pallas kernels: 29.5 us -> 24.4 us  [the longest x1 9.81 us: mlp(): pl.pallas_call(mlp_kernel, in_specs=[pl.BlockSpec(memory_space=pltpu.VMEM...]
    ppermute x15, waiting for transfers between devices: 38.9 us -> 42.2 us  [with_partners(): lax.ppermute(value, axis, [(i, i ^ d) for i in range(size)])]
    unnamed x36 -> x39, local copies, waits for them, and re-layouts: 7.25 us -> 8.26 us
  transfers between devices with their start and end apart: 26 -> 26, of which waited for: 16 -> 15; matrix products, arithmetic and copies ran while one was open for 0% -> 1% of each run, Pallas kernels for 3% -> 3%
where the time goes in v3:
time: 223 us
  waiting for transfers between devices  79 us (35%)
  starting transfers between devices  62 us (28%)
  blocking collectives  42.6 us (19%)
  Pallas kernels  27.5 us (12%)
  local copies, waits for them, and re-layouts  11.3 us (5%)
    all_to_all x1, blocking collectives, exchange(): return lax.all_to_all(value, axes, split_axis=0, concat_axis=0, tiled=True)  42.6 us
    ppermute x15, waiting for transfers between devices, with_partners(): lax.ppermute(value, axis, [(i, i ^ d) for i in range(size)])  42.2 us
    all_to_all x3, starting transfers between devices, exchange(): return lax.all_to_all(value, axes, split_axis=0, concat_axis=0, tiled=True)  34.6 us
    all_to_all x3, waiting for transfers between devices, exchange(): return lax.all_to_all(value, axes, split_axis=0, concat_axis=0, tiled=True)  32.2 us
    ppermute x15, starting transfers between devices, with_partners(): lax.ppermute(value, axis, [(i, i ^ d) for i in range(size)])  25.6 us
    pallas_call x1, Pallas kernels, mlp(): pl.pallas_call(mlp_kernel, in_specs=[pl.BlockSpec(memory_space=pltpu.VMEM...  9.81 us
    unnamed x39, local copies, waits for them, and re-layouts  8.26 us
    pallas_call x1, Pallas kernels, partial_inverses(): pl.pallas_call(spectrum_kernel, grid=(channels // step,), in_specs=[pl.Bl...  5.13 us
  transfers between devices with their start and end apart: 26, of which 15 were waited for; matrix products, arithmetic and copies ran while one was open for 1% of the time, Pallas kernels for 3%

profile of v3, /device:TPU:6, one launch (start us, length us, event | category | flops | bytes accessed | tf_op | source)
XLA Modules:
  0.0 222.6 jit_solution(6510412756744587247)
XLA Ops:
  0.0 0.8 constant_dynamic-slice_fusion.1
  0.8 0.7 fusion
  1.6 2.0 collective-permute-start
  3.6 3.3 %collective-permute-start.1 = (bf16[24,1152]{1,0:T(8,128)(2,1)S(1)}, bf16[24,1152]{1,0:T(8,128)(2,1)S(1)}, u32[]{:S(2)}, u32[]{:S(2)}) collective-permute-start(bf16[24,1152]{1,0:T(8,128)(2,1)S(1)} %maximum_select_fusion), channel_id=1, source_target_pairs={{0,2},{1,3},{2,0},{3,1},{4,6},{5,7},{6,4},{7,5},{8,10},{9,11},{10,... | collective-permute-start | bytes 165896 | tf_op jit(solution)/shard_map/ppermute | solution.py:290
  6.8 0.0 collective-permute-start.2
  6.8 4.5 %first_sections.1 = bf16[512,1536]{1,0:T(8,128)(2,1)} custom-call(bf16[48,16384]{1,0:T(8,128)(2,1)} %x_ref.3, bf16[512,512]{1,0:T(8,128)(2,1)} %factor_ref.1, bf16[256,256]{1,0:T(8,128)(2,1)} %constant.20.clone.swap_ref), custom_call_target="tpu_custom_call" | custom-call | tf_op jit(solution)/shard_map/first_sections/pallas_call | solution.py:62
  11.4 0.0 collective-permute-done
  11.4 1.4 collective-permute-done.2
  12.8 9.4 %all-to-all-start = ((bf16[16,32,1536]{2,1,0:T(8,128)(2,1)}), bf16[16,32,1536]{2,1,0:T(8,128)(2,1)S(1)}, u32[]{:S(2)}, u32[]{:S(2)}) async-start(bf16[16,32,1536]{2,1,0:T(8,128)(2,1)} %bitcast), calls=%async_computation | async-start | bytes 3145728 | tf_op jit(solution)/shard_map/all_to_all | solution.py:295
  22.2 1.7 collective-permute-start.6
  23.8 2.9 %collective-permute-start.7 = (bf16[48,1152]{1,0:T(8,128)(2,1)S(1)}, bf16[48,1152]{1,0:T(8,128)(2,1)S(1)}, u32[]{:S(2)}, u32[]{:S(2)}) collective-permute-start(bf16[48,1152]{1,0:T(8,128)(2,1)S(1)} %constant_dynamic-update-slice_fusion.2), channel_id=1, source_target_pairs={{0,8},{4,12},{8,0},{12,4},{1,9},{5,13},{9,1},{13,5},{2,10},{6,14},... | collective-permute-start | bytes 331784 | tf_op jit(solution)/shard_map/ppermute | solution.py:290
  26.7 0.2 collective-permute-start.8
  27.0 0.9 collective-permute-start.3
  27.9 0.7 collective-permute-start.4
  28.6 3.1 %collective-permute-start.5 = (bf16[48,1152]{1,0:T(8,128)(2,1)S(1)}, bf16[48,1152]{1,0:T(8,128)(2,1)S(1)}, u32[]{:S(2)}, u32[]{:S(2)}) collective-permute-start(bf16[48,1152]{1,0:T(8,128)(2,1)S(1)} %constant_dynamic-update-slice_fusion), channel_id=1, source_target_pairs={{0,96},{32,64},{64,32},{96,0},{1,97},{33,65},{65,33},{97,1},{2,98}... | collective-permute-start | bytes 331784 | tf_op jit(solution)/shard_map/ppermute | solution.py:290
  31.8 1.0 copy.14
  32.8 1.5 collective-permute-done.8
  34.3 4.1 %collective-permute-done.3 = bf16[48,1152]{1,0:T(8,128)(2,1)S(1)} collective-permute-done((bf16[48,1152]{1,0:T(8,128)(2,1)S(1)}, bf16[48,1152]{1,0:T(8,128)(2,1)S(1)}, u32[]{:S(2)}, u32[]{:S(2)}) %collective-permute-start.3) | collective-permute-done | bytes 110624 | tf_op jit(solution)/shard_map/ppermute | solution.py:290
  38.5 6.5 %collective-permute-done.4 = bf16[48,1152]{1,0:T(8,128)(2,1)S(1)} collective-permute-done((bf16[48,1152]{1,0:T(8,128)(2,1)S(1)}, bf16[48,1152]{1,0:T(8,128)(2,1)S(1)}, u32[]{:S(2)}, u32[]{:S(2)}) %collective-permute-start.4) | collective-permute-done | bytes 110624 | tf_op jit(solution)/shard_map/ppermute | solution.py:290
  45.0 0.0 collective-permute-done.5
  45.0 8.7 %all-to-all-done.in_ref = bf16[16,32,1536]{2,1,0:T(8,128)(2,1)S(1)} async-done(((bf16[16,32,1536]{2,1,0:T(8,128)(2,1)}), bf16[16,32,1536]{2,1,0:T(8,128)(2,1)S(1)}, u32[]{:S(2)}, u32[]{:S(2)}) %all-to-all-start) | async-done | bytes 1572896 | tf_op jit(solution)/shard_map/all_to_all | solution.py:295
  53.7 5.1 %partial_inverses.1 = bf16[512,1536]{1,0:T(8,128)(2,1)} custom-call(bf16[16,32,1536]{2,1,0:T(8,128)(2,1)S(1)} %all-to-all-done.in_ref, bf16[48,32,512]{2,1,0:T(8,128)(2,1)} %kernel_ref.1, bf16[512,512]{1,0:T(8,128)(2,1)} %forward_ref.1, bf16[512,512]{1,0:T(8,128)(2,1)} %bitcast.8), custom_call_target="tpu_custom_call" | custom-call | tf_op jit(solution)/shard_map/partial_inverses/pallas_call | solution.py:109
  58.9 11.4 %all-to-all-start.1 = ((bf16[16,32,1536]{2,1,0:T(8,128)(2,1)}), bf16[16,32,1536]{2,1,0:T(8,128)(2,1)S(1)}, u32[]{:S(2)}, u32[]{:S(2)}) async-start(bf16[16,32,1536]{2,1,0:T(8,128)(2,1)} %bitcast.2), calls=%async_computation.1 | async-start | bytes 3145728 | tf_op jit(solution)/shard_map/all_to_all | solution.py:295
  70.4 0.9 collective-permute-start.12
  71.4 0.7 collective-permute-start.13
  72.1 3.1 %collective-permute-start.14 = (bf16[192,1152]{1,0:T(8,128)(2,1)S(1)}, bf16[192,1152]{1,0:T(8,128)(2,1)}, u32[]{:S(2)}, u32[]{:S(2)}) collective-permute-start(bf16[192,1152]{1,0:T(8,128)(2,1)S(1)} %constant_dynamic-update-slice_fusion.8.refs_4_), channel_id=1, source_target_pairs={{0,96},{32,64},{64,32},{96,0},{1,97},{33,65},{65,33},{97,1},{2,98}... | collective-permute-start | bytes 1327112 | tf_op jit(solution)/shard_map/ppermute | solution.py:290
  75.3 3.3 %collective-permute-start.10 = (bf16[192,1152]{1,0:T(8,128)(2,1)S(1)}, bf16[192,1152]{1,0:T(8,128)(2,1)S(1)}, u32[]{:S(2)}, u32[]{:S(2)}) collective-permute-start(bf16[192,1152]{1,0:T(8,128)(2,1)S(1)} %constant_dynamic-update-slice_fusion.4.refs_0_), channel_id=1, source_target_pairs={{0,8},{4,12},{8,0},{12,4},{1,9},{5,13},{9,1},{13,5},{2,10},{6,14},... | collective-permute-start | bytes 1327112 | tf_op jit(solution)/shard_map/ppermute | solution.py:290
  78.6 1.0 collective-permute-start.11
  79.6 19.6 %collective-permute-done.12.refs_5_ = bf16[192,1152]{1,0:T(8,128)(2,1)S(1)} collective-permute-done((bf16[192,1152]{1,0:T(8,128)(2,1)S(1)}, bf16[192,1152]{1,0:T(8,128)(2,1)S(1)}, u32[]{:S(2)}, u32[]{:S(2)}) %collective-permute-start.12) | collective-permute-done | bytes 442400 | tf_op jit(solution)/shard_map/ppermute | solution.py:290
  99.3 1.6 collective-permute-start.9
  100.9 8.2 %collective-permute-done.13.refs_6_ = bf16[192,1152]{1,0:T(8,128)(2,1)} collective-permute-done((bf16[192,1152]{1,0:T(8,128)(2,1)S(1)}, bf16[192,1152]{1,0:T(8,128)(2,1)}, u32[]{:S(2)}, u32[]{:S(2)}) %collective-permute-start.13) | collective-permute-done | bytes 442400 | tf_op jit(solution)/shard_map/ppermute | solution.py:290
  109.0 0.0 collective-permute-done.14.refs_7_
  109.0 0.0 collective-permute-done.10.refs_2_
  109.0 0.0 collective-permute-done.11.refs_3_
  109.1 0.8 copy-done.5
  109.8 0.8 collective-permute-done.9.refs_1_
  110.6 0.0 all-to-all-done.1.in_ref
  110.6 5.0 %residuals.1 = bf16[16,48,1024]{2,1,0:T(8,128)(2,1)} custom-call(bf16[16,32,1536]{2,1,0:T(8,128)(2,1)S(1)} %all-to-all-done.1.in_ref, bf16[48,16384]{1,0:T(8,128)(2,1)} %x_ref.3, bf16[512,512]{1,0:T(8,128)(2,1)} %inverse_ref.1, bf16[256,256]{1,0:T(8,128)(2,1)} %constant.20.clone.swap_ref), custom_call_target="tpu_custom_call" | custom-call | tf_op jit(solution)/shard_map/residuals/pallas_call | solution.py:149
  115.6 13.8 %all-to-all-start.2 = ((bf16[16,48,1024]{2,1,0:T(8,128)(2,1)}), bf16[16,48,1024]{2,1,0:T(8,128)(2,1)S(1)}, u32[]{:S(2)}, u32[]{:S(2)}) async-start(bf16[16,48,1024]{2,1,0:T(8,128)(2,1)} %residuals.1), calls=%async_computation.2 | async-start | bytes 3145728 | tf_op jit(solution)/shard_map/all_to_all | solution.py:295
  129.4 0.1 collective-permute-start.15
  129.5 0.5 collective-permute-start.16
  130.0 0.1 collective-permute-start.17
  130.1 0.4 collective-permute-start.18
  130.5 0.1 collective-permute-start.19
  130.6 0.7 collective-permute-done.15.refs_8_
  131.3 0.1 collective-permute-start.20
  131.4 1.3 collective-permute-done.16.refs_9_
  132.8 0.1 collective-permute-start.21
  132.9 0.4 collective-permute-start.22
  133.3 0.2 reshape.20.gain_ref
  133.5 0.6 collective-permute-done.18.refs_11_
  134.1 0.4 collective-permute-done.20.refs_13_
  134.5 0.8 collective-permute-done.21.refs_14_
  135.3 0.6 collective-permute-done.22.refs_15_
  136.0 1.0 copy-done.4
  137.0 1.0 copy-done.6
  138.0 3.1 %lay_out_weights.1 = (bf16[1536,768]{1,0:T(8,128)(2,1)S(1)}, bf16[1536,768]{1,0:T(8,128)(2,1)S(1)}, bf16[768,1536]{1,0:T(8,128)(2,1)S(1)}) custom-call(s32[1]{0:T(128)} %bitcast.3.core_ref, bf16[192,1152]{1,0:T(8,128)(2,1)S(1)} %constant_dynamic-update-slice_fusion.4.refs_0_, bf16[192,1152]{1,0:T(8,128)(2,1)} %collective-permute-done.9.refs_1_, ...), custom_call_target="tpu_custom_call" | custom-call | bytes 42467328 | tf_op jit(solution)/shard_map/lay_out_weights/pallas_call | solution.py:192
  141.1 1.4 copy-done
  142.5 1.4 copy-done.1
  144.0 1.4 copy-done.2
  145.4 23.5 %all-to-all-done.2.x_ref = bf16[16,48,1024]{2,1,0:T(8,128)(2,1)S(1)} async-done(((bf16[16,48,1024]{2,1,0:T(8,128)(2,1)}), bf16[16,48,1024]{2,1,0:T(8,128)(2,1)S(1)}, u32[]{:S(2)}, u32[]{:S(2)}) %all-to-all-start.2) | async-done | bytes 1572896 | tf_op jit(solution)/shard_map/all_to_all | solution.py:295
  168.9 9.8 %mlp.1 = bf16[16,48,1024]{2,1,0:T(8,128)(2,1)S(1)} custom-call(bf16[16,48,1024]{2,1,0:T(8,128)(2,1)S(1)} %all-to-all-done.2.x_ref, f32[768,1]{1,0:T(8,128)S(1)} %reshape.20.gain_ref, bf16[1536,768]{1,0:T(8,128)(2,1)} %copy-done, bf16[1536,768]{1,0:T(8,128)(2,1)} %copy-done.1, bf16[768,1536]{1,0:T(8,128)(2,1)} %copy-done.2), custom_call_target="tpu_custom_call" | custom-call | tf_op jit(solution)/shard_map/mlp/pallas_call | solution.py:256
  178.7 42.6 %all_to_all.20 = bf16[16,48,1024]{2,1,0:T(8,128)(2,1)S(1)} all-to-all(bf16[16,48,1024]{2,1,0:T(8,128)(2,1)S(1)} %mlp.1), channel_id=1, replica_groups=mesh['zh'=2,'x'=4,'core'=2,'y'=4,'zl'=4] {'y','zl'}, dimensions={0} | all-to-all | bytes 3145728 | tf_op jit(solution)/shard_map/all_to_all | solution.py:295
  221.3 1.3 copy.17
  (42 shorter events, 0.2 us)
Async XLA Ops:
  1.6 9.8 %collective-permute-start = (bf16[24,1152]{1,0:T(8,128)(2,1)S(1)}, bf16[24,1152]{1,0:T(8,128)(2,1)S(1)}, u32[]{:S(2)}, u32[]{:S(2)}) collective-permute-start(bf16[24,1152]{1,0:T(8,128)(2,1)S(1)} %maximum_select_fusion), channel_id=1, source_target_pairs={{0,1},{1,0},{2,3},{3,2},{4,5},{5,4},{6,7},{7,6},{8,9},{9,8},{10,11... | collective-permute-start | bytes 165896 | tf_op jit(solution)/shard_map/ppermute | solution.py:290
  3.6 7.8 %collective-permute-start.1 = (bf16[24,1152]{1,0:T(8,128)(2,1)S(1)}, bf16[24,1152]{1,0:T(8,128)(2,1)S(1)}, u32[]{:S(2)}, u32[]{:S(2)}) collective-permute-start(bf16[24,1152]{1,0:T(8,128)(2,1)S(1)} %maximum_select_fusion), channel_id=1, source_target_pairs={{0,2},{1,3},{2,0},{3,1},{4,6},{5,7},{6,4},{7,5},{8,10},{9,11},{10,... | collective-permute-start | bytes 165896 | tf_op jit(solution)/shard_map/ppermute | solution.py:290
  6.8 6.0 %collective-permute-start.2 = (bf16[24,1152]{1,0:T(8,128)(2,1)S(1)}, bf16[24,1152]{1,0:T(8,128)(2,1)S(1)}, u32[]{:S(2)}, u32[]{:S(2)}) collective-permute-start(bf16[24,1152]{1,0:T(8,128)(2,1)S(1)} %maximum_select_fusion), channel_id=1, source_target_pairs={{0,3},{1,2},{2,1},{3,0},{4,7},{5,6},{6,5},{7,4},{8,11},{9,10},{10,... | collective-permute-start | bytes 165896 | tf_op jit(solution)/shard_map/ppermute | solution.py:290
  12.8 19.0 %copy-start.7 = (bf16[512,512]{1,0:T(8,128)(2,1)S(1)}, bf16[512,512]{1,0:T(8,128)(2,1)}, u32[]{:S(2)}) copy-start(bf16[512,512]{1,0:T(8,128)(2,1)} %param.17) | copy-start | bytes 1572868
  12.8 40.9 %all-to-all-start = ((bf16[16,32,1536]{2,1,0:T(8,128)(2,1)}), bf16[16,32,1536]{2,1,0:T(8,128)(2,1)S(1)}, u32[]{:S(2)}, u32[]{:S(2)}) async-start(bf16[16,32,1536]{2,1,0:T(8,128)(2,1)} %bitcast), calls=%async_computation | async-start | bytes 3145728 | tf_op jit(solution)/shard_map/all_to_all | solution.py:295
  22.2 6.5 %collective-permute-start.6 = (bf16[48,1152]{1,0:T(8,128)(2,1)S(1)}, bf16[48,1152]{1,0:T(8,128)(2,1)S(1)}, u32[]{:S(2)}, u32[]{:S(2)}) collective-permute-start(bf16[48,1152]{1,0:T(8,128)(2,1)S(1)} %constant_dynamic-update-slice_fusion.2), channel_id=1, source_target_pairs={{0,4},{4,0},{8,12},{12,8},{1,5},{5,1},{9,13},{13,9},{2,6},{6,2},{1... | collective-permute-start | bytes 331784 | tf_op jit(solution)/shard_map/ppermute | solution.py:290
  23.8 9.0 %collective-permute-start.7 = (bf16[48,1152]{1,0:T(8,128)(2,1)S(1)}, bf16[48,1152]{1,0:T(8,128)(2,1)S(1)}, u32[]{:S(2)}, u32[]{:S(2)}) collective-permute-start(bf16[48,1152]{1,0:T(8,128)(2,1)S(1)} %constant_dynamic-update-slice_fusion.2), channel_id=1, source_target_pairs={{0,8},{4,12},{8,0},{12,4},{1,9},{5,13},{9,1},{13,5},{2,10},{6,14},... | collective-permute-start | bytes 331784 | tf_op jit(solution)/shard_map/ppermute | solution.py:290
  26.7 7.6 %collective-permute-start.8 = (bf16[48,1152]{1,0:T(8,128)(2,1)S(1)}, bf16[48,1152]{1,0:T(8,128)(2,1)S(1)}, u32[]{:S(2)}, u32[]{:S(2)}) collective-permute-start(bf16[48,1152]{1,0:T(8,128)(2,1)S(1)} %constant_dynamic-update-slice_fusion.2), channel_id=1, source_target_pairs={{0,12},{4,8},{8,4},{12,0},{1,13},{5,9},{9,5},{13,1},{2,14},{6,10},... | collective-permute-start | bytes 331784 | tf_op jit(solution)/shard_map/ppermute | solution.py:290
  27.0 11.5 %collective-permute-start.3 = (bf16[48,1152]{1,0:T(8,128)(2,1)S(1)}, bf16[48,1152]{1,0:T(8,128)(2,1)S(1)}, u32[]{:S(2)}, u32[]{:S(2)}) collective-permute-start(bf16[48,1152]{1,0:T(8,128)(2,1)S(1)} %constant_dynamic-update-slice_fusion), channel_id=1, source_target_pairs={{0,32},{32,0},{64,96},{96,64},{1,33},{33,1},{65,97},{97,65},{2,34}... | collective-permute-start | bytes 331784 | tf_op jit(solution)/shard_map/ppermute | solution.py:290
  27.9 17.1 %collective-permute-start.4 = (bf16[48,1152]{1,0:T(8,128)(2,1)S(1)}, bf16[48,1152]{1,0:T(8,128)(2,1)S(1)}, u32[]{:S(2)}, u32[]{:S(2)}) collective-permute-start(bf16[48,1152]{1,0:T(8,128)(2,1)S(1)} %constant_dynamic-update-slice_fusion), channel_id=1, source_target_pairs={{0,64},{32,96},{64,0},{96,32},{1,65},{33,97},{65,1},{97,33},{2,66}... | collective-permute-start | bytes 331784 | tf_op jit(solution)/shard_map/ppermute | solution.py:290
  28.6 30.2 %copy-start.8 = (bf16[48,1152]{1,0:T(8,128)(2,1)}, bf16[48,1152]{1,0:T(8,128)(2,1)S(1)}, u32[]{:S(2)}) copy-start(bf16[48,1152]{1,0:T(8,128)(2,1)S(1)} %collective-permute-done.6) | copy-start | bytes 331780
  28.6 16.4 %collective-permute-start.5 = (bf16[48,1152]{1,0:T(8,128)(2,1)S(1)}, bf16[48,1152]{1,0:T(8,128)(2,1)S(1)}, u32[]{:S(2)}, u32[]{:S(2)}) collective-permute-start(bf16[48,1152]{1,0:T(8,128)(2,1)S(1)} %constant_dynamic-update-slice_fusion), channel_id=1, source_target_pairs={{0,96},{32,64},{64,32},{96,0},{1,97},{33,65},{65,33},{97,1},{2,98}... | collective-permute-start | bytes 331784 | tf_op jit(solution)/shard_map/ppermute | solution.py:290
  32.8 26.1 %copy-start.10 = (bf16[48,1152]{1,0:T(8,128)(2,1)}, bf16[48,1152]{1,0:T(8,128)(2,1)S(1)}, u32[]{:S(2)}) copy-start(bf16[48,1152]{1,0:T(8,128)(2,1)S(1)} %collective-permute-done.7) | copy-start | bytes 331780
  34.3 24.5 %copy-start.12 = (bf16[48,1152]{1,0:T(8,128)(2,1)}, bf16[48,1152]{1,0:T(8,128)(2,1)S(1)}, u32[]{:S(2)}) copy-start(bf16[48,1152]{1,0:T(8,128)(2,1)S(1)} %collective-permute-done.8) | copy-start | bytes 331780
  58.9 11.5 %copy-start.9 = (bf16[48,1152]{1,0:T(8,128)(2,1)S(1)}, bf16[48,1152]{1,0:T(8,128)(2,1)}, u32[]{:S(2)}) copy-start(bf16[48,1152]{1,0:T(8,128)(2,1)} %copy-done.8) | copy-start | bytes 331780
  58.9 11.5 %copy-start.11 = (bf16[48,1152]{1,0:T(8,128)(2,1)S(1)}, bf16[48,1152]{1,0:T(8,128)(2,1)}, u32[]{:S(2)}) copy-start(bf16[48,1152]{1,0:T(8,128)(2,1)} %copy-done.10) | copy-start | bytes 331780
  58.9 11.5 %copy-start.13 = (bf16[48,1152]{1,0:T(8,128)(2,1)S(1)}, bf16[48,1152]{1,0:T(8,128)(2,1)}, u32[]{:S(2)}) copy-start(bf16[48,1152]{1,0:T(8,128)(2,1)} %copy-done.12) | copy-start | bytes 331780
  58.9 51.7 %all-to-all-start.1 = ((bf16[16,32,1536]{2,1,0:T(8,128)(2,1)}), bf16[16,32,1536]{2,1,0:T(8,128)(2,1)S(1)}, u32[]{:S(2)}, u32[]{:S(2)}) async-start(bf16[16,32,1536]{2,1,0:T(8,128)(2,1)} %bitcast.2), calls=%async_computation.1 | async-start | bytes 3145728 | tf_op jit(solution)/shard_map/all_to_all | solution.py:295
  70.4 28.8 %collective-permute-start.12 = (bf16[192,1152]{1,0:T(8,128)(2,1)S(1)}, bf16[192,1152]{1,0:T(8,128)(2,1)S(1)}, u32[]{:S(2)}, u32[]{:S(2)}) collective-permute-start(bf16[192,1152]{1,0:T(8,128)(2,1)S(1)} %constant_dynamic-update-slice_fusion.8.refs_4_), channel_id=1, source_target_pairs={{0,32},{32,0},{64,96},{96,64},{1,33},{33,1},{65,97},{97,65},{2,34}... | collective-permute-start | bytes 1327112 | tf_op jit(solution)/shard_map/ppermute | solution.py:290
  71.4 37.7 %collective-permute-start.13 = (bf16[192,1152]{1,0:T(8,128)(2,1)S(1)}, bf16[192,1152]{1,0:T(8,128)(2,1)}, u32[]{:S(2)}, u32[]{:S(2)}) collective-permute-start(bf16[192,1152]{1,0:T(8,128)(2,1)S(1)} %constant_dynamic-update-slice_fusion.8.refs_4_), channel_id=1, source_target_pairs={{0,64},{32,96},{64,0},{96,32},{1,65},{33,97},{65,1},{97,33},{2,66}... | collective-permute-start | bytes 1327112 | tf_op jit(solution)/shard_map/ppermute | solution.py:290
  72.1 37.0 %collective-permute-start.14 = (bf16[192,1152]{1,0:T(8,128)(2,1)S(1)}, bf16[192,1152]{1,0:T(8,128)(2,1)}, u32[]{:S(2)}, u32[]{:S(2)}) collective-permute-start(bf16[192,1152]{1,0:T(8,128)(2,1)S(1)} %constant_dynamic-update-slice_fusion.8.refs_4_), channel_id=1, source_target_pairs={{0,96},{32,64},{64,32},{96,0},{1,97},{33,65},{65,33},{97,1},{2,98}... | collective-permute-start | bytes 1327112 | tf_op jit(solution)/shard_map/ppermute | solution.py:290
  75.3 33.7 %collective-permute-start.10 = (bf16[192,1152]{1,0:T(8,128)(2,1)S(1)}, bf16[192,1152]{1,0:T(8,128)(2,1)S(1)}, u32[]{:S(2)}, u32[]{:S(2)}) collective-permute-start(bf16[192,1152]{1,0:T(8,128)(2,1)S(1)} %constant_dynamic-update-slice_fusion.4.refs_0_), channel_id=1, source_target_pairs={{0,8},{4,12},{8,0},{12,4},{1,9},{5,13},{9,1},{13,5},{2,10},{6,14},... | collective-permute-start | bytes 1327112 | tf_op jit(solution)/shard_map/ppermute | solution.py:290
  78.6 30.4 %collective-permute-start.11 = (bf16[192,1152]{1,0:T(8,128)(2,1)S(1)}, bf16[192,1152]{1,0:T(8,128)(2,1)S(1)}, u32[]{:S(2)}, u32[]{:S(2)}) collective-permute-start(bf16[192,1152]{1,0:T(8,128)(2,1)S(1)} %constant_dynamic-update-slice_fusion.4.refs_0_), channel_id=1, source_target_pairs={{0,12},{4,8},{8,4},{12,0},{1,13},{5,9},{9,5},{13,1},{2,14},{6,10},... | collective-permute-start | bytes 1327112 | tf_op jit(solution)/shard_map/ppermute | solution.py:290
  99.3 11.3 %collective-permute-start.9 = (bf16[192,1152]{1,0:T(8,128)(2,1)S(1)}, bf16[192,1152]{1,0:T(8,128)(2,1)}, u32[]{:S(2)}, u32[]{:S(2)}) collective-permute-start(bf16[192,1152]{1,0:T(8,128)(2,1)S(1)} %constant_dynamic-update-slice_fusion.4.refs_0_), channel_id=1, source_target_pairs={{0,4},{4,0},{8,12},{12,8},{1,5},{5,1},{9,13},{13,9},{2,6},{6,2},{1... | collective-permute-start | bytes 1327112 | tf_op jit(solution)/shard_map/ppermute | solution.py:290
  109.0 21.0 %copy-start.3 = (bf16[192,1152]{1,0:T(8,128)(2,1)}, bf16[192,1152]{1,0:T(8,128)(2,1)S(1)}, u32[]{:S(2)}) copy-start(bf16[192,1152]{1,0:T(8,128)(2,1)S(1)} %collective-permute-done.10.refs_2_) | copy-start | bytes 1327108
  109.1 0.8 copy-start.5
  115.6 17.7 %copy-start.14 = (f32[768]{0:T(1024)S(1)}, f32[768]{0:T(1024)}, u32[]{:S(2)}) copy-start(f32[768]{0:T(1024)} %param.18) | copy-start | bytes 9220
  115.6 53.3 %all-to-all-start.2 = ((bf16[16,48,1024]{2,1,0:T(8,128)(2,1)}), bf16[16,48,1024]{2,1,0:T(8,128)(2,1)S(1)}, u32[]{:S(2)}, u32[]{:S(2)}) async-start(bf16[16,48,1024]{2,1,0:T(8,128)(2,1)} %residuals.1), calls=%async_computation.2 | async-start | bytes 3145728 | tf_op jit(solution)/shard_map/all_to_all | solution.py:295
  129.4 1.9 collective-permute-start.15
  129.5 3.3 %collective-permute-start.16 = (bf16[192,1152]{1,0:T(8,128)(2,1)}, bf16[192,1152]{1,0:T(8,128)(2,1)S(1)}, u32[]{:S(2)}, u32[]{:S(2)}) collective-permute-start(bf16[192,1152]{1,0:T(8,128)(2,1)} %collective-permute-done.9.refs_1_), channel_id=1, source_target_pairs={{0,16},{16,0},{1,17},{17,1},{2,18},{18,2},{3,19},{19,3},{4,20},{20... | collective-permute-start | bytes 1327112 | tf_op jit(solution)/shard_map/ppermute | solution.py:325
  130.0 2.9 %collective-permute-start.17 = (bf16[192,1152]{1,0:T(8,128)(2,1)S(1)}, bf16[192,1152]{1,0:T(8,128)(2,1)S(1)}, u32[]{:S(2)}, u32[]{:S(2)}) collective-permute-start(bf16[192,1152]{1,0:T(8,128)(2,1)S(1)} %collective-permute-done.10.refs_2_), channel_id=1, source_target_pairs={{0,16},{16,0},{1,17},{17,1},{2,18},{18,2},{3,19},{19,3},{4,20},{20... | collective-permute-start | bytes 1327112 | tf_op jit(solution)/shard_map/ppermute | solution.py:325
  130.1 3.9 %collective-permute-start.18 = (bf16[192,1152]{1,0:T(8,128)(2,1)}, bf16[192,1152]{1,0:T(8,128)(2,1)S(1)}, u32[]{:S(2)}, u32[]{:S(2)}) collective-permute-start(bf16[192,1152]{1,0:T(8,128)(2,1)} %copy-done.5), channel_id=1, source_target_pairs={{0,16},{16,0},{1,17},{17,1},{2,18},{18,2},{3,19},{19,3},{4,20},{20... | collective-permute-start | bytes 1327112 | tf_op jit(solution)/shard_map/ppermute | solution.py:325
  130.5 3.5 %collective-permute-start.19 = (bf16[192,1152]{1,0:T(8,128)(2,1)S(1)}, bf16[192,1152]{1,0:T(8,128)(2,1)S(1)}, u32[]{:S(2)}, u32[]{:S(2)}) collective-permute-start(bf16[192,1152]{1,0:T(8,128)(2,1)S(1)} %constant_dynamic-update-slice_fusion.8.refs_4_), channel_id=1, source_target_pairs={{0,16},{16,0},{1,17},{17,1},{2,18},{18,2},{3,19},{19,3},{4,20},{20... | collective-permute-start | bytes 1327112 | tf_op jit(solution)/shard_map/ppermute | solution.py:325
  131.3 3.2 %collective-permute-start.20 = (bf16[192,1152]{1,0:T(8,128)(2,1)S(1)}, bf16[192,1152]{1,0:T(8,128)(2,1)S(1)}, u32[]{:S(2)}, u32[]{:S(2)}) collective-permute-start(bf16[192,1152]{1,0:T(8,128)(2,1)S(1)} %collective-permute-done.12.refs_5_), channel_id=1, source_target_pairs={{0,16},{16,0},{1,17},{17,1},{2,18},{18,2},{3,19},{19,3},{4,20},{20... | collective-permute-start | bytes 1327112 | tf_op jit(solution)/shard_map/ppermute | solution.py:325
  132.8 2.5 %collective-permute-start.21 = (bf16[192,1152]{1,0:T(8,128)(2,1)}, bf16[192,1152]{1,0:T(8,128)(2,1)S(1)}, u32[]{:S(2)}, u32[]{:S(2)}) collective-permute-start(bf16[192,1152]{1,0:T(8,128)(2,1)} %collective-permute-done.13.refs_6_), channel_id=1, source_target_pairs={{0,16},{16,0},{1,17},{17,1},{2,18},{18,2},{3,19},{19,3},{4,20},{20... | collective-permute-start | bytes 1327112 | tf_op jit(solution)/shard_map/ppermute | solution.py:325
  132.9 3.0 %collective-permute-start.22 = (bf16[192,1152]{1,0:T(8,128)(2,1)}, bf16[192,1152]{1,0:T(8,128)(2,1)S(1)}, u32[]{:S(2)}, u32[]{:S(2)}) collective-permute-start(bf16[192,1152]{1,0:T(8,128)(2,1)} %collective-permute-done.14.refs_7_), channel_id=1, source_target_pairs={{0,16},{16,0},{1,17},{17,1},{2,18},{18,2},{3,19},{19,3},{4,20},{20... | collective-permute-start | bytes 1327112 | tf_op jit(solution)/shard_map/ppermute | solution.py:325
  136.0 1.0 copy-start.4
  137.0 1.0 copy-start.6
  141.1 1.4 copy-start
  142.5 1.4 copy-start.1
  144.0 1.4 copy-start.2

commit v4 on v3

--- a/solution.py
+++ b/solution.py
@@ -321,7 +321,7 @@
     pieces += with_partners(jnp.concatenate(first[1], axis=0), "x", lines)
     parts = partial_inverses(sections, kernel, forward_two, inverse_two.T)
     parts = exchange(parts.reshape(16, 32, channels * 32), SEQ_AXES)
-    parts, pieces = lax.optimization_barrier((parts, pieces))
+    parts, pieces[:6] = lax.optimization_barrier((parts, pieces[:6]))
     others = [lax.ppermute(piece, "core", [(0, 1), (1, 0)]) for piece in pieces]
     tokens = exchange(residuals(parts, inputs, inverse_one), CHAN_AXES)
     weights = lay_out(core, pieces, others)

time: 223 us -> 221 us (level)
  starting transfers between devices: 62 us -> 65.6 us
  waiting for transfers between devices: 79 us -> 75.8 us
  local copies, waits for them, and re-layouts: 11.3 us -> 8.42 us
    all_to_all x3, waiting for transfers between devices: 32.2 us -> 12.1 us  [exchange(): return lax.all_to_all(value, axes, split_axis=0, concat_axis=0, tiled=True)]
    ppermute x15, waiting for transfers between devices: 42.2 us -> 59.4 us  [with_partners(): lax.ppermute(value, axis, [(i, i ^ d) for i in range(size)])]
    all_to_all x3, starting transfers between devices: 34.6 us -> 43.9 us  [exchange(): return lax.all_to_all(value, axes, split_axis=0, concat_axis=0, tiled=True)]
    ppermute x15, starting transfers between devices: 25.6 us -> 20.4 us  [with_partners(): lax.ppermute(value, axis, [(i, i ^ d) for i in range(size)])]
    unnamed x39 -> x31, local copies, waits for them, and re-layouts: 8.26 us -> 5.39 us
  transfers between devices with their start and end apart: 26 -> 26, of which waited for: 15 -> 13; matrix products, arithmetic and copies ran while one was open for 1% -> 1% of each run, Pallas kernels for 3% -> 3%
where the time goes in v4:
time: 221 us
  waiting for transfers between devices  75.8 us (34%)
  starting transfers between devices  65.6 us (30%)
  blocking collectives  42.9 us (19%)
  Pallas kernels  27.7 us (13%)
  local copies, waits for them, and re-layouts  8.42 us (4%)
    ppermute x15, waiting for transfers between devices, with_partners(): lax.ppermute(value, axis, [(i, i ^ d) for i in range(size)])  59.4 us
    all_to_all x3, starting transfers between devices, exchange(): return lax.all_to_all(value, axes, split_axis=0, concat_axis=0, tiled=True)  43.9 us
    all_to_all x1, blocking collectives, exchange(): return lax.all_to_all(value, axes, split_axis=0, concat_axis=0, tiled=True)  42.9 us
    ppermute x15, starting transfers between devices, with_partners(): lax.ppermute(value, axis, [(i, i ^ d) for i in range(size)])  20.4 us
    all_to_all x3, waiting for transfers between devices, exchange(): return lax.all_to_all(value, axes, split_axis=0, concat_axis=0, tiled=True)  12.1 us
    pallas_call x1, Pallas kernels, mlp(): pl.pallas_call(mlp_kernel, in_specs=[pl.BlockSpec(memory_space=pltpu.VMEM...  9.81 us
    unnamed x31, local copies, waits for them, and re-layouts  5.39 us
    pallas_call x1, Pallas kernels, partial_inverses(): pl.pallas_call(spectrum_kernel, grid=(channels // step,), in_specs=[pl.Bl...  5.2 us
  transfers between devices with their start and end apart: 26, of which 13 were waited for; matrix products, arithmetic and copies ran while one was open for 1% of the time, Pallas kernels for 3%

profile of v4, /device:TPU:6, one launch (start us, length us, event | category | flops | bytes accessed | tf_op | source)
XLA Modules:
  0.0 220.5 jit_solution(4630204786458820139)
XLA Ops:
  0.0 0.8 constant_dynamic-slice_fusion.1
  0.8 0.7 fusion
  1.6 2.0 collective-permute-start
  3.6 3.3 %collective-permute-start.1 = (bf16[24,1152]{1,0:T(8,128)(2,1)S(1)}, bf16[24,1152]{1,0:T(8,128)(2,1)S(1)}, u32[]{:S(2)}, u32[]{:S(2)}) collective-permute-start(bf16[24,1152]{1,0:T(8,128)(2,1)S(1)} %maximum_select_fusion), channel_id=1, source_target_pairs={{0,2},{1,3},{2,0},{3,1},{4,6},{5,7},{6,4},{7,5},{8,10},{9,11},{10,... | collective-permute-start | bytes 165896 | tf_op jit(solution)/shard_map/ppermute | solution.py:290
  6.8 0.0 collective-permute-start.2
  6.8 4.5 %first_sections.1 = bf16[512,1536]{1,0:T(8,128)(2,1)} custom-call(bf16[48,16384]{1,0:T(8,128)(2,1)} %x_ref.3, bf16[512,512]{1,0:T(8,128)(2,1)} %factor_ref.1, bf16[256,256]{1,0:T(8,128)(2,1)} %constant.20.clone.swap_ref), custom_call_target="tpu_custom_call" | custom-call | tf_op jit(solution)/shard_map/first_sections/pallas_call | solution.py:62
  11.4 0.0 collective-permute-done
  11.4 0.0 collective-permute-done.1
  11.4 1.4 collective-permute-done.2
  12.8 9.4 %all-to-all-start = ((bf16[16,32,1536]{2,1,0:T(8,128)(2,1)}), bf16[16,32,1536]{2,1,0:T(8,128)(2,1)S(1)}, u32[]{:S(2)}, u32[]{:S(2)}) async-start(bf16[16,32,1536]{2,1,0:T(8,128)(2,1)} %bitcast), calls=%async_computation | async-start | bytes 3145728 | tf_op jit(solution)/shard_map/all_to_all | solution.py:295
  22.2 1.7 collective-permute-start.6
  23.8 2.9 %collective-permute-start.7 = (bf16[48,1152]{1,0:T(8,128)(2,1)S(1)}, bf16[48,1152]{1,0:T(8,128)(2,1)S(1)}, u32[]{:S(2)}, u32[]{:S(2)}) collective-permute-start(bf16[48,1152]{1,0:T(8,128)(2,1)S(1)} %constant_dynamic-update-slice_fusion.2), channel_id=1, source_target_pairs={{0,8},{4,12},{8,0},{12,4},{1,9},{5,13},{9,1},{13,5},{2,10},{6,14},... | collective-permute-start | bytes 331784 | tf_op jit(solution)/shard_map/ppermute | solution.py:290
  26.7 0.2 collective-permute-start.8
  27.0 0.9 collective-permute-start.3
  27.9 0.7 collective-permute-start.4
  28.6 0.0 collective-permute-done.6
  28.6 3.1 %collective-permute-start.5 = (bf16[48,1152]{1,0:T(8,128)(2,1)S(1)}, bf16[48,1152]{1,0:T(8,128)(2,1)S(1)}, u32[]{:S(2)}, u32[]{:S(2)}) collective-permute-start(bf16[48,1152]{1,0:T(8,128)(2,1)S(1)} %constant_dynamic-update-slice_fusion), channel_id=1, source_target_pairs={{0,96},{32,64},{64,32},{96,0},{1,97},{33,65},{65,33},{97,1},{2,98}... | collective-permute-start | bytes 331784 | tf_op jit(solution)/shard_map/ppermute | solution.py:290
  31.8 1.0 copy.14
  32.8 0.0 collective-permute-done.7
  32.8 1.6 collective-permute-done.8
  34.3 4.2 %collective-permute-done.3 = bf16[48,1152]{1,0:T(8,128)(2,1)S(1)} collective-permute-done((bf16[48,1152]{1,0:T(8,128)(2,1)S(1)}, bf16[48,1152]{1,0:T(8,128)(2,1)S(1)}, u32[]{:S(2)}, u32[]{:S(2)}) %collective-permute-start.3) | collective-permute-done | bytes 110624 | tf_op jit(solution)/shard_map/ppermute | solution.py:290
  38.5 6.5 %collective-permute-done.4 = bf16[48,1152]{1,0:T(8,128)(2,1)S(1)} collective-permute-done((bf16[48,1152]{1,0:T(8,128)(2,1)S(1)}, bf16[48,1152]{1,0:T(8,128)(2,1)S(1)}, u32[]{:S(2)}, u32[]{:S(2)}) %collective-permute-start.4) | collective-permute-done | bytes 110624 | tf_op jit(solution)/shard_map/ppermute | solution.py:290
  45.0 0.0 collective-permute-done.5
  45.0 8.7 %all-to-all-done.in_ref = bf16[16,32,1536]{2,1,0:T(8,128)(2,1)S(1)} async-done(((bf16[16,32,1536]{2,1,0:T(8,128)(2,1)}), bf16[16,32,1536]{2,1,0:T(8,128)(2,1)S(1)}, u32[]{:S(2)}, u32[]{:S(2)}) %all-to-all-start) | async-done | bytes 1572896 | tf_op jit(solution)/shard_map/all_to_all | solution.py:295
  53.7 5.2 %partial_inverses.1 = bf16[512,1536]{1,0:T(8,128)(2,1)} custom-call(bf16[16,32,1536]{2,1,0:T(8,128)(2,1)S(1)} %all-to-all-done.in_ref, bf16[48,32,512]{2,1,0:T(8,128)(2,1)} %kernel_ref.1, bf16[512,512]{1,0:T(8,128)(2,1)} %forward_ref.1, bf16[512,512]{1,0:T(8,128)(2,1)} %bitcast.8), custom_call_target="tpu_custom_call" | custom-call | tf_op jit(solution)/shard_map/partial_inverses/pallas_call | solution.py:109
  59.0 11.4 %all-to-all-start.1 = ((bf16[16,32,1536]{2,1,0:T(8,128)(2,1)}), bf16[16,32,1536]{2,1,0:T(8,128)(2,1)S(1)}, u32[]{:S(2)}, u32[]{:S(2)}) async-start(bf16[16,32,1536]{2,1,0:T(8,128)(2,1)} %bitcast.2), calls=%async_computation.1 | async-start | bytes 3145728 | tf_op jit(solution)/shard_map/all_to_all | solution.py:295
  70.5 0.9 collective-permute-start.12
  71.5 3.3 %collective-permute-start.10 = (bf16[192,1152]{1,0:T(8,128)(2,1)S(1)}, bf16[192,1152]{1,0:T(8,128)(2,1)}, u32[]{:S(2)}, u32[]{:S(2)}) collective-permute-start(bf16[192,1152]{1,0:T(8,128)(2,1)S(1)} %constant_dynamic-update-slice_fusion.4.refs_0_), channel_id=1, source_target_pairs={{0,8},{4,12},{8,0},{12,4},{1,9},{5,13},{9,1},{13,5},{2,10},{6,14},... | collective-permute-start | bytes 1327112 | tf_op jit(solution)/shard_map/ppermute | solution.py:290
  74.8 1.1 collective-permute-start.11
  75.9 0.0 collective-permute-start.9
  75.9 23.0 %collective-permute-done.12.refs_5_ = bf16[192,1152]{1,0:T(8,128)(2,1)S(1)} collective-permute-done((bf16[192,1152]{1,0:T(8,128)(2,1)S(1)}, bf16[192,1152]{1,0:T(8,128)(2,1)S(1)}, u32[]{:S(2)}, u32[]{:S(2)}) %collective-permute-start.12) | collective-permute-done | bytes 442400 | tf_op jit(solution)/shard_map/ppermute | solution.py:290
  98.9 0.0 collective-permute-done.10.refs_2_
  98.9 0.0 collective-permute-done.11.refs_3_
  98.9 0.0 collective-permute-done.9.refs_1_
  98.9 0.0 all-to-all-done.1.in_ref
  98.9 5.1 %residuals.1 = bf16[16,48,1024]{2,1,0:T(8,128)(2,1)} custom-call(bf16[16,32,1536]{2,1,0:T(8,128)(2,1)S(1)} %all-to-all-done.1.in_ref, bf16[48,16384]{1,0:T(8,128)(2,1)} %x_ref.3, bf16[512,512]{1,0:T(8,128)(2,1)} %inverse_ref.1, bf16[256,256]{1,0:T(8,128)(2,1)} %constant.20.clone.swap_ref), custom_call_target="tpu_custom_call" | custom-call | tf_op jit(solution)/shard_map/residuals/pallas_call | solution.py:149
  104.0 23.1 %all-to-all-start.2 = ((bf16[16,48,1024]{2,1,0:T(8,128)(2,1)}), bf16[16,48,1024]{2,1,0:T(8,128)(2,1)S(1)}, u32[]{:S(2)}, u32[]{:S(2)}) async-start(bf16[16,48,1024]{2,1,0:T(8,128)(2,1)} %residuals.1), calls=%async_computation.2 | async-start | bytes 3145728 | tf_op jit(solution)/shard_map/all_to_all | solution.py:295
  127.1 0.1 collective-permute-start.13
  127.2 0.2 collective-permute-start.14
  127.3 13.5 %collective-permute-done.13.refs_6_ = bf16[192,1152]{1,0:T(8,128)(2,1)S(1)} collective-permute-done((bf16[192,1152]{1,0:T(8,128)(2,1)S(1)}, bf16[192,1152]{1,0:T(8,128)(2,1)S(1)}, u32[]{:S(2)}, u32[]{:S(2)}) %collective-permute-start.13) | collective-permute-done | bytes 442400 | tf_op jit(solution)/shard_map/ppermute | solution.py:290
  140.8 9.2 %collective-permute-done.14.refs_7_ = bf16[192,1152]{1,0:T(8,128)(2,1)S(1)} collective-permute-done((bf16[192,1152]{1,0:T(8,128)(2,1)S(1)}, bf16[192,1152]{1,0:T(8,128)(2,1)S(1)}, u32[]{:S(2)}, u32[]{:S(2)}) %collective-permute-start.14) | collective-permute-done | bytes 442400 | tf_op jit(solution)/shard_map/ppermute | solution.py:290
  150.0 0.0 collective-permute-start.22
  150.0 0.5 collective-permute-start.15
  150.5 0.0 collective-permute-start.16
  150.5 0.5 collective-permute-start.17
  151.0 0.0 collective-permute-start.18
  151.0 0.8 collective-permute-done.22.refs_15_
  151.8 0.1 collective-permute-start.19
  151.9 1.1 collective-permute-done.15.refs_8_
  153.1 0.1 collective-permute-start.20
  153.2 0.2 reshape.20.gain_ref
  153.4 0.0 collective-permute-done.16.refs_9_
  153.4 1.2 collective-permute-done.17.refs_10_
  154.5 1.3 collective-permute-done.18.refs_11_
  155.8 0.0 collective-permute-done.19.refs_12_
  155.8 0.0 collective-permute-done.20.refs_13_
  155.8 3.1 %lay_out_weights.1 = (bf16[1536,768]{1,0:T(8,128)(2,1)S(1)}, bf16[1536,768]{1,0:T(8,128)(2,1)S(1)}, bf16[768,1536]{1,0:T(8,128)(2,1)S(1)}) custom-call(s32[1]{0:T(128)} %bitcast.3.core_ref, bf16[192,1152]{1,0:T(8,128)(2,1)S(1)} %constant_dynamic-update-slice_fusion.4.refs_0_, bf16[192,1152]{1,0:T(8,128)(2,1)} %collective-permute-done.9.refs_1_, ...), custom_call_target="tpu_custom_call" | custom-call | bytes 42467328 | tf_op jit(solution)/shard_map/lay_out_weights/pallas_call | solution.py:192
  158.9 1.4 copy-done
  160.3 1.4 copy-done.1
  161.8 1.4 copy-done.2
  163.2 3.4 %all-to-all-done.2.x_ref = bf16[16,48,1024]{2,1,0:T(8,128)(2,1)S(1)} async-done(((bf16[16,48,1024]{2,1,0:T(8,128)(2,1)}), bf16[16,48,1024]{2,1,0:T(8,128)(2,1)S(1)}, u32[]{:S(2)}, u32[]{:S(2)}) %all-to-all-start.2) | async-done | bytes 1572896 | tf_op jit(solution)/shard_map/all_to_all | solution.py:295
  166.6 9.8 %mlp.1 = bf16[16,48,1024]{2,1,0:T(8,128)(2,1)S(1)} custom-call(bf16[16,48,1024]{2,1,0:T(8,128)(2,1)S(1)} %all-to-all-done.2.x_ref, f32[768,1]{1,0:T(8,128)S(1)} %reshape.20.gain_ref, bf16[1536,768]{1,0:T(8,128)(2,1)} %copy-done, bf16[1536,768]{1,0:T(8,128)(2,1)} %copy-done.1, bf16[768,1536]{1,0:T(8,128)(2,1)} %copy-done.2), custom_call_target="tpu_custom_call" | custom-call | tf_op jit(solution)/shard_map/mlp/pallas_call | solution.py:256
  176.4 42.9 %all_to_all.20 = bf16[16,48,1024]{2,1,0:T(8,128)(2,1)S(1)} all-to-all(bf16[16,48,1024]{2,1,0:T(8,128)(2,1)S(1)} %mlp.1), channel_id=1, replica_groups=mesh['zh'=2,'x'=4,'core'=2,'y'=4,'zl'=4] {'y','zl'}, dimensions={0} | all-to-all | bytes 3145728 | tf_op jit(solution)/shard_map/all_to_all | solution.py:295
  219.2 1.3 copy.17
  (34 shorter events, 0.2 us)
Async XLA Ops:
  1.6 9.8 %collective-permute-start = (bf16[24,1152]{1,0:T(8,128)(2,1)S(1)}, bf16[24,1152]{1,0:T(8,128)(2,1)S(1)}, u32[]{:S(2)}, u32[]{:S(2)}) collective-permute-start(bf16[24,1152]{1,0:T(8,128)(2,1)S(1)} %maximum_select_fusion), channel_id=1, source_target_pairs={{0,1},{1,0},{2,3},{3,2},{4,5},{5,4},{6,7},{7,6},{8,9},{9,8},{10,11... | collective-permute-start | bytes 165896 | tf_op jit(solution)/shard_map/ppermute | solution.py:290
  3.6 7.8 %collective-permute-start.1 = (bf16[24,1152]{1,0:T(8,128)(2,1)S(1)}, bf16[24,1152]{1,0:T(8,128)(2,1)S(1)}, u32[]{:S(2)}, u32[]{:S(2)}) collective-permute-start(bf16[24,1152]{1,0:T(8,128)(2,1)S(1)} %maximum_select_fusion), channel_id=1, source_target_pairs={{0,2},{1,3},{2,0},{3,1},{4,6},{5,7},{6,4},{7,5},{8,10},{9,11},{10,... | collective-permute-start | bytes 165896 | tf_op jit(solution)/shard_map/ppermute | solution.py:290
  6.8 6.0 %collective-permute-start.2 = (bf16[24,1152]{1,0:T(8,128)(2,1)S(1)}, bf16[24,1152]{1,0:T(8,128)(2,1)S(1)}, u32[]{:S(2)}, u32[]{:S(2)}) collective-permute-start(bf16[24,1152]{1,0:T(8,128)(2,1)S(1)} %maximum_select_fusion), channel_id=1, source_target_pairs={{0,3},{1,2},{2,1},{3,0},{4,7},{5,6},{6,5},{7,4},{8,11},{9,10},{10,... | collective-permute-start | bytes 165896 | tf_op jit(solution)/shard_map/ppermute | solution.py:290
  12.8 19.0 %copy-start.3 = (bf16[512,512]{1,0:T(8,128)(2,1)S(1)}, bf16[512,512]{1,0:T(8,128)(2,1)}, u32[]{:S(2)}) copy-start(bf16[512,512]{1,0:T(8,128)(2,1)} %param.17) | copy-start | bytes 1572868
  12.8 40.9 %all-to-all-start = ((bf16[16,32,1536]{2,1,0:T(8,128)(2,1)}), bf16[16,32,1536]{2,1,0:T(8,128)(2,1)S(1)}, u32[]{:S(2)}, u32[]{:S(2)}) async-start(bf16[16,32,1536]{2,1,0:T(8,128)(2,1)} %bitcast), calls=%async_computation | async-start | bytes 3145728 | tf_op jit(solution)/shard_map/all_to_all | solution.py:295
  22.2 6.5 %collective-permute-start.6 = (bf16[48,1152]{1,0:T(8,128)(2,1)S(1)}, bf16[48,1152]{1,0:T(8,128)(2,1)S(1)}, u32[]{:S(2)}, u32[]{:S(2)}) collective-permute-start(bf16[48,1152]{1,0:T(8,128)(2,1)S(1)} %constant_dynamic-update-slice_fusion.2), channel_id=1, source_target_pairs={{0,4},{4,0},{8,12},{12,8},{1,5},{5,1},{9,13},{13,9},{2,6},{6,2},{1... | collective-permute-start | bytes 331784 | tf_op jit(solution)/shard_map/ppermute | solution.py:290
  23.8 8.9 %collective-permute-start.7 = (bf16[48,1152]{1,0:T(8,128)(2,1)S(1)}, bf16[48,1152]{1,0:T(8,128)(2,1)S(1)}, u32[]{:S(2)}, u32[]{:S(2)}) collective-permute-start(bf16[48,1152]{1,0:T(8,128)(2,1)S(1)} %constant_dynamic-update-slice_fusion.2), channel_id=1, source_target_pairs={{0,8},{4,12},{8,0},{12,4},{1,9},{5,13},{9,1},{13,5},{2,10},{6,14},... | collective-permute-start | bytes 331784 | tf_op jit(solution)/shard_map/ppermute | solution.py:290
  26.7 7.6 %collective-permute-start.8 = (bf16[48,1152]{1,0:T(8,128)(2,1)S(1)}, bf16[48,1152]{1,0:T(8,128)(2,1)S(1)}, u32[]{:S(2)}, u32[]{:S(2)}) collective-permute-start(bf16[48,1152]{1,0:T(8,128)(2,1)S(1)} %constant_dynamic-update-slice_fusion.2), channel_id=1, source_target_pairs={{0,12},{4,8},{8,4},{12,0},{1,13},{5,9},{9,5},{13,1},{2,14},{6,10},... | collective-permute-start | bytes 331784 | tf_op jit(solution)/shard_map/ppermute | solution.py:290
  27.0 11.5 %collective-permute-start.3 = (bf16[48,1152]{1,0:T(8,128)(2,1)S(1)}, bf16[48,1152]{1,0:T(8,128)(2,1)S(1)}, u32[]{:S(2)}, u32[]{:S(2)}) collective-permute-start(bf16[48,1152]{1,0:T(8,128)(2,1)S(1)} %constant_dynamic-update-slice_fusion), channel_id=1, source_target_pairs={{0,32},{32,0},{64,96},{96,64},{1,33},{33,1},{65,97},{97,65},{2,34}... | collective-permute-start | bytes 331784 | tf_op jit(solution)/shard_map/ppermute | solution.py:290
  27.9 17.1 %collective-permute-start.4 = (bf16[48,1152]{1,0:T(8,128)(2,1)S(1)}, bf16[48,1152]{1,0:T(8,128)(2,1)S(1)}, u32[]{:S(2)}, u32[]{:S(2)}) collective-permute-start(bf16[48,1152]{1,0:T(8,128)(2,1)S(1)} %constant_dynamic-update-slice_fusion), channel_id=1, source_target_pairs={{0,64},{32,96},{64,0},{96,32},{1,65},{33,97},{65,1},{97,33},{2,66}... | collective-permute-start | bytes 331784 | tf_op jit(solution)/shard_map/ppermute | solution.py:290
  28.6 16.4 %collective-permute-start.5 = (bf16[48,1152]{1,0:T(8,128)(2,1)S(1)}, bf16[48,1152]{1,0:T(8,128)(2,1)S(1)}, u32[]{:S(2)}, u32[]{:S(2)}) collective-permute-start(bf16[48,1152]{1,0:T(8,128)(2,1)S(1)} %constant_dynamic-update-slice_fusion), channel_id=1, source_target_pairs={{0,96},{32,64},{64,32},{96,0},{1,97},{33,65},{65,33},{97,1},{2,98}... | collective-permute-start | bytes 331784 | tf_op jit(solution)/shard_map/ppermute | solution.py:290
  38.5 20.5 %copy-start.4 = (bf16[48,1152]{1,0:T(8,128)(2,1)}, bf16[48,1152]{1,0:T(8,128)(2,1)S(1)}, u32[]{:S(2)}) copy-start(bf16[48,1152]{1,0:T(8,128)(2,1)S(1)} %collective-permute-done.3) | copy-start | bytes 331780
  45.0 13.9 %copy-start.6 = (bf16[48,1152]{1,0:T(8,128)(2,1)}, bf16[48,1152]{1,0:T(8,128)(2,1)S(1)}, u32[]{:S(2)}) copy-start(bf16[48,1152]{1,0:T(8,128)(2,1)S(1)} %collective-permute-done.4) | copy-start | bytes 331780
  45.0 13.9 %copy-start.8 = (bf16[48,1152]{1,0:T(8,128)(2,1)}, bf16[48,1152]{1,0:T(8,128)(2,1)S(1)}, u32[]{:S(2)}) copy-start(bf16[48,1152]{1,0:T(8,128)(2,1)S(1)} %collective-permute-done.5) | copy-start | bytes 331780
  58.9 12.5 %copy-start.5 = (bf16[48,1152]{1,0:T(8,128)(2,1)S(1)}, bf16[48,1152]{1,0:T(8,128)(2,1)}, u32[]{:S(2)}) copy-start(bf16[48,1152]{1,0:T(8,128)(2,1)} %copy-done.4) | copy-start | bytes 331780
  58.9 12.5 %copy-start.7 = (bf16[48,1152]{1,0:T(8,128)(2,1)S(1)}, bf16[48,1152]{1,0:T(8,128)(2,1)}, u32[]{:S(2)}) copy-start(bf16[48,1152]{1,0:T(8,128)(2,1)} %copy-done.6) | copy-start | bytes 331780
  59.0 12.6 %copy-start.9 = (bf16[48,1152]{1,0:T(8,128)(2,1)S(1)}, bf16[48,1152]{1,0:T(8,128)(2,1)}, u32[]{:S(2)}) copy-start(bf16[48,1152]{1,0:T(8,128)(2,1)} %copy-done.8) | copy-start | bytes 331780
  59.0 39.9 %all-to-all-start.1 = ((bf16[16,32,1536]{2,1,0:T(8,128)(2,1)}), bf16[16,32,1536]{2,1,0:T(8,128)(2,1)S(1)}, u32[]{:S(2)}, u32[]{:S(2)}) async-start(bf16[16,32,1536]{2,1,0:T(8,128)(2,1)} %bitcast.2), calls=%async_computation.1 | async-start | bytes 3145728 | tf_op jit(solution)/shard_map/all_to_all | solution.py:295
  70.5 28.4 %collective-permute-start.12 = (bf16[192,1152]{1,0:T(8,128)(2,1)S(1)}, bf16[192,1152]{1,0:T(8,128)(2,1)S(1)}, u32[]{:S(2)}, u32[]{:S(2)}) collective-permute-start(bf16[192,1152]{1,0:T(8,128)(2,1)S(1)} %constant_dynamic-update-slice_fusion.8.refs_4_), channel_id=1, source_target_pairs={{0,32},{32,0},{64,96},{96,64},{1,33},{33,1},{65,97},{97,65},{2,34}... | collective-permute-start | bytes 1327112 | tf_op jit(solution)/shard_map/ppermute | solution.py:290
  71.5 27.4 %collective-permute-start.10 = (bf16[192,1152]{1,0:T(8,128)(2,1)S(1)}, bf16[192,1152]{1,0:T(8,128)(2,1)}, u32[]{:S(2)}, u32[]{:S(2)}) collective-permute-start(bf16[192,1152]{1,0:T(8,128)(2,1)S(1)} %constant_dynamic-update-slice_fusion.4.refs_0_), channel_id=1, source_target_pairs={{0,8},{4,12},{8,0},{12,4},{1,9},{5,13},{9,1},{13,5},{2,10},{6,14},... | collective-permute-start | bytes 1327112 | tf_op jit(solution)/shard_map/ppermute | solution.py:290
  74.8 24.1 %collective-permute-start.11 = (bf16[192,1152]{1,0:T(8,128)(2,1)S(1)}, bf16[192,1152]{1,0:T(8,128)(2,1)}, u32[]{:S(2)}, u32[]{:S(2)}) collective-permute-start(bf16[192,1152]{1,0:T(8,128)(2,1)S(1)} %constant_dynamic-update-slice_fusion.4.refs_0_), channel_id=1, source_target_pairs={{0,12},{4,8},{8,4},{12,0},{1,13},{5,9},{9,5},{13,1},{2,14},{6,10},... | collective-permute-start | bytes 1327112 | tf_op jit(solution)/shard_map/ppermute | solution.py:290
  75.9 23.0 %collective-permute-start.9 = (bf16[192,1152]{1,0:T(8,128)(2,1)S(1)}, bf16[192,1152]{1,0:T(8,128)(2,1)}, u32[]{:S(2)}, u32[]{:S(2)}) collective-permute-start(bf16[192,1152]{1,0:T(8,128)(2,1)S(1)} %constant_dynamic-update-slice_fusion.4.refs_0_), channel_id=1, source_target_pairs={{0,4},{4,0},{8,12},{12,8},{1,5},{5,1},{9,13},{13,9},{2,6},{6,2},{1... | collective-permute-start | bytes 1327112 | tf_op jit(solution)/shard_map/ppermute | solution.py:290
  104.0 49.2 %copy-start.10 = (f32[768]{0:T(1024)S(1)}, f32[768]{0:T(1024)}, u32[]{:S(2)}) copy-start(f32[768]{0:T(1024)} %param.18) | copy-start | bytes 9220
  104.0 62.6 %all-to-all-start.2 = ((bf16[16,48,1024]{2,1,0:T(8,128)(2,1)}), bf16[16,48,1024]{2,1,0:T(8,128)(2,1)S(1)}, u32[]{:S(2)}, u32[]{:S(2)}) async-start(bf16[16,48,1024]{2,1,0:T(8,128)(2,1)} %residuals.1), calls=%async_computation.2 | async-start | bytes 3145728 | tf_op jit(solution)/shard_map/all_to_all | solution.py:295
  127.1 13.8 %collective-permute-start.13 = (bf16[192,1152]{1,0:T(8,128)(2,1)S(1)}, bf16[192,1152]{1,0:T(8,128)(2,1)S(1)}, u32[]{:S(2)}, u32[]{:S(2)}) collective-permute-start(bf16[192,1152]{1,0:T(8,128)(2,1)S(1)} %constant_dynamic-update-slice_fusion.8.refs_4_), channel_id=1, source_target_pairs={{0,64},{32,96},{64,0},{96,32},{1,65},{33,97},{65,1},{97,33},{2,66}... | collective-permute-start | bytes 1327112 | tf_op jit(solution)/shard_map/ppermute | solution.py:290
  127.2 22.8 %collective-permute-start.14 = (bf16[192,1152]{1,0:T(8,128)(2,1)S(1)}, bf16[192,1152]{1,0:T(8,128)(2,1)S(1)}, u32[]{:S(2)}, u32[]{:S(2)}) collective-permute-start(bf16[192,1152]{1,0:T(8,128)(2,1)S(1)} %constant_dynamic-update-slice_fusion.8.refs_4_), channel_id=1, source_target_pairs={{0,96},{32,64},{64,32},{96,0},{1,97},{33,65},{65,33},{97,1},{2,98}... | collective-permute-start | bytes 1327112 | tf_op jit(solution)/shard_map/ppermute | solution.py:290
  140.8 10.2 %collective-permute-start.21 = (bf16[192,1152]{1,0:T(8,128)(2,1)S(1)}, bf16[192,1152]{1,0:T(8,128)(2,1)S(1)}, u32[]{:S(2)}, u32[]{:S(2)}) collective-permute-start(bf16[192,1152]{1,0:T(8,128)(2,1)S(1)} %collective-permute-done.13.refs_6_), channel_id=1, source_target_pairs={{0,16},{16,0},{1,17},{17,1},{2,18},{18,2},{3,19},{19,3},{4,20},{20... | collective-permute-start | bytes 1327112 | tf_op jit(solution)/shard_map/ppermute | solution.py:325
  150.0 1.8 collective-permute-start.22
  150.0 3.1 %collective-permute-start.15 = (bf16[192,1152]{1,0:T(8,128)(2,1)S(1)}, bf16[192,1152]{1,0:T(8,128)(2,1)S(1)}, u32[]{:S(2)}, u32[]{:S(2)}) collective-permute-start(bf16[192,1152]{1,0:T(8,128)(2,1)S(1)} %constant_dynamic-update-slice_fusion.4.refs_0_), channel_id=1, source_target_pairs={{0,16},{16,0},{1,17},{17,1},{2,18},{18,2},{3,19},{19,3},{4,20},{20... | collective-permute-start | bytes 1327112 | tf_op jit(solution)/shard_map/ppermute | solution.py:325
  150.5 2.9 %collective-permute-start.16 = (bf16[192,1152]{1,0:T(8,128)(2,1)}, bf16[192,1152]{1,0:T(8,128)(2,1)S(1)}, u32[]{:S(2)}, u32[]{:S(2)}) collective-permute-start(bf16[192,1152]{1,0:T(8,128)(2,1)} %collective-permute-done.9.refs_1_), channel_id=1, source_target_pairs={{0,16},{16,0},{1,17},{17,1},{2,18},{18,2},{3,19},{19,3},{4,20},{20... | collective-permute-start | bytes 1327112 | tf_op jit(solution)/shard_map/ppermute | solution.py:325
  150.5 4.0 %collective-permute-start.17 = (bf16[192,1152]{1,0:T(8,128)(2,1)}, bf16[192,1152]{1,0:T(8,128)(2,1)S(1)}, u32[]{:S(2)}, u32[]{:S(2)}) collective-permute-start(bf16[192,1152]{1,0:T(8,128)(2,1)} %collective-permute-done.10.refs_2_), channel_id=1, source_target_pairs={{0,16},{16,0},{1,17},{17,1},{2,18},{18,2},{3,19},{19,3},{4,20},{20... | collective-permute-start | bytes 1327112 | tf_op jit(solution)/shard_map/ppermute | solution.py:325
  151.0 4.8 %collective-permute-start.18 = (bf16[192,1152]{1,0:T(8,128)(2,1)}, bf16[192,1152]{1,0:T(8,128)(2,1)S(1)}, u32[]{:S(2)}, u32[]{:S(2)}) collective-permute-start(bf16[192,1152]{1,0:T(8,128)(2,1)} %collective-permute-done.11.refs_3_), channel_id=1, source_target_pairs={{0,16},{16,0},{1,17},{17,1},{2,18},{18,2},{3,19},{19,3},{4,20},{20... | collective-permute-start | bytes 1327112 | tf_op jit(solution)/shard_map/ppermute | solution.py:325
  151.8 4.0 %collective-permute-start.19 = (bf16[192,1152]{1,0:T(8,128)(2,1)S(1)}, bf16[192,1152]{1,0:T(8,128)(2,1)S(1)}, u32[]{:S(2)}, u32[]{:S(2)}) collective-permute-start(bf16[192,1152]{1,0:T(8,128)(2,1)S(1)} %constant_dynamic-update-slice_fusion.8.refs_4_), channel_id=1, source_target_pairs={{0,16},{16,0},{1,17},{17,1},{2,18},{18,2},{3,19},{19,3},{4,20},{20... | collective-permute-start | bytes 1327112 | tf_op jit(solution)/shard_map/ppermute | solution.py:325
  153.1 2.7 %collective-permute-start.20 = (bf16[192,1152]{1,0:T(8,128)(2,1)S(1)}, bf16[192,1152]{1,0:T(8,128)(2,1)S(1)}, u32[]{:S(2)}, u32[]{:S(2)}) collective-permute-start(bf16[192,1152]{1,0:T(8,128)(2,1)S(1)} %collective-permute-done.12.refs_5_), channel_id=1, source_target_pairs={{0,16},{16,0},{1,17},{17,1},{2,18},{18,2},{3,19},{19,3},{4,20},{20... | collective-permute-start | bytes 1327112 | tf_op jit(solution)/shard_map/ppermute | solution.py:325
  158.9 1.4 copy-start
  160.3 1.4 copy-start.1
  161.8 1.4 copy-start.2

commit v5 on v4

--- a/solution.py
+++ b/solution.py
@@ -199,9 +199,9 @@
             whole((channels, hidden_units)),
         ],
         out_shape=[
-            jax.ShapeDtypeStruct((hidden_units, channels), BF16),
-            jax.ShapeDtypeStruct((hidden_units, channels), BF16),
-            jax.ShapeDtypeStruct((channels, hidden_units), BF16),
+            pltpu.HBM((hidden_units, channels), BF16),
+            pltpu.HBM((hidden_units, channels), BF16),
+            pltpu.HBM((channels, hidden_units), BF16),
         ],
         compiler_params=params(40),
         cost_estimate=pl.CostEstimate(flops=0, bytes_accessed=12 * rows * columns * len(pieces), transcendentals=0),

time: 221 us -> 221 us (level)
  local copies, waits for them, and re-layouts: 8.42 us -> 4.17 us
  Pallas kernels: 27.7 us -> 30.5 us
    unnamed x31 -> x25, local copies, waits for them, and re-layouts: 5.39 us -> 1.13 us
    pallas_call x1, Pallas kernels: 3.09 us -> 5.95 us  [lay_out(): pl.pallas_call(layout_kernel, in_specs=[pl.BlockSpec(memory_space=pltpu.S...]
  transfers between devices with their start and end apart: 26 -> 26, of which waited for: 13 -> 13; matrix products, arithmetic and copies ran while one was open for 1% -> 1% of each run, Pallas kernels for 3% -> 5%
where the time goes in v5:
time: 221 us; the launch traced here: 220 us
  waiting for transfers between devices  77.2 us (35%)
  starting transfers between devices  65.6 us (30%)
  blocking collectives  42.6 us (19%)
  Pallas kernels  30.5 us (14%)
  local copies, waits for them, and re-layouts  4.17 us (2%)
    ppermute x15, waiting for transfers between devices, with_partners(): lax.ppermute(value, axis, [(i, i ^ d) for i in range(size)])  59.3 us
    all_to_all x3, starting transfers between devices, exchange(): return lax.all_to_all(value, axes, split_axis=0, concat_axis=0, tiled=True)  43.9 us
    all_to_all x1, blocking collectives, exchange(): return lax.all_to_all(value, axes, split_axis=0, concat_axis=0, tiled=True)  42.6 us
    ppermute x15, starting transfers between devices, with_partners(): lax.ppermute(value, axis, [(i, i ^ d) for i in range(size)])  20.4 us
    all_to_all x3, waiting for transfers between devices, exchange(): return lax.all_to_all(value, axes, split_axis=0, concat_axis=0, tiled=True)  13.5 us
    pallas_call x1, Pallas kernels, mlp(): pl.pallas_call(mlp_kernel, in_specs=[pl.BlockSpec(memory_space=pltpu.VMEM...  9.81 us
    pallas_call x1, Pallas kernels, lay_out(): pl.pallas_call(layout_kernel, in_specs=[pl.BlockSpec(memory_space=pltpu.S...  5.95 us
    pallas_call x1, Pallas kernels, partial_inverses(): pl.pallas_call(spectrum_kernel, grid=(channels // step,), in_specs=[pl.Bl...  5.2 us
  transfers between devices with their start and end apart: 26, of which 13 were waited for; matrix products, arithmetic and copies ran while one was open for 1% of the time, Pallas kernels for 5%

profile of v5, /device:TPU:6, one launch (start us, length us, event | category | flops | bytes accessed | tf_op | source)
XLA Modules:
  0.0 220.3 jit_solution(11451102947028517564)
XLA Ops:
  0.0 0.8 constant_dynamic-slice_fusion.1
  0.8 0.7 fusion
  1.6 2.0 collective-permute-start
  3.6 3.3 %collective-permute-start.1 = (bf16[24,1152]{1,0:T(8,128)(2,1)S(1)}, bf16[24,1152]{1,0:T(8,128)(2,1)S(1)}, u32[]{:S(2)}, u32[]{:S(2)}) collective-permute-start(bf16[24,1152]{1,0:T(8,128)(2,1)S(1)} %maximum_select_fusion), channel_id=1, source_target_pairs={{0,2},{1,3},{2,0},{3,1},{4,6},{5,7},{6,4},{7,5},{8,10},{9,11},{10,... | collective-permute-start | bytes 165896 | tf_op jit(solution)/shard_map/ppermute | solution.py:290
  6.8 0.0 collective-permute-start.2
  6.8 4.5 %first_sections.1 = bf16[512,1536]{1,0:T(8,128)(2,1)} custom-call(bf16[48,16384]{1,0:T(8,128)(2,1)} %x_ref.3, bf16[512,512]{1,0:T(8,128)(2,1)} %factor_ref.1, bf16[256,256]{1,0:T(8,128)(2,1)} %constant.20.clone.swap_ref), custom_call_target="tpu_custom_call" | custom-call | tf_op jit(solution)/shard_map/first_sections/pallas_call | solution.py:62
  11.4 0.0 collective-permute-done
  11.4 0.0 collective-permute-done.1
  11.4 1.4 collective-permute-done.2
  12.8 9.4 %all-to-all-start = ((bf16[16,32,1536]{2,1,0:T(8,128)(2,1)}), bf16[16,32,1536]{2,1,0:T(8,128)(2,1)S(1)}, u32[]{:S(2)}, u32[]{:S(2)}) async-start(bf16[16,32,1536]{2,1,0:T(8,128)(2,1)} %bitcast), calls=%async_computation | async-start | bytes 3145728 | tf_op jit(solution)/shard_map/all_to_all | solution.py:295
  22.2 1.7 collective-permute-start.6
  23.8 2.9 %collective-permute-start.7 = (bf16[48,1152]{1,0:T(8,128)(2,1)S(1)}, bf16[48,1152]{1,0:T(8,128)(2,1)S(1)}, u32[]{:S(2)}, u32[]{:S(2)}) collective-permute-start(bf16[48,1152]{1,0:T(8,128)(2,1)S(1)} %constant_dynamic-update-slice_fusion.2), channel_id=1, source_target_pairs={{0,8},{4,12},{8,0},{12,4},{1,9},{5,13},{9,1},{13,5},{2,10},{6,14},... | collective-permute-start | bytes 331784 | tf_op jit(solution)/shard_map/ppermute | solution.py:290
  26.7 0.2 collective-permute-start.8
  27.0 0.9 collective-permute-start.3
  27.9 0.7 collective-permute-start.4
  28.6 0.0 collective-permute-done.6
  28.6 3.1 %collective-permute-start.5 = (bf16[48,1152]{1,0:T(8,128)(2,1)S(1)}, bf16[48,1152]{1,0:T(8,128)(2,1)S(1)}, u32[]{:S(2)}, u32[]{:S(2)}) collective-permute-start(bf16[48,1152]{1,0:T(8,128)(2,1)S(1)} %constant_dynamic-update-slice_fusion), channel_id=1, source_target_pairs={{0,96},{32,64},{64,32},{96,0},{1,97},{33,65},{65,33},{97,1},{2,98}... | collective-permute-start | bytes 331784 | tf_op jit(solution)/shard_map/ppermute | solution.py:290
  31.8 0.0 copy-done
  31.8 1.0 copy.14
  32.8 0.0 collective-permute-done.7
  32.8 1.5 collective-permute-done.8
  34.3 4.2 %collective-permute-done.3 = bf16[48,1152]{1,0:T(8,128)(2,1)S(1)} collective-permute-done((bf16[48,1152]{1,0:T(8,128)(2,1)S(1)}, bf16[48,1152]{1,0:T(8,128)(2,1)S(1)}, u32[]{:S(2)}, u32[]{:S(2)}) %collective-permute-start.3) | collective-permute-done | bytes 110624 | tf_op jit(solution)/shard_map/ppermute | solution.py:290
  38.5 6.5 %collective-permute-done.4 = bf16[48,1152]{1,0:T(8,128)(2,1)S(1)} collective-permute-done((bf16[48,1152]{1,0:T(8,128)(2,1)S(1)}, bf16[48,1152]{1,0:T(8,128)(2,1)S(1)}, u32[]{:S(2)}, u32[]{:S(2)}) %collective-permute-start.4) | collective-permute-done | bytes 110624 | tf_op jit(solution)/shard_map/ppermute | solution.py:290
  45.0 0.0 collective-permute-done.5
  45.0 8.7 %all-to-all-done.in_ref = bf16[16,32,1536]{2,1,0:T(8,128)(2,1)S(1)} async-done(((bf16[16,32,1536]{2,1,0:T(8,128)(2,1)}), bf16[16,32,1536]{2,1,0:T(8,128)(2,1)S(1)}, u32[]{:S(2)}, u32[]{:S(2)}) %all-to-all-start) | async-done | bytes 1572896 | tf_op jit(solution)/shard_map/all_to_all | solution.py:295
  53.7 5.2 %partial_inverses.1 = bf16[512,1536]{1,0:T(8,128)(2,1)} custom-call(bf16[16,32,1536]{2,1,0:T(8,128)(2,1)S(1)} %all-to-all-done.in_ref, bf16[48,32,512]{2,1,0:T(8,128)(2,1)} %kernel_ref.1, bf16[512,512]{1,0:T(8,128)(2,1)} %forward_ref.1, bf16[512,512]{1,0:T(8,128)(2,1)} %bitcast.8), custom_call_target="tpu_custom_call" | custom-call | tf_op jit(solution)/shard_map/partial_inverses/pallas_call | solution.py:109
  59.0 11.4 %all-to-all-start.1 = ((bf16[16,32,1536]{2,1,0:T(8,128)(2,1)}), bf16[16,32,1536]{2,1,0:T(8,128)(2,1)S(1)}, u32[]{:S(2)}, u32[]{:S(2)}) async-start(bf16[16,32,1536]{2,1,0:T(8,128)(2,1)} %bitcast.2), calls=%async_computation.1 | async-start | bytes 3145728 | tf_op jit(solution)/shard_map/all_to_all | solution.py:295
  70.5 0.9 collective-permute-start.12
  71.5 3.3 %collective-permute-start.10 = (bf16[192,1152]{1,0:T(8,128)(2,1)S(1)}, bf16[192,1152]{1,0:T(8,128)(2,1)}, u32[]{:S(2)}, u32[]{:S(2)}) collective-permute-start(bf16[192,1152]{1,0:T(8,128)(2,1)S(1)} %constant_dynamic-update-slice_fusion.4.refs_0_), channel_id=1, source_target_pairs={{0,8},{4,12},{8,0},{12,4},{1,9},{5,13},{9,1},{13,5},{2,10},{6,14},... | collective-permute-start | bytes 1327112 | tf_op jit(solution)/shard_map/ppermute | solution.py:290
  74.8 1.1 collective-permute-start.11
  75.9 0.0 collective-permute-start.9
  75.9 23.0 %collective-permute-done.12.refs_5_ = bf16[192,1152]{1,0:T(8,128)(2,1)S(1)} collective-permute-done((bf16[192,1152]{1,0:T(8,128)(2,1)S(1)}, bf16[192,1152]{1,0:T(8,128)(2,1)S(1)}, u32[]{:S(2)}, u32[]{:S(2)}) %collective-permute-start.12) | collective-permute-done | bytes 442400 | tf_op jit(solution)/shard_map/ppermute | solution.py:290
  98.9 0.0 collective-permute-done.10.refs_2_
  98.9 0.0 collective-permute-done.11.refs_3_
  98.9 0.0 collective-permute-done.9.refs_1_
  98.9 0.0 all-to-all-done.1.in_ref
  98.9 5.1 %residuals.1 = bf16[16,48,1024]{2,1,0:T(8,128)(2,1)} custom-call(bf16[16,32,1536]{2,1,0:T(8,128)(2,1)S(1)} %all-to-all-done.1.in_ref, bf16[48,16384]{1,0:T(8,128)(2,1)} %x_ref.3, bf16[512,512]{1,0:T(8,128)(2,1)} %inverse_ref.1, bf16[256,256]{1,0:T(8,128)(2,1)} %constant.20.clone.swap_ref), custom_call_target="tpu_custom_call" | custom-call | tf_op jit(solution)/shard_map/residuals/pallas_call | solution.py:149
  104.0 23.1 %all-to-all-start.2 = ((bf16[16,48,1024]{2,1,0:T(8,128)(2,1)}), bf16[16,48,1024]{2,1,0:T(8,128)(2,1)S(1)}, u32[]{:S(2)}, u32[]{:S(2)}) async-start(bf16[16,48,1024]{2,1,0:T(8,128)(2,1)} %residuals.1), calls=%async_computation.2 | async-start | bytes 3145728 | tf_op jit(solution)/shard_map/all_to_all | solution.py:295
  127.1 0.1 collective-permute-start.13
  127.2 0.2 collective-permute-start.14
  127.3 13.5 %collective-permute-done.13.refs_6_ = bf16[192,1152]{1,0:T(8,128)(2,1)S(1)} collective-permute-done((bf16[192,1152]{1,0:T(8,128)(2,1)S(1)}, bf16[192,1152]{1,0:T(8,128)(2,1)S(1)}, u32[]{:S(2)}, u32[]{:S(2)}) %collective-permute-start.13) | collective-permute-done | bytes 442400 | tf_op jit(solution)/shard_map/ppermute | solution.py:290
  140.8 0.0 collective-permute-start.21
  140.8 9.2 %collective-permute-done.14.refs_7_ = bf16[192,1152]{1,0:T(8,128)(2,1)S(1)} collective-permute-done((bf16[192,1152]{1,0:T(8,128)(2,1)S(1)}, bf16[192,1152]{1,0:T(8,128)(2,1)S(1)}, u32[]{:S(2)}, u32[]{:S(2)}) %collective-permute-start.14) | collective-permute-done | bytes 442400 | tf_op jit(solution)/shard_map/ppermute | solution.py:290
  150.0 0.0 collective-permute-start.22
  150.0 0.5 collective-permute-start.15
  150.5 0.0 collective-permute-start.16
  150.5 0.5 collective-permute-start.17
  151.0 0.0 collective-permute-done.21.refs_14_
  151.0 0.0 collective-permute-start.18
  151.0 0.8 collective-permute-done.22.refs_15_
  151.8 0.1 collective-permute-start.19
  151.9 1.1 collective-permute-done.15.refs_8_
  153.1 0.1 collective-permute-start.20
  153.2 0.2 reshape.20.gain_ref
  153.4 0.0 collective-permute-done.16.refs_9_
  153.4 1.2 collective-permute-done.17.refs_10_
  154.5 1.3 collective-permute-done.18.refs_11_
  155.8 0.0 collective-permute-done.19.refs_12_
  155.8 0.0 collective-permute-done.20.refs_13_
  155.8 6.0 %lay_out_weights.1 = (bf16[1536,768]{1,0:T(8,128)(2,1)}, bf16[1536,768]{1,0:T(8,128)(2,1)}, bf16[768,1536]{1,0:T(8,128)(2,1)}) custom-call(s32[1]{0:T(128)} %bitcast.3.core_ref, bf16[192,1152]{1,0:T(8,128)(2,1)S(1)} %constant_dynamic-update-slice_fusion.4.refs_0_, bf16[192,1152]{1,0:T(8,128)(2,1)} %collective-permute-done.9.refs_1_, ...), custom_call_target="tpu_custom_call" | custom-call | bytes 42467328 | tf_op jit(solution)/shard_map/lay_out_weights/pallas_call | solution.py:192
  161.8 4.8 %all-to-all-done.2.x_ref = bf16[16,48,1024]{2,1,0:T(8,128)(2,1)S(1)} async-done(((bf16[16,48,1024]{2,1,0:T(8,128)(2,1)}), bf16[16,48,1024]{2,1,0:T(8,128)(2,1)S(1)}, u32[]{:S(2)}, u32[]{:S(2)}) %all-to-all-start.2) | async-done | bytes 1572896 | tf_op jit(solution)/shard_map/all_to_all | solution.py:295
  166.6 9.8 %mlp.1 = bf16[16,48,1024]{2,1,0:T(8,128)(2,1)S(1)} custom-call(bf16[16,48,1024]{2,1,0:T(8,128)(2,1)S(1)} %all-to-all-done.2.x_ref, f32[768,1]{1,0:T(8,128)S(1)} %reshape.20.gain_ref, bf16[1536,768]{1,0:T(8,128)(2,1)} %get-tuple-element.50.gate_hbm, bf16[1536,768]{1,0:T(8,128)(2,1)} %get-tuple-element.51.up_hbm, bf16[768,1536]{1,0:T(8,128)(2,1)} %get-tuple-element.52.down_hbm), custom_call_target="tpu_custom_call" | custom-call | tf_op jit(solution)/shard_map/mlp/pallas_call | solution.py:256
  176.4 42.6 %all_to_all.20 = bf16[16,48,1024]{2,1,0:T(8,128)(2,1)S(1)} all-to-all(bf16[16,48,1024]{2,1,0:T(8,128)(2,1)S(1)} %mlp.1), channel_id=1, replica_groups=mesh['zh'=2,'x'=4,'core'=2,'y'=4,'zl'=4] {'y','zl'}, dimensions={0} | all-to-all | bytes 3145728 | tf_op jit(solution)/shard_map/all_to_all | solution.py:295
  219.0 1.3 copy.17
  (28 shorter events, 0.2 us)
Async XLA Ops:
  1.6 9.8 %collective-permute-start = (bf16[24,1152]{1,0:T(8,128)(2,1)S(1)}, bf16[24,1152]{1,0:T(8,128)(2,1)S(1)}, u32[]{:S(2)}, u32[]{:S(2)}) collective-permute-start(bf16[24,1152]{1,0:T(8,128)(2,1)S(1)} %maximum_select_fusion), channel_id=1, source_target_pairs={{0,1},{1,0},{2,3},{3,2},{4,5},{5,4},{6,7},{7,6},{8,9},{9,8},{10,11... | collective-permute-start | bytes 165896 | tf_op jit(solution)/shard_map/ppermute | solution.py:290
  3.6 7.8 %collective-permute-start.1 = (bf16[24,1152]{1,0:T(8,128)(2,1)S(1)}, bf16[24,1152]{1,0:T(8,128)(2,1)S(1)}, u32[]{:S(2)}, u32[]{:S(2)}) collective-permute-start(bf16[24,1152]{1,0:T(8,128)(2,1)S(1)} %maximum_select_fusion), channel_id=1, source_target_pairs={{0,2},{1,3},{2,0},{3,1},{4,6},{5,7},{6,4},{7,5},{8,10},{9,11},{10,... | collective-permute-start | bytes 165896 | tf_op jit(solution)/shard_map/ppermute | solution.py:290
  6.8 6.0 %collective-permute-start.2 = (bf16[24,1152]{1,0:T(8,128)(2,1)S(1)}, bf16[24,1152]{1,0:T(8,128)(2,1)S(1)}, u32[]{:S(2)}, u32[]{:S(2)}) collective-permute-start(bf16[24,1152]{1,0:T(8,128)(2,1)S(1)} %maximum_select_fusion), channel_id=1, source_target_pairs={{0,3},{1,2},{2,1},{3,0},{4,7},{5,6},{6,5},{7,4},{8,11},{9,10},{10,... | collective-permute-start | bytes 165896 | tf_op jit(solution)/shard_map/ppermute | solution.py:290
  12.8 19.0 %copy-start = (bf16[512,512]{1,0:T(8,128)(2,1)S(1)}, bf16[512,512]{1,0:T(8,128)(2,1)}, u32[]{:S(2)}) copy-start(bf16[512,512]{1,0:T(8,128)(2,1)} %param.17) | copy-start | bytes 1572868
  12.8 40.9 %all-to-all-start = ((bf16[16,32,1536]{2,1,0:T(8,128)(2,1)}), bf16[16,32,1536]{2,1,0:T(8,128)(2,1)S(1)}, u32[]{:S(2)}, u32[]{:S(2)}) async-start(bf16[16,32,1536]{2,1,0:T(8,128)(2,1)} %bitcast), calls=%async_computation | async-start | bytes 3145728 | tf_op jit(solution)/shard_map/all_to_all | solution.py:295
  22.2 6.5 %collective-permute-start.6 = (bf16[48,1152]{1,0:T(8,128)(2,1)S(1)}, bf16[48,1152]{1,0:T(8,128)(2,1)S(1)}, u32[]{:S(2)}, u32[]{:S(2)}) collective-permute-start(bf16[48,1152]{1,0:T(8,128)(2,1)S(1)} %constant_dynamic-update-slice_fusion.2), channel_id=1, source_target_pairs={{0,4},{4,0},{8,12},{12,8},{1,5},{5,1},{9,13},{13,9},{2,6},{6,2},{1... | collective-permute-start | bytes 331784 | tf_op jit(solution)/shard_map/ppermute | solution.py:290
  23.8 8.9 %collective-permute-start.7 = (bf16[48,1152]{1,0:T(8,128)(2,1)S(1)}, bf16[48,1152]{1,0:T(8,128)(2,1)S(1)}, u32[]{:S(2)}, u32[]{:S(2)}) collective-permute-start(bf16[48,1152]{1,0:T(8,128)(2,1)S(1)} %constant_dynamic-update-slice_fusion.2), channel_id=1, source_target_pairs={{0,8},{4,12},{8,0},{12,4},{1,9},{5,13},{9,1},{13,5},{2,10},{6,14},... | collective-permute-start | bytes 331784 | tf_op jit(solution)/shard_map/ppermute | solution.py:290
  26.7 7.6 %collective-permute-start.8 = (bf16[48,1152]{1,0:T(8,128)(2,1)S(1)}, bf16[48,1152]{1,0:T(8,128)(2,1)S(1)}, u32[]{:S(2)}, u32[]{:S(2)}) collective-permute-start(bf16[48,1152]{1,0:T(8,128)(2,1)S(1)} %constant_dynamic-update-slice_fusion.2), channel_id=1, source_target_pairs={{0,12},{4,8},{8,4},{12,0},{1,13},{5,9},{9,5},{13,1},{2,14},{6,10},... | collective-permute-start | bytes 331784 | tf_op jit(solution)/shard_map/ppermute | solution.py:290
  27.0 11.5 %collective-permute-start.3 = (bf16[48,1152]{1,0:T(8,128)(2,1)S(1)}, bf16[48,1152]{1,0:T(8,128)(2,1)S(1)}, u32[]{:S(2)}, u32[]{:S(2)}) collective-permute-start(bf16[48,1152]{1,0:T(8,128)(2,1)S(1)} %constant_dynamic-update-slice_fusion), channel_id=1, source_target_pairs={{0,32},{32,0},{64,96},{96,64},{1,33},{33,1},{65,97},{97,65},{2,34}... | collective-permute-start | bytes 331784 | tf_op jit(solution)/shard_map/ppermute | solution.py:290
  27.9 17.1 %collective-permute-start.4 = (bf16[48,1152]{1,0:T(8,128)(2,1)S(1)}, bf16[48,1152]{1,0:T(8,128)(2,1)S(1)}, u32[]{:S(2)}, u32[]{:S(2)}) collective-permute-start(bf16[48,1152]{1,0:T(8,128)(2,1)S(1)} %constant_dynamic-update-slice_fusion), channel_id=1, source_target_pairs={{0,64},{32,96},{64,0},{96,32},{1,65},{33,97},{65,1},{97,33},{2,66}... | collective-permute-start | bytes 331784 | tf_op jit(solution)/shard_map/ppermute | solution.py:290
  28.6 16.4 %collective-permute-start.5 = (bf16[48,1152]{1,0:T(8,128)(2,1)S(1)}, bf16[48,1152]{1,0:T(8,128)(2,1)S(1)}, u32[]{:S(2)}, u32[]{:S(2)}) collective-permute-start(bf16[48,1152]{1,0:T(8,128)(2,1)S(1)} %constant_dynamic-update-slice_fusion), channel_id=1, source_target_pairs={{0,96},{32,64},{64,32},{96,0},{1,97},{33,65},{65,33},{97,1},{2,98}... | collective-permute-start | bytes 331784 | tf_op jit(solution)/shard_map/ppermute | solution.py:290
  38.5 20.5 %copy-start.1 = (bf16[48,1152]{1,0:T(8,128)(2,1)}, bf16[48,1152]{1,0:T(8,128)(2,1)S(1)}, u32[]{:S(2)}) copy-start(bf16[48,1152]{1,0:T(8,128)(2,1)S(1)} %collective-permute-done.3) | copy-start | bytes 331780
  45.0 13.9 %copy-start.3 = (bf16[48,1152]{1,0:T(8,128)(2,1)}, bf16[48,1152]{1,0:T(8,128)(2,1)S(1)}, u32[]{:S(2)}) copy-start(bf16[48,1152]{1,0:T(8,128)(2,1)S(1)} %collective-permute-done.4) | copy-start | bytes 331780
  45.0 13.9 %copy-start.5 = (bf16[48,1152]{1,0:T(8,128)(2,1)}, bf16[48,1152]{1,0:T(8,128)(2,1)S(1)}, u32[]{:S(2)}) copy-start(bf16[48,1152]{1,0:T(8,128)(2,1)S(1)} %collective-permute-done.5) | copy-start | bytes 331780
  58.9 12.5 %copy-start.2 = (bf16[48,1152]{1,0:T(8,128)(2,1)S(1)}, bf16[48,1152]{1,0:T(8,128)(2,1)}, u32[]{:S(2)}) copy-start(bf16[48,1152]{1,0:T(8,128)(2,1)} %copy-done.1) | copy-start | bytes 331780
  58.9 12.5 %copy-start.4 = (bf16[48,1152]{1,0:T(8,128)(2,1)S(1)}, bf16[48,1152]{1,0:T(8,128)(2,1)}, u32[]{:S(2)}) copy-start(bf16[48,1152]{1,0:T(8,128)(2,1)} %copy-done.3) | copy-start | bytes 331780
  59.0 12.6 %copy-start.6 = (bf16[48,1152]{1,0:T(8,128)(2,1)S(1)}, bf16[48,1152]{1,0:T(8,128)(2,1)}, u32[]{:S(2)}) copy-start(bf16[48,1152]{1,0:T(8,128)(2,1)} %copy-done.5) | copy-start | bytes 331780
  59.0 39.9 %all-to-all-start.1 = ((bf16[16,32,1536]{2,1,0:T(8,128)(2,1)}), bf16[16,32,1536]{2,1,0:T(8,128)(2,1)S(1)}, u32[]{:S(2)}, u32[]{:S(2)}) async-start(bf16[16,32,1536]{2,1,0:T(8,128)(2,1)} %bitcast.2), calls=%async_computation.1 | async-start | bytes 3145728 | tf_op jit(solution)/shard_map/all_to_all | solution.py:295
  70.5 28.4 %collective-permute-start.12 = (bf16[192,1152]{1,0:T(8,128)(2,1)S(1)}, bf16[192,1152]{1,0:T(8,128)(2,1)S(1)}, u32[]{:S(2)}, u32[]{:S(2)}) collective-permute-start(bf16[192,1152]{1,0:T(8,128)(2,1)S(1)} %constant_dynamic-update-slice_fusion.8.refs_4_), channel_id=1, source_target_pairs={{0,32},{32,0},{64,96},{96,64},{1,33},{33,1},{65,97},{97,65},{2,34}... | collective-permute-start | bytes 1327112 | tf_op jit(solution)/shard_map/ppermute | solution.py:290
  71.5 27.4 %collective-permute-start.10 = (bf16[192,1152]{1,0:T(8,128)(2,1)S(1)}, bf16[192,1152]{1,0:T(8,128)(2,1)}, u32[]{:S(2)}, u32[]{:S(2)}) collective-permute-start(bf16[192,1152]{1,0:T(8,128)(2,1)S(1)} %constant_dynamic-update-slice_fusion.4.refs_0_), channel_id=1, source_target_pairs={{0,8},{4,12},{8,0},{12,4},{1,9},{5,13},{9,1},{13,5},{2,10},{6,14},... | collective-permute-start | bytes 1327112 | tf_op jit(solution)/shard_map/ppermute | solution.py:290
  74.8 24.1 %collective-permute-start.11 = (bf16[192,1152]{1,0:T(8,128)(2,1)S(1)}, bf16[192,1152]{1,0:T(8,128)(2,1)}, u32[]{:S(2)}, u32[]{:S(2)}) collective-permute-start(bf16[192,1152]{1,0:T(8,128)(2,1)S(1)} %constant_dynamic-update-slice_fusion.4.refs_0_), channel_id=1, source_target_pairs={{0,12},{4,8},{8,4},{12,0},{1,13},{5,9},{9,5},{13,1},{2,14},{6,10},... | collective-permute-start | bytes 1327112 | tf_op jit(solution)/shard_map/ppermute | solution.py:290
  75.9 23.0 %collective-permute-start.9 = (bf16[192,1152]{1,0:T(8,128)(2,1)S(1)}, bf16[192,1152]{1,0:T(8,128)(2,1)}, u32[]{:S(2)}, u32[]{:S(2)}) collective-permute-start(bf16[192,1152]{1,0:T(8,128)(2,1)S(1)} %constant_dynamic-update-slice_fusion.4.refs_0_), channel_id=1, source_target_pairs={{0,4},{4,0},{8,12},{12,8},{1,5},{5,1},{9,13},{13,9},{2,6},{6,2},{1... | collective-permute-start | bytes 1327112 | tf_op jit(solution)/shard_map/ppermute | solution.py:290
  104.0 49.2 %copy-start.7 = (f32[768]{0:T(1024)S(1)}, f32[768]{0:T(1024)}, u32[]{:S(2)}) copy-start(f32[768]{0:T(1024)} %param.18) | copy-start | bytes 9220
  104.0 62.6 %all-to-all-start.2 = ((bf16[16,48,1024]{2,1,0:T(8,128)(2,1)}), bf16[16,48,1024]{2,1,0:T(8,128)(2,1)S(1)}, u32[]{:S(2)}, u32[]{:S(2)}) async-start(bf16[16,48,1024]{2,1,0:T(8,128)(2,1)} %residuals.1), calls=%async_computation.2 | async-start | bytes 3145728 | tf_op jit(solution)/shard_map/all_to_all | solution.py:295
  127.1 13.8 %collective-permute-start.13 = (bf16[192,1152]{1,0:T(8,128)(2,1)S(1)}, bf16[192,1152]{1,0:T(8,128)(2,1)S(1)}, u32[]{:S(2)}, u32[]{:S(2)}) collective-permute-start(bf16[192,1152]{1,0:T(8,128)(2,1)S(1)} %constant_dynamic-update-slice_fusion.8.refs_4_), channel_id=1, source_target_pairs={{0,64},{32,96},{64,0},{96,32},{1,65},{33,97},{65,1},{97,33},{2,66}... | collective-permute-start | bytes 1327112 | tf_op jit(solution)/shard_map/ppermute | solution.py:290
  127.2 22.8 %collective-permute-start.14 = (bf16[192,1152]{1,0:T(8,128)(2,1)S(1)}, bf16[192,1152]{1,0:T(8,128)(2,1)S(1)}, u32[]{:S(2)}, u32[]{:S(2)}) collective-permute-start(bf16[192,1152]{1,0:T(8,128)(2,1)S(1)} %constant_dynamic-update-slice_fusion.8.refs_4_), channel_id=1, source_target_pairs={{0,96},{32,64},{64,32},{96,0},{1,97},{33,65},{65,33},{97,1},{2,98}... | collective-permute-start | bytes 1327112 | tf_op jit(solution)/shard_map/ppermute | solution.py:290
  140.8 10.2 %collective-permute-start.21 = (bf16[192,1152]{1,0:T(8,128)(2,1)S(1)}, bf16[192,1152]{1,0:T(8,128)(2,1)S(1)}, u32[]{:S(2)}, u32[]{:S(2)}) collective-permute-start(bf16[192,1152]{1,0:T(8,128)(2,1)S(1)} %collective-permute-done.13.refs_6_), channel_id=1, source_target_pairs={{0,16},{16,0},{1,17},{17,1},{2,18},{18,2},{3,19},{19,3},{4,20},{20... | collective-permute-start | bytes 1327112 | tf_op jit(solution)/shard_map/ppermute | solution.py:325
  150.0 1.8 collective-permute-start.22
  150.0 3.1 %collective-permute-start.15 = (bf16[192,1152]{1,0:T(8,128)(2,1)S(1)}, bf16[192,1152]{1,0:T(8,128)(2,1)S(1)}, u32[]{:S(2)}, u32[]{:S(2)}) collective-permute-start(bf16[192,1152]{1,0:T(8,128)(2,1)S(1)} %constant_dynamic-update-slice_fusion.4.refs_0_), channel_id=1, source_target_pairs={{0,16},{16,0},{1,17},{17,1},{2,18},{18,2},{3,19},{19,3},{4,20},{20... | collective-permute-start | bytes 1327112 | tf_op jit(solution)/shard_map/ppermute | solution.py:325
  150.5 2.9 %collective-permute-start.16 = (bf16[192,1152]{1,0:T(8,128)(2,1)}, bf16[192,1152]{1,0:T(8,128)(2,1)S(1)}, u32[]{:S(2)}, u32[]{:S(2)}) collective-permute-start(bf16[192,1152]{1,0:T(8,128)(2,1)} %collective-permute-done.9.refs_1_), channel_id=1, source_target_pairs={{0,16},{16,0},{1,17},{17,1},{2,18},{18,2},{3,19},{19,3},{4,20},{20... | collective-permute-start | bytes 1327112 | tf_op jit(solution)/shard_map/ppermute | solution.py:325
  150.5 4.0 %collective-permute-start.17 = (bf16[192,1152]{1,0:T(8,128)(2,1)}, bf16[192,1152]{1,0:T(8,128)(2,1)S(1)}, u32[]{:S(2)}, u32[]{:S(2)}) collective-permute-start(bf16[192,1152]{1,0:T(8,128)(2,1)} %collective-permute-done.10.refs_2_), channel_id=1, source_target_pairs={{0,16},{16,0},{1,17},{17,1},{2,18},{18,2},{3,19},{19,3},{4,20},{20... | collective-permute-start | bytes 1327112 | tf_op jit(solution)/shard_map/ppermute | solution.py:325
  151.0 4.8 %collective-permute-start.18 = (bf16[192,1152]{1,0:T(8,128)(2,1)}, bf16[192,1152]{1,0:T(8,128)(2,1)S(1)}, u32[]{:S(2)}, u32[]{:S(2)}) collective-permute-start(bf16[192,1152]{1,0:T(8,128)(2,1)} %collective-permute-done.11.refs_3_), channel_id=1, source_target_pairs={{0,16},{16,0},{1,17},{17,1},{2,18},{18,2},{3,19},{19,3},{4,20},{20... | collective-permute-start | bytes 1327112 | tf_op jit(solution)/shard_map/ppermute | solution.py:325
  151.8 4.0 %collective-permute-start.19 = (bf16[192,1152]{1,0:T(8,128)(2,1)S(1)}, bf16[192,1152]{1,0:T(8,128)(2,1)S(1)}, u32[]{:S(2)}, u32[]{:S(2)}) collective-permute-start(bf16[192,1152]{1,0:T(8,128)(2,1)S(1)} %constant_dynamic-update-slice_fusion.8.refs_4_), channel_id=1, source_target_pairs={{0,16},{16,0},{1,17},{17,1},{2,18},{18,2},{3,19},{19,3},{4,20},{20... | collective-permute-start | bytes 1327112 | tf_op jit(solution)/shard_map/ppermute | solution.py:325
  153.1 2.7 %collective-permute-start.20 = (bf16[192,1152]{1,0:T(8,128)(2,1)S(1)}, bf16[192,1152]{1,0:T(8,128)(2,1)S(1)}, u32[]{:S(2)}, u32[]{:S(2)}) collective-permute-start(bf16[192,1152]{1,0:T(8,128)(2,1)S(1)} %collective-permute-done.12.refs_5_), channel_id=1, source_target_pairs={{0,16},{16,0},{1,17},{17,1},{2,18},{18,2},{3,19},{19,3},{4,20},{20... | collective-permute-start | bytes 1327112 | tf_op jit(solution)/shard_map/ppermute | solution.py:325
